TPU v7x, 128 devices: a whole 4x4x4 slice. The times are simulated.
128 devices in a mesh: row: 16 (over y, x_lo, core), col: 8 (over x_hi, z).
Axes of the slice: x: 4 (x_hi: 2, x_lo: 2; x = x_hi * 2 + x_lo), y: 4, z: 4, core: 2. Of those that a mesh axis runs over, the one named last changes fastest.
Arguments:
- amplitudes: float32 [512, 32, 32, 32], P('col', 'row'), may hold values from -6 to 6
- integrals: float32 [1024, 16384], P('col', 'row'), may hold values from -0.1875 to 0.1875
- occ_energy: float32 [32], replicated, may hold values from -2 to -0.5
- vir_energy: float32 [512], replicated, may hold values from 0.3 to 3
Outputs:
- residual: float32 [16384, 16384], P('col', 'row')
All inputs are finite; a program needn't handle non-finite values.
Results may differ from a plain program's by a relative error of at most 0.00007.
Values sent between devices are 32-bit elements; how exact they have to be, the bound alone decides.
No kernel may reach another device: no remote copies, remote signals or barrier semaphores. Data moves between devices by JAX's collectives and lax.ppermute only.
A program may use at most 128 MiB of HBM per device.

v0:
```python
import jax
import jax.numpy as jnp
from jax import lax
from jax.sharding import PartitionSpec as P


def body(amplitudes, integrals, occ_energy, vir_energy):
    columns = integrals.shape[1]
    virtuals = amplitudes.shape[0]
    whole_w = lax.all_gather(integrals, "col", axis=0, tiled=True)
    occupied = amplitudes.shape[1] * lax.axis_size("row")
    portion = lax.all_gather(amplitudes, "row", axis=1, tiled=True)
    amount = portion.shape[1]
    flattened = portion.reshape(virtuals * amount, portion.shape[2] * portion.shape[3])
    product = jnp.dot(
        flattened, whole_w, preferred_element_type=jnp.float32, precision=lax.Precision.HIGHEST
    )
    folded = product.reshape(virtuals, amount, columns)
    summed = folded.reshape(virtuals * occupied, columns)
    height = summed.shape[0]
    gap_flat = (vir_energy[:, None] - occ_energy[None, :]).reshape(-1)
    row_gap = lax.dynamic_slice_in_dim(gap_flat, lax.axis_index("col") * height, height)
    col_gap = lax.dynamic_slice_in_dim(gap_flat, lax.axis_index("row") * columns, columns)
    return summed / (row_gap[:, None] + col_gap[None, :])


def solution(mesh):
    in_specs = (P("col", "row", None, None), P("col", "row"), P(), P())
    out_specs = P("col", "row")
    return jax.shard_map(body, mesh=mesh, in_specs=in_specs, out_specs=out_specs, check_vma=False)
```

profile of v0, /device:TPU:1, one launch (start us, length us, event | category | flops | bytes accessed | tf_op | source)
XLA Modules:
  0.0 217.1 jit_solution(794362143846984651)
XLA Ops:
  6.5 0.0 all-gather.3.cloned.1.call-start
  6.5 0.7 all-gather.3.cloned.1.call-update
  7.3 0.0 all-gather.5.cloned.1.call-start
  7.3 0.7 all-gather.5.cloned.1.call-update
  8.0 0.8 broadcast_subtract_fusion
  8.8 0.1 sub.20
  9.0 95.3 %all-gather.3.cloned.1.call-done = f32[64,32,32,32]{0,3,2,1:T(8,128)} async-done(((f32[64,2,32,32]{0,3,2,1:T(8,128)}), f32[64,32,32,32]{0,3,2,1:T(8,128)}) %all-gather.3.cloned.1.call-update) | async-done | bytes 8388624 | tf_op jit(solution)/shard_map/all_gather | solution.py:12
  104.3 30.4 %copy.6 = f32[64,32,32,32]{3,2,1,0:T(8,128)} copy(f32[64,32,32,32]{0,3,2,1:T(8,128)} %all-gather.3.cloned.1.call-done) | data formatting | bytes 16777216 | tf_op jit(solution)/shard_map/all_gather | solution.py:12
  134.7 26.3 %reshape.11 = f32[2048,1024]{1,0:T(8,128)} reshape(f32[64,32,32,32]{3,2,1,0:T(8,128)} %copy.6) | data formatting | bytes 16777216 | tf_op jit(solution)/shard_map/reshape | solution.py:14
  161.0 17.4 %all-gather.5.cloned.1.call-done = f32[1024,1024]{1,0:T(8,128)} async-done(((f32[128,1024]{1,0:T(8,128)}), f32[1024,1024]{1,0:T(8,128)}) %all-gather.5.cloned.1.call-update) | async-done | bytes 4194320 | tf_op jit(solution)/shard_map/all_gather | solution.py:10
  178.4 31.9 %add_divide_fusion = f32[2048,1024]{1,0:T(8,128)} fusion(f32[1024]{0:T(1024)S(1)} %dynamic_slice.7, f32[2048]{0:T(1024)S(1)} %dynamic_slice.6, f32[2048,1024]{1,0:T(8,128)} %reshape.11, f32[1024,1024]{1,0:T(8,128)} %all-gather.5.cloned.1.call-done), kind=kOutput, calls=%fused_computation | convolution fusion | flops 25773998080 | bytes 20983808 | tf_op jit(solution)/shard_map/dot_general | solution.py:15
  (2 shorter events, 0.0 us)
Async XLA Ops:
  6.5 97.8 %all-gather.3.cloned.1.call-start = ((), (), s32[]{:S(2)}) async-start(), calls=%async_computation | async-start | bytes 17825792 | tf_op jit(solution)/shard_map/all_gather | solution.py:12
  7.3 171.2 %all-gather.5.cloned.1.call-start = ((), (), s32[]{:S(2)}) async-start(), calls=%async_computation.1 | async-start | bytes 4718592 | tf_op jit(solution)/shard_map/all_gather | solution.py:10
Sparse Core Ops, SparseCore 0:
  9.1 95.2 all-gather.2
  106.7 71.7 all-gather.4
where the time goes:
time: 218 us; the launch traced here: 217 us
  waiting for transfers between devices  114 us (52%)
  local copies, waits for them, and re-layouts  56.8 us (26%)
  matrix products  31.9 us (15%)
  between operations  13.4 us (6%)
    all_gather x1, waiting for transfers between devices, body(): portion = lax.all_gather(amplitudes, 'row', axis=1, tiled=True)  95.3 us
    dot_general x1, matrix products, body(): jnp.dot(flattened, whole_w, preferred_element_type=jnp.float32, precision...  31.9 us
    all_gather x1, local copies, waits for them, and re-layouts, body(): portion = lax.all_gather(amplitudes, 'row', axis=1, tiled=True)  30.4 us
    reshape x1, local copies, waits for them, and re-layouts, body(): portion.reshape(virtuals * amount, portion.shape[2] * portion.shape[3])  26.3 us
    all_gather x1, waiting for transfers between devices, body(): whole_w = lax.all_gather(integrals, 'col', axis=0, tiled=True)  17.4 us
  transfers between devices with their start and end apart: 2, of which 2 were waited for; matrix products, arithmetic and copies ran while one was open for 27% of the time, Pallas kernels for 0%

commit v1 on v0

v1 whole, which is shorter than its diff:
```python
import functools

import jax
import jax.numpy as jnp
import numpy as np
from jax import lax
from jax.experimental import pallas as pl
from jax.experimental.pallas import tpu as pltpu
from jax.sharding import Mesh, PartitionSpec as P

ROW = ("y", "xl", "core")
COL = ("xh", "z")
AXES = ROW + COL
SIZES = (4, 2, 2, 2, 4)
f32, bf16 = jnp.float32, jnp.bfloat16
MIB = 1 << 20


def hop(value, **move):
    pairs = []
    for source in range(int(np.prod(SIZES))):
        place = list(np.unravel_index(source, SIZES))
        for axis, step in move.items():
            k = AXES.index(axis)
            place[k] = (place[k] + step) % SIZES[k]
        pairs.append((source, int(np.ravel_multi_index(place, SIZES))))
    return lax.ppermute(value, AXES, pairs)


def after(value, *needed):
    return lax.optimization_barrier((value,) + needed)[0]


def split(value):
    high = value.astype(bf16)
    return high, (value - high.astype(f32)).astype(bf16)


def turn_kernel(amp_ref, out_ref):
    for n in range(out_ref.shape[0]):
        lanes = slice(n * 128, n * 128 + 128)
        both = jnp.concatenate([amp_ref[0, lanes], amp_ref[1, lanes]], axis=1)
        out_ref[n] = both.T


def turn(amp):
    two, depth, width = amp.shape
    return pl.pallas_call(
        turn_kernel,
        out_shape=jax.ShapeDtypeStruct((depth // 128, two * width, 128), f32),
        in_specs=[pl.BlockSpec(memory_space=pltpu.VMEM)],
        out_specs=pl.BlockSpec(memory_space=pltpu.VMEM),
        name="turn",
    )(amp)


def prep_kernel(pieces, slots_ref, *refs):
    sources, (high_ref, low_ref), (held, sem) = refs[: len(pieces)], refs[len(pieces) : len(pieces) + 2], refs[len(pieces) + 2 :]
    copies = []
    number = 0
    for ref, parts in zip(sources, pieces):
        for start, rows, slot, offset in parts:
            row = pl.multiple_of(slots_ref[slot] * 128 + offset, 8)
            copies.append(pltpu.make_async_copy(ref.at[:, pl.ds(start, rows)], held.at[:, pl.ds(row, rows)], sem.at[number]))
            number += 1
    for copy in copies:
        copy.start()
    for copy in copies:
        copy.wait()
    width = held.shape[1] // 8
    for n in range(held.shape[0]):
        lane = n * 128
        for a in range(0, width, 2):
            value = jnp.concatenate(
                [held[n, pl.ds(a + b, 8, stride=width), :] for b in range(2)], axis=0
            )
            high, low = split(value)
            high_ref[a * 8 : a * 8 + 16, lane : lane + 128] = high
            low_ref[a * 8 : a * 8 + 16, lane : lane + 128] = low


def prep(slots, sources, pieces):
    depth = sources[0].shape[0] * 128
    rows = 4 * sources[0].shape[1]
    count = sum(len(p) for p in pieces)
    return pl.pallas_call(
        functools.partial(prep_kernel, pieces),
        out_shape=[jax.ShapeDtypeStruct((rows, depth), bf16)] * 2,
        in_specs=[pl.BlockSpec(memory_space=pltpu.SMEM)] + [pl.BlockSpec(memory_space=pl.ANY)] * len(sources),
        out_specs=[pl.BlockSpec(memory_space=pltpu.VMEM)] * 2,
        scratch_shapes=[pltpu.VMEM((depth // 128, rows, 128), f32), pltpu.SemaphoreType.DMA((count,))],
        cost_estimate=pl.CostEstimate(flops=rows * depth * 4, bytes_accessed=rows * depth * 8, transcendentals=0),
        name="prep",
    )(slots, *sources)


def prep_w_kernel(slots_ref, *refs):
    sources, (high_ref, low_ref), (held, sem) = refs[:8], refs[8:10], refs[10:]
    copies = [
        pltpu.make_async_copy(ref, held.at[slots_ref[n]], sem.at[n]) for n, ref in enumerate(sources)
    ]
    for copy in copies:
        copy.start()
    for copy in copies:
        copy.wait()
    for n in range(8):
        high, low = split(held[n])
        high_ref[n] = high
        low_ref[n] = low


def prep_w(slots, sources):
    rows, columns = sources[0].shape
    return pl.pallas_call(
        prep_w_kernel,
        out_shape=[jax.ShapeDtypeStruct((8, rows, columns), bf16)] * 2,
        in_specs=[pl.BlockSpec(memory_space=pltpu.SMEM)] + [pl.BlockSpec(memory_space=pl.ANY)] * 8,
        out_specs=[pl.BlockSpec(memory_space=pltpu.VMEM)] * 2,
        scratch_shapes=[pltpu.VMEM((8, rows, columns), f32), pltpu.SemaphoreType.DMA((8,))],
        name="prep_w",
    )(slots, *sources)


def mm_kernel(ys_ref, *refs):
    (*a_refs, whigh_ref, wlow_ref, rgap_ref, cgap_ref, out_ref) = refs
    chunk = pl.program_id(0)
    depth, columns = whigh_ref.shape

    def work(high_ref, low_ref):
        high, low = high_ref[...], low_ref[...]
        tall = rgap_ref[...].reshape(-1, 128)
        for n in range(0, columns, 256):
            wh, wl = whigh_ref[:, n : n + 256], wlow_ref[:, n : n + 256]
            total = jnp.dot(high, wh, preferred_element_type=f32)
            total += jnp.dot(high, wl, preferred_element_type=f32)
            total += jnp.dot(low, wh, preferred_element_type=f32)
            for m in range(0, 256, 128):
                gap = tall + cgap_ref[:, n + m : n + m + 128]
                out_ref[:, 0, :, n + m : n + m + 128] = (total[:, m : m + 128] / gap).reshape(-1, 8, 128)

    for j in range(4):
        pl.when(chunk == j)(functools.partial(work, a_refs[2 * j], a_refs[2 * j + 1]))


def matmul(ys, parts, whigh, wlow, rgap, cgap, virtuals):
    depth, columns = whigh.shape
    steps = 2
    rows = parts[0].shape[0] // steps

    def a_spec(j):
        return pl.BlockSpec(
            (rows, depth), lambda c, s, ys: (jnp.where(c == j, s, jnp.where(c < j, 0, steps - 1)), 0)
        )

    return pl.pallas_call(
        mm_kernel,
        out_shape=jax.ShapeDtypeStruct((virtuals, 4, 8, columns), f32),
        grid_spec=pltpu.PrefetchScalarGridSpec(
            num_scalar_prefetch=1,
            grid=(4, steps),
            in_specs=[a_spec(j // 2) for j in range(8)]
            + [
                pl.BlockSpec((depth, columns), lambda c, s, ys: (0, 0)),
                pl.BlockSpec((depth, columns), lambda c, s, ys: (0, 0)),
                pl.BlockSpec((virtuals // steps, 1, 8, 128), lambda c, s, ys: (s, ys[c], 0, 0)),
                pl.BlockSpec((1, columns), lambda c, s, ys: (0, 0)),
            ],
            out_specs=pl.BlockSpec((virtuals // steps, 1, 8, columns), lambda c, s, ys: (s, ys[c], 0, 0)),
        ),
        compiler_params=pltpu.CompilerParams(vmem_limit_bytes=40 * MIB),
        name="contract",
    )(ys, *parts, whigh, wlow, rgap, cgap)


def body(amplitudes, integrals, occ_energy, vir_energy):
    virtuals, own = amplitudes.shape[:2]
    depth = amplitudes.shape[2] * amplitudes.shape[3]
    columns = integrals.shape[1]
    y, xl, core, xh, z = (lax.axis_index(a) for a in AXES)

    x = turn(amplitudes.transpose(1, 2, 3, 0).reshape(own, depth, virtuals))
    w = integrals
    half = x.shape[1] // 2

    wp, wm = hop(w, z=1), hop(w, z=3)
    xp, xm, xx = hop(x, y=1), hop(x, y=3), hop(x, xl=1)
    xxp, xxm = hop(xx, y=1), hop(xx, y=3)
    w2, wx = hop(after(w, wp), z=2), hop(after(w, xx), xh=1)
    c0 = [hop(x, core=1), hop(xx, core=1)]
    c1 = [hop(xp, core=1), hop(xxp, core=1)]
    c2 = [hop(xm, core=1), hop(xxm, core=1)]
    up = hop(jnp.concatenate([xp[:, :half], xxp[:, :half]], axis=1), y=1)
    down = hop(jnp.concatenate([xm[:, half:], xxm[:, half:]], axis=1), y=3)
    wxp, wxm, wx2 = hop(wx, z=1), hop(wx, z=3), hop(w2, xh=1)
    c3 = [hop(up, core=1), hop(down, core=1)]

    slots = jnp.stack([xl * 2 + core, (1 - xl) * 2 + core, xl * 2 + 1 - core, (1 - xl) * 2 + 1 - core]).astype(jnp.int32)
    rows = 2 * half
    whole = [((0, rows, n, 0),) for n in range(4)]
    up_parts = lambda n: ((0, half, n, 0), (half, half, n + 1, 0))
    down_parts = lambda n: ((0, half, n, half), (half, half, n + 1, half))
    parts = []
    parts += prep(slots, [x, xx, *c0], whole)
    parts += prep(slots, [xp, xxp, *c1], whole)
    parts += prep(slots, [xm, xxm, *c2], whole)
    parts += prep(slots, [up, down, *c3], [up_parts(0), down_parts(0), up_parts(2), down_parts(2)])
    ys = jnp.stack([y, (y + 3) % 4, (y + 1) % 4, (y + 2) % 4]).astype(jnp.int32)

    here, there = xh * 4, (1 - xh) * 4
    wslots = jnp.stack(
        [here + z, here + (z + 3) % 4, here + (z + 1) % 4, here + (z + 2) % 4]
        + [there + z, there + (z + 3) % 4, there + (z + 1) % 4, there + (z + 2) % 4]
    ).astype(jnp.int32)
    whigh, wlow = prep_w(wslots, [w, wp, wm, w2, wx, wxp, wxm, wx2])

    gap = vir_energy[:, None] - occ_energy[None, :]
    first = (xh * 4 + z) * virtuals
    row_gap = lax.dynamic_slice_in_dim(gap, first, virtuals)
    rgap = jnp.broadcast_to(row_gap.reshape(virtuals, 4, 8, 1), (virtuals, 4, 8, 128))
    start = ((y * 2 + xl) * 2 + core) * columns
    cgap = lax.dynamic_slice_in_dim(gap.reshape(-1), start, columns).reshape(1, columns)

    out = matmul(ys, parts, whigh.reshape(depth, columns), wlow.reshape(depth, columns), rgap, cgap, virtuals)
    return out.reshape(virtuals * 32, columns)


def solution(mesh):
    fine = Mesh(mesh.devices.reshape(SIZES), AXES)
    in_specs = (P(COL, ROW, None, None), P(COL, ROW), P(), P())
    return jax.shard_map(body, mesh=fine, in_specs=in_specs, out_specs=P(COL, ROW), check_vma=False)
```

time: 218 us -> 122 us (0.56)
  waiting for transfers between devices: 114 us -> 25.8 us
  Pallas kernels: 0 us -> 44.6 us
  local copies, waits for them, and re-layouts: 56.8 us -> 13.3 us
  starting transfers between devices: 0.04 us -> 34.5 us
  matrix products: 31.9 us -> 0 us
  between operations: 13.4 us -> 0.28 us
    all_gather x2 -> x0, waiting for transfers between devices: 113 us -> none  [the longest x1 95.3 us: body(): portion = lax.all_gather(amplitudes, 'row', axis=1, tiled=True)]
    pallas_call x0 -> x7, Pallas kernels: none -> 44.6 us  [the longest x4 19.9 us: prep(): pl.pallas_call(functools.partial(prep_kernel, pieces), out_shape=[jax.Sha...]
    ppermute x0 -> x22, starting transfers between devices: none -> 34.5 us  [hop(): return lax.ppermute(value, AXES, pairs)]
    dot_general x1 -> x0, matrix products: 31.9 us -> none  [body(): jnp.dot(flattened, whole_w, preferred_element_type=jnp.float32, precision...]
    all_gather x1 -> x0, local copies, waits for them, and re-layouts: 30.4 us -> none  [body(): portion = lax.all_gather(amplitudes, 'row', axis=1, tiled=True)]
    reshape x1 -> x0, local copies, waits for them, and re-layouts: 26.3 us -> none  [body(): portion.reshape(virtuals * amount, portion.shape[2] * portion.shape[3])]
    ppermute x0 -> x22, waiting for transfers between devices: none -> 25.8 us  [hop(): return lax.ppermute(value, AXES, pairs)]
    unnamed x0 -> x48, local copies, waits for them, and re-layouts: none -> 11.8 us
  transfers between devices with their start and end apart: 2 -> 22, of which waited for: 2 -> 6; matrix products, arithmetic and copies ran while one was open for 27% -> 3% of each run, Pallas kernels for 0% -> 17%
where the time goes in v1:
time: 122 us; the launch traced here: 121 us
  Pallas kernels  44.6 us (37%)
  starting transfers between devices  34.5 us (28%)
  waiting for transfers between devices  25.8 us (21%)
  local copies, waits for them, and re-layouts  13.3 us (11%)
  other arithmetic  2.53 us (2%)
    ppermute x22, starting transfers between devices, hop(): return lax.ppermute(value, AXES, pairs)  34.5 us
    ppermute x22, waiting for transfers between devices, hop(): return lax.ppermute(value, AXES, pairs)  25.8 us
    pallas_call x4, Pallas kernels, prep(): pl.pallas_call(functools.partial(prep_kernel, pieces), out_shape=[jax.Sha...  19.9 us
    pallas_call x1, Pallas kernels, matmul(): pl.pallas_call(mm_kernel, out_shape=jax.ShapeDtypeStruct((virtuals, 4, 8,...  16.9 us
    unnamed x48, local copies, waits for them, and re-layouts  11.8 us
    pallas_call x1, Pallas kernels, prep_w(): pl.pallas_call(prep_w_kernel, out_shape=[jax.ShapeDtypeStruct((8, rows, c...  5.46 us
  transfers between devices with their start and end apart: 22, of which 6 were waited for; matrix products, arithmetic and copies ran while one was open for 3% of the time, Pallas kernels for 17%

profile of v1, /device:TPU:1, one launch (start us, length us, event | category | flops | bytes accessed | tf_op | source)
XLA Modules:
  0.0 121.0 jit_solution(17936722154433976580)
XLA Ops:
  0.0 2.4 %turn.1.refs_0_ = f32[8,128,128]{2,1,0:T(8,128)} custom-call(f32[2,1024,64]{2,1,0:T(8,128)} %bitcast.28), custom_call_target="tpu_custom_call" | custom-call | tf_op jit(solution)/shard_map/turn/pallas_call | solution.py:48
  2.4 2.0 %collective-permute-start = (f32[8,128,128]{2,1,0:T(8,128)}, f32[8,128,128]{2,1,0:T(8,128)S(1)}, u32[]{:S(2)}, u32[]{:S(2)}) collective-permute-start(f32[8,128,128]{2,1,0:T(8,128)} %turn.1.refs_0_), channel_id=1, source_target_pairs={{0,16},{1,17},{2,18},{3,19},{4,20},{5,21},{6,22},{7,23},{8,24},{9,... | collective-permute-start | bytes 1572872 | tf_op jit(solution)/shard_map/ppermute | solution.py:27
  4.4 1.6 %collective-permute-start.15 = (f32[128,1024]{1,0:T(8,128)}, f32[128,1024]{1,0:T(8,128)S(1)}, u32[]{:S(2)}, u32[]{:S(2)}) collective-permute-start(f32[128,1024]{1,0:T(8,128)} %refs_0_.1), channel_id=1, source_target_pairs={{0,1},{1,2},{2,3},{3,0},{4,5},{5,6},{6,7},{7,4},{8,9},{9,10},{10,1... | collective-permute-start | bytes 1572872 | tf_op jit(solution)/shard_map/ppermute | solution.py:27
  6.1 2.7 %collective-permute-start.7 = (f32[8,128,128]{2,1,0:T(8,128)}, f32[8,128,128]{2,1,0:T(8,128)S(1)}, u32[]{:S(2)}, u32[]{:S(2)}) collective-permute-start(f32[8,128,128]{2,1,0:T(8,128)} %turn.1.refs_0_), channel_id=1, source_target_pairs={{0,96},{1,97},{2,98},{3,99},{4,100},{5,101},{6,102},{7,103},{8,104... | collective-permute-start | bytes 1572872 | tf_op jit(solution)/shard_map/ppermute | solution.py:27
  8.8 0.0 collective-permute-start.3
  8.8 1.5 %collective-permute-start.1 = (f32[8,128,128]{2,1,0:T(8,128)}, f32[8,128,128]{2,1,0:T(8,128)S(1)}, u32[]{:S(2)}, u32[]{:S(2)}) collective-permute-start(f32[8,128,128]{2,1,0:T(8,128)} %turn.1.refs_0_), channel_id=1, source_target_pairs={{0,8},{1,9},{2,10},{3,11},{4,12},{5,13},{6,14},{7,15},{8,0},{9,1},... | collective-permute-start | bytes 1572872 | tf_op jit(solution)/shard_map/ppermute | solution.py:27
  10.3 5.5 %collective-permute-done.refs_1_ = f32[8,128,128]{2,1,0:T(8,128)S(1)} collective-permute-done((f32[8,128,128]{2,1,0:T(8,128)}, f32[8,128,128]{2,1,0:T(8,128)S(1)}, u32[]{:S(2)}, u32[]{:S(2)}) %collective-permute-start) | collective-permute-done | bytes 524320 | tf_op jit(solution)/shard_map/ppermute | solution.py:27
  15.8 3.2 %collective-permute-start.8 = (f32[8,128,128]{2,1,0:T(8,128)S(1)}, f32[8,128,128]{2,1,0:T(8,128)S(1)}, u32[]{:S(2)}, u32[]{:S(2)}) collective-permute-start(f32[8,128,128]{2,1,0:T(8,128)S(1)} %collective-permute-done.refs_1_), channel_id=1, source_target_pairs={{0,96},{1,97},{2,98},{3,99},{4,100},{5,101},{6,102},{7,103},{8,104... | collective-permute-start | bytes 1572872 | tf_op jit(solution)/shard_map/ppermute | solution.py:27
  18.9 0.8 collective-permute-done.15.refs_1_
  19.7 1.3 %collective-permute-start.4 = (f32[8,128,128]{2,1,0:T(8,128)S(1)}, f32[8,128,128]{2,1,0:T(8,128)S(1)}, u32[]{:S(2)}, u32[]{:S(2)}) collective-permute-start(f32[8,128,128]{2,1,0:T(8,128)S(1)} %collective-permute-done.refs_1_), channel_id=1, source_target_pairs={{0,32},{1,33},{2,34},{3,35},{4,36},{5,37},{6,38},{7,39},{8,40},{9,... | collective-permute-start | bytes 1572872 | tf_op jit(solution)/shard_map/ppermute | solution.py:27
  21.0 0.0 collective-permute-done.7.refs_0_
  21.0 2.5 %collective-permute-start.18 = (f32[128,1024]{1,0:T(8,128)}, f32[128,1024]{1,0:T(8,128)}, u32[]{:S(2)}, u32[]{:S(2)}) collective-permute-start(f32[128,1024]{1,0:T(8,128)} %refs_0_.1), channel_id=1, source_target_pairs={{0,4},{1,5},{2,6},{3,7},{4,0},{5,1},{6,2},{7,3},{8,12},{9,13},{10,... | collective-permute-start | bytes 1572872 | tf_op jit(solution)/shard_map/ppermute | solution.py:27
  23.5 0.0 collective-permute-done.3.refs_0_
  23.5 2.1 %collective-permute-start.16 = (f32[128,1024]{1,0:T(8,128)}, f32[128,1024]{1,0:T(8,128)S(1)}, u32[]{:S(2)}, u32[]{:S(2)}) collective-permute-start(f32[128,1024]{1,0:T(8,128)} %refs_0_.1), channel_id=1, source_target_pairs={{0,3},{1,0},{2,1},{3,2},{4,7},{5,4},{6,5},{7,6},{8,11},{9,8},{10,9... | collective-permute-start | bytes 1572872 | tf_op jit(solution)/shard_map/ppermute | solution.py:27
  25.6 2.4 %collective-permute-start.9 = (f32[8,128,128]{2,1,0:T(8,128)S(1)}, f32[8,128,128]{2,1,0:T(8,128)S(1)}, u32[]{:S(2)}, u32[]{:S(2)}) collective-permute-start(f32[8,128,128]{2,1,0:T(8,128)S(1)} %collective-permute-done.7.refs_0_), channel_id=1, source_target_pairs={{0,8},{1,9},{2,10},{3,11},{4,12},{5,13},{6,14},{7,15},{8,0},{9,1},... | collective-permute-start | bytes 1572872 | tf_op jit(solution)/shard_map/ppermute | solution.py:27
  28.0 2.8 %collective-permute-done.8.refs_1_ = f32[8,128,128]{2,1,0:T(8,128)S(1)} collective-permute-done((f32[8,128,128]{2,1,0:T(8,128)S(1)}, f32[8,128,128]{2,1,0:T(8,128)S(1)}, u32[]{:S(2)}, u32[]{:S(2)}) %collective-permute-start.8) | collective-permute-done | bytes 524320 | tf_op jit(solution)/shard_map/ppermute | solution.py:27
  30.8 1.6 %collective-permute-start.2 = (f32[8,128,128]{2,1,0:T(8,128)S(1)}, f32[8,128,128]{2,1,0:T(8,128)S(1)}, u32[]{:S(2)}, u32[]{:S(2)}) collective-permute-start(f32[8,128,128]{2,1,0:T(8,128)S(1)} %collective-permute-done.refs_1_), channel_id=1, source_target_pairs={{0,8},{1,9},{2,10},{3,11},{4,12},{5,13},{6,14},{7,15},{8,0},{9,1},... | collective-permute-start | bytes 1572872 | tf_op jit(solution)/shard_map/ppermute | solution.py:27
  32.4 1.6 %collective-permute-done.4.refs_1_ = f32[8,128,128]{2,1,0:T(8,128)S(1)} collective-permute-done((f32[8,128,128]{2,1,0:T(8,128)S(1)}, f32[8,128,128]{2,1,0:T(8,128)S(1)}, u32[]{:S(2)}, u32[]{:S(2)}) %collective-permute-start.4) | collective-permute-done | bytes 524320 | tf_op jit(solution)/shard_map/ppermute | solution.py:27
  33.9 3.5 %collective-permute-start.17 = (f32[128,1024]{1,0:T(8,128)}, f32[128,1024]{1,0:T(8,128)}, u32[]{:S(2)}, u32[]{:S(2)}) collective-permute-start(f32[128,1024]{1,0:T(8,128)} %refs_0_.1), channel_id=1, source_target_pairs={{0,2},{1,3},{2,0},{3,1},{4,6},{5,7},{6,4},{7,5},{8,10},{9,11},{10,... | collective-permute-start | bytes 1572872 | tf_op jit(solution)/shard_map/ppermute | solution.py:27
  37.5 0.8 pad_maximum_fusion.1
  38.4 0.9 pad_maximum_fusion
  39.3 0.0 collective-permute-done.18.refs_4_
  39.3 0.9 collective-permute-start.20
  40.1 0.0 collective-permute-done.16.refs_2_
  40.1 0.6 collective-permute-start.19
  40.7 0.0 collective-permute-done.9.refs_2_
  40.7 1.7 %collective-permute-start.12 = (f32[8,128,128]{2,1,0:T(8,128)}, f32[8,128,128]{2,1,0:T(8,128)}, u32[]{:S(2)}, u32[]{:S(2)}) collective-permute-start(f32[8,128,128]{2,1,0:T(8,128)} %pad_maximum_fusion.1), channel_id=1, source_target_pairs={{0,96},{1,97},{2,98},{3,99},{4,100},{5,101},{6,102},{7,103},{8,104... | collective-permute-start | bytes 1572872 | tf_op jit(solution)/shard_map/ppermute | solution.py:27
  42.5 0.1 collective-permute-start.11
  42.6 5.8 %collective-permute-done.17.refs_3_ = f32[128,1024]{1,0:T(8,128)} collective-permute-done((f32[128,1024]{1,0:T(8,128)}, f32[128,1024]{1,0:T(8,128)}, u32[]{:S(2)}, u32[]{:S(2)}) %collective-permute-start.17) | collective-permute-done | bytes 524320 | tf_op jit(solution)/shard_map/ppermute | solution.py:27
  48.4 1.7 %collective-permute-start.21 = (f32[128,1024]{1,0:T(8,128)}, f32[128,1024]{1,0:T(8,128)}, u32[]{:S(2)}, u32[]{:S(2)}) collective-permute-start(f32[128,1024]{1,0:T(8,128)} %collective-permute-done.17.refs_3_), channel_id=1, source_target_pairs={{0,4},{1,5},{2,6},{3,7},{4,0},{5,1},{6,2},{7,3},{8,12},{9,13},{10,... | collective-permute-start | bytes 1572872 | tf_op jit(solution)/shard_map/ppermute | solution.py:27
  50.0 9.3 %collective-permute-done.20.refs_6_ = f32[128,1024]{1,0:T(8,128)} collective-permute-done((f32[128,1024]{1,0:T(8,128)}, f32[128,1024]{1,0:T(8,128)}, u32[]{:S(2)}, u32[]{:S(2)}) %collective-permute-start.20) | collective-permute-done | bytes 524320 | tf_op jit(solution)/shard_map/ppermute | solution.py:27
  59.4 1.3 %collective-permute-start.5 = (f32[8,128,128]{2,1,0:T(8,128)S(1)}, f32[8,128,128]{2,1,0:T(8,128)S(1)}, u32[]{:S(2)}, u32[]{:S(2)}) collective-permute-start(f32[8,128,128]{2,1,0:T(8,128)S(1)} %collective-permute-done.3.refs_0_), channel_id=1, source_target_pairs={{0,8},{1,9},{2,10},{3,11},{4,12},{5,13},{6,14},{7,15},{8,0},{9,1},... | collective-permute-start | bytes 1572872 | tf_op jit(solution)/shard_map/ppermute | solution.py:27
  60.7 1.2 collective-permute-start.10
  61.9 0.0 collective-permute-done.12.refs_1_
  61.9 0.1 collective-permute-start.6
  62.0 0.0 collective-permute-done.11.refs_0_
  62.0 1.4 %collective-permute-start.14 = (f32[8,128,128]{2,1,0:T(8,128)}, f32[8,128,128]{2,1,0:T(8,128)}, u32[]{:S(2)}, u32[]{:S(2)}) collective-permute-start(f32[8,128,128]{2,1,0:T(8,128)} %collective-permute-done.12.refs_1_), channel_id=1, source_target_pairs={{0,8},{1,9},{2,10},{3,11},{4,12},{5,13},{6,14},{7,15},{8,0},{9,1},... | collective-permute-start | bytes 1572872 | tf_op jit(solution)/shard_map/ppermute | solution.py:27
  63.4 1.1 collective-permute-start.13
  64.5 0.1 broadcast_subtract_fusion
  64.6 0.1 copy.6
  64.8 0.1 dynamic-slice_bitcast_fusion
  64.8 0.1 copy.5
  64.9 0.1 sub.37
  65.1 0.7 stack.75.slots_ref
  65.8 0.7 pad_add_fusion.1.slots_ref
  66.4 0.1 pad_add_fusion.ys_ref
  66.5 4.9 %prep.4 = (bf16[512,1024]{1,0:T(8,128)(2,1)}, bf16[512,1024]{1,0:T(8,128)(2,1)}) custom-call(s32[4]{0:T(128)} %pad_add_fusion.1.slots_ref, f32[8,128,128]{2,1,0:T(8,128)} %turn.1.refs_0_, f32[8,128,128]{2,1,0:T(8,128)} %copy-done.15, f32[8,128,128]{2,1,0:T(8,128)} %copy-done.16, f32[8,128,128]{2,1,0:T(8,128)} %copy-done.19), custom_call_target="tpu_custom_call" | custom-call | flops 2097152 | bytes 4194304 | tf_op jit(solution)/shard_map/prep/pallas_call | solution.py:86
  71.4 5.5 %prep_w.1 = (bf16[8,128,1024]{2,1,0:T(8,128)(2,1)}, bf16[8,128,1024]{2,1,0:T(8,128)(2,1)}) custom-call(s32[8]{0:T(128)} %stack.75.slots_ref, f32[128,1024]{1,0:T(8,128)} %refs_0_.1, f32[128,1024]{1,0:T(8,128)} %copy-done.14, f32[128,1024]{1,0:T(8,128)} %copy-done.18, f32[128,1024]{1,0:T(8,128)} %collective-permute-done.17.refs_3_, ...), custom_call_target="tpu_custom_call" | custom-call | tf_op jit(solution)/shard_map/prep_w/pallas_call | solution.py:114
  76.9 4.9 %prep.6 = (bf16[512,1024]{1,0:T(8,128)(2,1)}, bf16[512,1024]{1,0:T(8,128)(2,1)}) custom-call(s32[4]{0:T(128)} %pad_add_fusion.1.slots_ref, f32[8,128,128]{2,1,0:T(8,128)} %copy-done.11, f32[8,128,128]{2,1,0:T(8,128)} %copy-done.13, f32[8,128,128]{2,1,0:T(8,128)} %copy-done.17, f32[8,128,128]{2,1,0:T(8,128)} %collective-permute-done.10.refs_3_), custom_call_target="tpu_custom_call" | custom-call | flops 2097152 | bytes 4194304 | tf_op jit(solution)/shard_map/prep/pallas_call | solution.py:86
  81.8 0.8 copy-done.20
  82.6 0.8 copy-done.21
  83.4 5.0 %prep.5 = (bf16[512,1024]{1,0:T(8,128)(2,1)}, bf16[512,1024]{1,0:T(8,128)(2,1)}) custom-call(s32[4]{0:T(128)} %pad_add_fusion.1.slots_ref, f32[8,128,128]{2,1,0:T(8,128)} %copy-done.10, f32[8,128,128]{2,1,0:T(8,128)} %copy-done.12, f32[8,128,128]{2,1,0:T(8,128)} %copy-done.20, f32[8,128,128]{2,1,0:T(8,128)} %copy-done.21), custom_call_target="tpu_custom_call" | custom-call | flops 2097152 | bytes 4194304 | tf_op jit(solution)/shard_map/prep/pallas_call | solution.py:86
  88.4 0.0 copy-start
  88.5 5.1 %prep.7 = (bf16[512,1024]{1,0:T(8,128)(2,1)}, bf16[512,1024]{1,0:T(8,128)(2,1)}) custom-call(s32[4]{0:T(128)} %pad_add_fusion.1.slots_ref, f32[8,128,128]{2,1,0:T(8,128)} %collective-permute-done.11.refs_0_, f32[8,128,128]{2,1,0:T(8,128)} %collective-permute-done.12.refs_1_, f32[8,128,128]{2,1,0:T(8,128)} %collective-permute-done.13.refs_2_, ...), custom_call_target="tpu_custom_call" | custom-call | flops 2097152 | bytes 4194304 | tf_op jit(solution)/shard_map/prep/pallas_call | solution.py:86
  93.6 0.3 broadcast_in_dim.10.refs_10_
  94.0 1.6 %copy-done.1 = bf16[8,128,1024]{2,1,0:T(8,128)(2,1)S(1)} copy-done((bf16[8,128,1024]{2,1,0:T(8,128)(2,1)S(1)}, bf16[8,128,1024]{2,1,0:T(8,128)(2,1)}, u32[]{:S(2)}) %copy-start.1) | copy-done | bytes 2097176
  95.5 1.2 %copy-done.3 = bf16[512,1024]{1,0:T(8,128)(2,1)S(1)} copy-done((bf16[512,1024]{1,0:T(8,128)(2,1)S(1)}, bf16[512,1024]{1,0:T(8,128)(2,1)}, u32[]{:S(2)}) %copy-start.3) | copy-done | bytes 1048600
  96.8 1.2 %copy-done.4 = bf16[512,1024]{1,0:T(8,128)(2,1)S(1)} copy-done((bf16[512,1024]{1,0:T(8,128)(2,1)S(1)}, bf16[512,1024]{1,0:T(8,128)(2,1)}, u32[]{:S(2)}) %copy-start.4) | copy-done | bytes 1048600
  98.0 1.2 %copy-done.5 = bf16[512,1024]{1,0:T(8,128)(2,1)S(1)} copy-done((bf16[512,1024]{1,0:T(8,128)(2,1)S(1)}, bf16[512,1024]{1,0:T(8,128)(2,1)}, u32[]{:S(2)}) %copy-start.5) | copy-done | bytes 1048600
  99.2 1.2 %copy-done.6 = bf16[512,1024]{1,0:T(8,128)(2,1)S(1)} copy-done((bf16[512,1024]{1,0:T(8,128)(2,1)S(1)}, bf16[512,1024]{1,0:T(8,128)(2,1)}, u32[]{:S(2)}) %copy-start.6) | copy-done | bytes 1048600
  100.5 1.2 %copy-done.7 = bf16[512,1024]{1,0:T(8,128)(2,1)S(1)} copy-done((bf16[512,1024]{1,0:T(8,128)(2,1)S(1)}, bf16[512,1024]{1,0:T(8,128)(2,1)}, u32[]{:S(2)}) %copy-start.7) | copy-done | bytes 1048600
  101.7 1.2 %copy-done.8 = bf16[512,1024]{1,0:T(8,128)(2,1)S(1)} copy-done((bf16[512,1024]{1,0:T(8,128)(2,1)S(1)}, bf16[512,1024]{1,0:T(8,128)(2,1)}, u32[]{:S(2)}) %copy-start.8) | copy-done | bytes 1048600
  102.9 1.2 %copy-done.9 = bf16[512,1024]{1,0:T(8,128)(2,1)S(1)} copy-done((bf16[512,1024]{1,0:T(8,128)(2,1)S(1)}, bf16[512,1024]{1,0:T(8,128)(2,1)}, u32[]{:S(2)}) %copy-start.9) | copy-done | bytes 1048600
  104.1 16.9 %contract.1 = f32[64,4,8,1024]{3,2,1,0:T(8,128)} custom-call(s32[4]{0:T(128)S(1)} %pad_add_fusion.ys_ref, bf16[512,1024]{1,0:T(8,128)(2,1)S(1)} %copy-done.2, bf16[512,1024]{1,0:T(8,128)(2,1)S(1)} %copy-done.3, bf16[512,1024]{1,0:T(8,128)(2,1)S(1)} %copy-done.6, bf16[512,1024]{1,0:T(8,128)(2,1)S(1)} %copy-done.7, bf16[512,1024]{1,0:T(8,128)(2,1)S(1)} %copy-done.4, ...), custom_call_target="tpu_custom_call" | custom-call | tf_op jit(solution)/shard_map/contract/pallas_call | solution.py:155
  (51 shorter events, 0.2 us)
Async XLA Ops:
  2.4 62.2 %copy-start.22 = (f32[512]{0:T(512)S(1)}, f32[512]{0:T(512)}, u32[]{:S(2)}) copy-start(f32[512]{0:T(512)} %param.7) | copy-start | bytes 6148
  2.4 62.2 %copy-start.23 = (f32[32]{0:T(128)S(1)}, f32[32]{0:T(128)}, u32[]{:S(2)}) copy-start(f32[32]{0:T(128)} %param.6) | copy-start | bytes 388
  2.4 13.4 %collective-permute-start = (f32[8,128,128]{2,1,0:T(8,128)}, f32[8,128,128]{2,1,0:T(8,128)S(1)}, u32[]{:S(2)}, u32[]{:S(2)}) collective-permute-start(f32[8,128,128]{2,1,0:T(8,128)} %turn.1.refs_0_), channel_id=1, source_target_pairs={{0,16},{1,17},{2,18},{3,19},{4,20},{5,21},{6,22},{7,23},{8,24},{9,... | collective-permute-start | bytes 1572872 | tf_op jit(solution)/shard_map/ppermute | solution.py:27
  4.4 15.3 %collective-permute-start.15 = (f32[128,1024]{1,0:T(8,128)}, f32[128,1024]{1,0:T(8,128)S(1)}, u32[]{:S(2)}, u32[]{:S(2)}) collective-permute-start(f32[128,1024]{1,0:T(8,128)} %refs_0_.1), channel_id=1, source_target_pairs={{0,1},{1,2},{2,3},{3,0},{4,5},{5,6},{6,7},{7,4},{8,9},{9,10},{10,1... | collective-permute-start | bytes 1572872 | tf_op jit(solution)/shard_map/ppermute | solution.py:27
  6.1 15.0 %collective-permute-start.7 = (f32[8,128,128]{2,1,0:T(8,128)}, f32[8,128,128]{2,1,0:T(8,128)S(1)}, u32[]{:S(2)}, u32[]{:S(2)}) collective-permute-start(f32[8,128,128]{2,1,0:T(8,128)} %turn.1.refs_0_), channel_id=1, source_target_pairs={{0,96},{1,97},{2,98},{3,99},{4,100},{5,101},{6,102},{7,103},{8,104... | collective-permute-start | bytes 1572872 | tf_op jit(solution)/shard_map/ppermute | solution.py:27
  8.8 14.7 %collective-permute-start.3 = (f32[8,128,128]{2,1,0:T(8,128)}, f32[8,128,128]{2,1,0:T(8,128)S(1)}, u32[]{:S(2)}, u32[]{:S(2)}) collective-permute-start(f32[8,128,128]{2,1,0:T(8,128)} %turn.1.refs_0_), channel_id=1, source_target_pairs={{0,32},{1,33},{2,34},{3,35},{4,36},{5,37},{6,38},{7,39},{8,40},{9,... | collective-permute-start | bytes 1572872 | tf_op jit(solution)/shard_map/ppermute | solution.py:27
  8.8 16.8 %collective-permute-start.1 = (f32[8,128,128]{2,1,0:T(8,128)}, f32[8,128,128]{2,1,0:T(8,128)S(1)}, u32[]{:S(2)}, u32[]{:S(2)}) collective-permute-start(f32[8,128,128]{2,1,0:T(8,128)} %turn.1.refs_0_), channel_id=1, source_target_pairs={{0,8},{1,9},{2,10},{3,11},{4,12},{5,13},{6,14},{7,15},{8,0},{9,1},... | collective-permute-start | bytes 1572872 | tf_op jit(solution)/shard_map/ppermute | solution.py:27
  15.8 34.3 %copy-start.15 = (f32[8,128,128]{2,1,0:T(8,128)}, f32[8,128,128]{2,1,0:T(8,128)S(1)}, u32[]{:S(2)}) copy-start(f32[8,128,128]{2,1,0:T(8,128)S(1)} %collective-permute-done.refs_1_) | copy-start | bytes 1572868
  15.8 15.0 %collective-permute-start.8 = (f32[8,128,128]{2,1,0:T(8,128)S(1)}, f32[8,128,128]{2,1,0:T(8,128)S(1)}, u32[]{:S(2)}, u32[]{:S(2)}) collective-permute-start(f32[8,128,128]{2,1,0:T(8,128)S(1)} %collective-permute-done.refs_1_), channel_id=1, source_target_pairs={{0,96},{1,97},{2,98},{3,99},{4,100},{5,101},{6,102},{7,103},{8,104... | collective-permute-start | bytes 1572872 | tf_op jit(solution)/shard_map/ppermute | solution.py:27
  19.7 30.3 %copy-start.14 = (f32[128,1024]{1,0:T(8,128)}, f32[128,1024]{1,0:T(8,128)S(1)}, u32[]{:S(2)}) copy-start(f32[128,1024]{1,0:T(8,128)S(1)} %collective-permute-done.15.refs_1_) | copy-start | bytes 1572868
  19.7 14.2 %collective-permute-start.4 = (f32[8,128,128]{2,1,0:T(8,128)S(1)}, f32[8,128,128]{2,1,0:T(8,128)S(1)}, u32[]{:S(2)}, u32[]{:S(2)}) collective-permute-start(f32[8,128,128]{2,1,0:T(8,128)S(1)} %collective-permute-done.refs_1_), channel_id=1, source_target_pairs={{0,32},{1,33},{2,34},{3,35},{4,36},{5,37},{6,38},{7,39},{8,40},{9,... | collective-permute-start | bytes 1572872 | tf_op jit(solution)/shard_map/ppermute | solution.py:27
  21.0 29.0 %copy-start.11 = (f32[8,128,128]{2,1,0:T(8,128)}, f32[8,128,128]{2,1,0:T(8,128)S(1)}, u32[]{:S(2)}) copy-start(f32[8,128,128]{2,1,0:T(8,128)S(1)} %collective-permute-done.7.refs_0_) | copy-start | bytes 1572868
  21.0 18.2 %collective-permute-start.18 = (f32[128,1024]{1,0:T(8,128)}, f32[128,1024]{1,0:T(8,128)}, u32[]{:S(2)}, u32[]{:S(2)}) collective-permute-start(f32[128,1024]{1,0:T(8,128)} %refs_0_.1), channel_id=1, source_target_pairs={{0,4},{1,5},{2,6},{3,7},{4,0},{5,1},{6,2},{7,3},{8,12},{9,13},{10,... | collective-permute-start | bytes 1572872 | tf_op jit(solution)/shard_map/ppermute | solution.py:27
  23.5 35.9 %copy-start.10 = (f32[8,128,128]{2,1,0:T(8,128)}, f32[8,128,128]{2,1,0:T(8,128)S(1)}, u32[]{:S(2)}) copy-start(f32[8,128,128]{2,1,0:T(8,128)S(1)} %collective-permute-done.3.refs_0_) | copy-start | bytes 1572868
  23.5 16.7 %collective-permute-start.16 = (f32[128,1024]{1,0:T(8,128)}, f32[128,1024]{1,0:T(8,128)S(1)}, u32[]{:S(2)}, u32[]{:S(2)}) collective-permute-start(f32[128,1024]{1,0:T(8,128)} %refs_0_.1), channel_id=1, source_target_pairs={{0,3},{1,0},{2,1},{3,2},{4,7},{5,4},{6,5},{7,6},{8,11},{9,8},{10,9... | collective-permute-start | bytes 1572872 | tf_op jit(solution)/shard_map/ppermute | solution.py:27
  25.6 8.4 %copy-start.16 = (f32[8,128,128]{2,1,0:T(8,128)}, f32[8,128,128]{2,1,0:T(8,128)S(1)}, u32[]{:S(2)}) copy-start(f32[8,128,128]{2,1,0:T(8,128)S(1)} %collective-permute-done.1.refs_2_) | copy-start | bytes 1572868
  25.6 15.2 %collective-permute-start.9 = (f32[8,128,128]{2,1,0:T(8,128)S(1)}, f32[8,128,128]{2,1,0:T(8,128)S(1)}, u32[]{:S(2)}, u32[]{:S(2)}) collective-permute-start(f32[8,128,128]{2,1,0:T(8,128)S(1)} %collective-permute-done.7.refs_0_), channel_id=1, source_target_pairs={{0,8},{1,9},{2,10},{3,11},{4,12},{5,13},{6,14},{7,15},{8,0},{9,1},... | collective-permute-start | bytes 1572872 | tf_op jit(solution)/shard_map/ppermute | solution.py:27
  30.8 29.9 %copy-start.13 = (f32[8,128,128]{2,1,0:T(8,128)}, f32[8,128,128]{2,1,0:T(8,128)S(1)}, u32[]{:S(2)}) copy-start(f32[8,128,128]{2,1,0:T(8,128)S(1)} %collective-permute-done.8.refs_1_) | copy-start | bytes 1572868
  30.8 11.7 %collective-permute-start.2 = (f32[8,128,128]{2,1,0:T(8,128)S(1)}, f32[8,128,128]{2,1,0:T(8,128)S(1)}, u32[]{:S(2)}, u32[]{:S(2)}) collective-permute-start(f32[8,128,128]{2,1,0:T(8,128)S(1)} %collective-permute-done.refs_1_), channel_id=1, source_target_pairs={{0,8},{1,9},{2,10},{3,11},{4,12},{5,13},{6,14},{7,15},{8,0},{9,1},... | collective-permute-start | bytes 1572872 | tf_op jit(solution)/shard_map/ppermute | solution.py:27
  33.9 27.9 %copy-start.12 = (f32[8,128,128]{2,1,0:T(8,128)}, f32[8,128,128]{2,1,0:T(8,128)S(1)}, u32[]{:S(2)}) copy-start(f32[8,128,128]{2,1,0:T(8,128)S(1)} %collective-permute-done.4.refs_1_) | copy-start | bytes 1572868
  33.9 14.4 %collective-permute-start.17 = (f32[128,1024]{1,0:T(8,128)}, f32[128,1024]{1,0:T(8,128)}, u32[]{:S(2)}, u32[]{:S(2)}) collective-permute-start(f32[128,1024]{1,0:T(8,128)} %refs_0_.1), channel_id=1, source_target_pairs={{0,2},{1,3},{2,0},{3,1},{4,6},{5,7},{6,4},{7,5},{8,10},{9,11},{10,... | collective-permute-start | bytes 1572872 | tf_op jit(solution)/shard_map/ppermute | solution.py:27
  39.3 20.1 %collective-permute-start.20 = (f32[128,1024]{1,0:T(8,128)}, f32[128,1024]{1,0:T(8,128)}, u32[]{:S(2)}, u32[]{:S(2)}) collective-permute-start(f32[128,1024]{1,0:T(8,128)} %collective-permute-done.18.refs_4_), channel_id=1, source_target_pairs={{0,3},{1,0},{2,1},{3,2},{4,7},{5,4},{6,5},{7,6},{8,11},{9,8},{10,9... | collective-permute-start | bytes 1572872 | tf_op jit(solution)/shard_map/ppermute | solution.py:27
  40.1 2.4 %copy-start.18 = (f32[128,1024]{1,0:T(8,128)}, f32[128,1024]{1,0:T(8,128)S(1)}, u32[]{:S(2)}) copy-start(f32[128,1024]{1,0:T(8,128)S(1)} %collective-permute-done.16.refs_2_) | copy-start | bytes 1572868
  40.1 20.5 %collective-permute-start.19 = (f32[128,1024]{1,0:T(8,128)}, f32[128,1024]{1,0:T(8,128)}, u32[]{:S(2)}, u32[]{:S(2)}) collective-permute-start(f32[128,1024]{1,0:T(8,128)} %collective-permute-done.18.refs_4_), channel_id=1, source_target_pairs={{0,1},{1,2},{2,3},{3,0},{4,5},{5,6},{6,7},{7,4},{8,9},{9,10},{10,1... | collective-permute-start | bytes 1572872 | tf_op jit(solution)/shard_map/ppermute | solution.py:27
  40.7 1.7 %copy-start.17 = (f32[8,128,128]{2,1,0:T(8,128)}, f32[8,128,128]{2,1,0:T(8,128)S(1)}, u32[]{:S(2)}) copy-start(f32[8,128,128]{2,1,0:T(8,128)S(1)} %collective-permute-done.9.refs_2_) | copy-start | bytes 1572868
  40.7 21.1 %collective-permute-start.12 = (f32[8,128,128]{2,1,0:T(8,128)}, f32[8,128,128]{2,1,0:T(8,128)}, u32[]{:S(2)}, u32[]{:S(2)}) collective-permute-start(f32[8,128,128]{2,1,0:T(8,128)} %pad_maximum_fusion.1), channel_id=1, source_target_pairs={{0,96},{1,97},{2,98},{3,99},{4,100},{5,101},{6,102},{7,103},{8,104... | collective-permute-start | bytes 1572872 | tf_op jit(solution)/shard_map/ppermute | solution.py:27
  42.5 5.9 %copy-start.19 = (f32[8,128,128]{2,1,0:T(8,128)}, f32[8,128,128]{2,1,0:T(8,128)S(1)}, u32[]{:S(2)}) copy-start(f32[8,128,128]{2,1,0:T(8,128)S(1)} %collective-permute-done.2.refs_3_) | copy-start | bytes 1572868
  42.5 19.5 %collective-permute-start.11 = (f32[8,128,128]{2,1,0:T(8,128)}, f32[8,128,128]{2,1,0:T(8,128)}, u32[]{:S(2)}, u32[]{:S(2)}) collective-permute-start(f32[8,128,128]{2,1,0:T(8,128)} %pad_maximum_fusion), channel_id=1, source_target_pairs={{0,32},{1,33},{2,34},{3,35},{4,36},{5,37},{6,38},{7,39},{8,40},{9,... | collective-permute-start | bytes 1572872 | tf_op jit(solution)/shard_map/ppermute | solution.py:27
  48.4 15.0 %collective-permute-start.21 = (f32[128,1024]{1,0:T(8,128)}, f32[128,1024]{1,0:T(8,128)}, u32[]{:S(2)}, u32[]{:S(2)}) collective-permute-start(f32[128,1024]{1,0:T(8,128)} %collective-permute-done.17.refs_3_), channel_id=1, source_target_pairs={{0,4},{1,5},{2,6},{3,7},{4,0},{5,1},{6,2},{7,3},{8,12},{9,13},{10,... | collective-permute-start | bytes 1572872 | tf_op jit(solution)/shard_map/ppermute | solution.py:27
  59.4 22.4 %collective-permute-start.5 = (f32[8,128,128]{2,1,0:T(8,128)S(1)}, f32[8,128,128]{2,1,0:T(8,128)S(1)}, u32[]{:S(2)}, u32[]{:S(2)}) collective-permute-start(f32[8,128,128]{2,1,0:T(8,128)S(1)} %collective-permute-done.3.refs_0_), channel_id=1, source_target_pairs={{0,8},{1,9},{2,10},{3,11},{4,12},{5,13},{6,14},{7,15},{8,0},{9,1},... | collective-permute-start | bytes 1572872 | tf_op jit(solution)/shard_map/ppermute | solution.py:27
  60.7 16.2 %collective-permute-start.10 = (f32[8,128,128]{2,1,0:T(8,128)S(1)}, f32[8,128,128]{2,1,0:T(8,128)}, u32[]{:S(2)}, u32[]{:S(2)}) collective-permute-start(f32[8,128,128]{2,1,0:T(8,128)S(1)} %collective-permute-done.8.refs_1_), channel_id=1, source_target_pairs={{0,8},{1,9},{2,10},{3,11},{4,12},{5,13},{6,14},{7,15},{8,0},{9,1},... | collective-permute-start | bytes 1572872 | tf_op jit(solution)/shard_map/ppermute | solution.py:27
  61.9 20.0 %collective-permute-start.6 = (f32[8,128,128]{2,1,0:T(8,128)S(1)}, f32[8,128,128]{2,1,0:T(8,128)S(1)}, u32[]{:S(2)}, u32[]{:S(2)}) collective-permute-start(f32[8,128,128]{2,1,0:T(8,128)S(1)} %collective-permute-done.4.refs_1_), channel_id=1, source_target_pairs={{0,8},{1,9},{2,10},{3,11},{4,12},{5,13},{6,14},{7,15},{8,0},{9,1},... | collective-permute-start | bytes 1572872 | tf_op jit(solution)/shard_map/ppermute | solution.py:27
  62.0 26.5 %collective-permute-start.14 = (f32[8,128,128]{2,1,0:T(8,128)}, f32[8,128,128]{2,1,0:T(8,128)}, u32[]{:S(2)}, u32[]{:S(2)}) collective-permute-start(f32[8,128,128]{2,1,0:T(8,128)} %collective-permute-done.12.refs_1_), channel_id=1, source_target_pairs={{0,8},{1,9},{2,10},{3,11},{4,12},{5,13},{6,14},{7,15},{8,0},{9,1},... | collective-permute-start | bytes 1572872 | tf_op jit(solution)/shard_map/ppermute | solution.py:27
  63.4 25.0 %collective-permute-start.13 = (f32[8,128,128]{2,1,0:T(8,128)}, f32[8,128,128]{2,1,0:T(8,128)}, u32[]{:S(2)}, u32[]{:S(2)}) collective-permute-start(f32[8,128,128]{2,1,0:T(8,128)} %collective-permute-done.11.refs_0_), channel_id=1, source_target_pairs={{0,8},{1,9},{2,10},{3,11},{4,12},{5,13},{6,14},{7,15},{8,0},{9,1},... | collective-permute-start | bytes 1572872 | tf_op jit(solution)/shard_map/ppermute | solution.py:27
  81.8 0.8 copy-start.20
  82.6 0.8 copy-start.21
  88.4 5.5 %copy-start = (bf16[8,128,1024]{2,1,0:T(8,128)(2,1)S(1)}, bf16[8,128,1024]{2,1,0:T(8,128)(2,1)}, u32[]{:S(2)}) copy-start(bf16[8,128,1024]{2,1,0:T(8,128)(2,1)} %get-tuple-element.27) | copy-start | bytes 6291460
  88.4 5.5 %copy-start.2 = (bf16[512,1024]{1,0:T(8,128)(2,1)S(1)}, bf16[512,1024]{1,0:T(8,128)(2,1)}, u32[]{:S(2)}) copy-start(bf16[512,1024]{1,0:T(8,128)(2,1)} %get-tuple-element.17.refs_0_) | copy-start | bytes 3145732
  94.0 1.6 %copy-start.1 = (bf16[8,128,1024]{2,1,0:T(8,128)(2,1)S(1)}, bf16[8,128,1024]{2,1,0:T(8,128)(2,1)}, u32[]{:S(2)}) copy-start(bf16[8,128,1024]{2,1,0:T(8,128)(2,1)} %get-tuple-element.28) | copy-start | bytes 6291460
  95.5 1.2 %copy-start.3 = (bf16[512,1024]{1,0:T(8,128)(2,1)S(1)}, bf16[512,1024]{1,0:T(8,128)(2,1)}, u32[]{:S(2)}) copy-start(bf16[512,1024]{1,0:T(8,128)(2,1)} %get-tuple-element.18.refs_1_) | copy-start | bytes 3145732
  96.8 1.2 %copy-start.4 = (bf16[512,1024]{1,0:T(8,128)(2,1)S(1)}, bf16[512,1024]{1,0:T(8,128)(2,1)}, u32[]{:S(2)}) copy-start(bf16[512,1024]{1,0:T(8,128)(2,1)} %get-tuple-element.21.refs_4_) | copy-start | bytes 3145732
  98.0 1.2 %copy-start.5 = (bf16[512,1024]{1,0:T(8,128)(2,1)S(1)}, bf16[512,1024]{1,0:T(8,128)(2,1)}, u32[]{:S(2)}) copy-start(bf16[512,1024]{1,0:T(8,128)(2,1)} %get-tuple-element.22.refs_5_) | copy-start | bytes 3145732
  99.2 1.2 %copy-start.6 = (bf16[512,1024]{1,0:T(8,128)(2,1)S(1)}, bf16[512,1024]{1,0:T(8,128)(2,1)}, u32[]{:S(2)}) copy-start(bf16[512,1024]{1,0:T(8,128)(2,1)} %get-tuple-element.19.refs_2_) | copy-start | bytes 3145732
  100.4 1.2 %copy-start.7 = (bf16[512,1024]{1,0:T(8,128)(2,1)S(1)}, bf16[512,1024]{1,0:T(8,128)(2,1)}, u32[]{:S(2)}) copy-start(bf16[512,1024]{1,0:T(8,128)(2,1)} %get-tuple-element.20.refs_3_) | copy-start | bytes 3145732
  101.7 1.2 %copy-start.8 = (bf16[512,1024]{1,0:T(8,128)(2,1)S(1)}, bf16[512,1024]{1,0:T(8,128)(2,1)}, u32[]{:S(2)}) copy-start(bf16[512,1024]{1,0:T(8,128)(2,1)} %get-tuple-element.23.refs_6_) | copy-start | bytes 3145732
  102.9 1.2 %copy-start.9 = (bf16[512,1024]{1,0:T(8,128)(2,1)S(1)}, bf16[512,1024]{1,0:T(8,128)(2,1)}, u32[]{:S(2)}) copy-start(bf16[512,1024]{1,0:T(8,128)(2,1)} %get-tuple-element.24.refs_7_) | copy-start | bytes 3145732

commit v2 on v0

v2 whole, which is shorter than its diff:
```python
import functools

import jax
import jax.numpy as jnp
import numpy as np
from jax import lax
from jax.experimental import pallas as pl
from jax.experimental.pallas import tpu as pltpu
from jax.sharding import Mesh, PartitionSpec as P

ROW = ("y", "xl", "core")
COL = ("xh", "z")
AXES = ROW + COL
SIZES = (4, 2, 2, 2, 4)
f32, bf16 = jnp.float32, jnp.bfloat16
MIB = 1 << 20
HALF = 64


def hop(value, **move):
    pairs = []
    for source in range(int(np.prod(SIZES))):
        place = list(np.unravel_index(source, SIZES))
        for axis, step in move.items():
            k = AXES.index(axis)
            place[k] = (place[k] + step) % SIZES[k]
        pairs.append((source, int(np.ravel_multi_index(place, SIZES))))
    return lax.ppermute(value, AXES, pairs)


def after(value, *needed):
    return lax.optimization_barrier((value,) + needed)[0]


def split(value):
    high = value.astype(bf16)
    return high, (value - high.astype(f32)).astype(bf16)


def turn_kernel(amp_ref, out_ref):
    for n in range(out_ref.shape[0]):
        lanes = slice(n * 128, n * 128 + 128)
        both = jnp.concatenate([amp_ref[0, lanes], amp_ref[1, lanes]], axis=1)
        out_ref[n] = both.T


def turn(amp):
    two, depth, width = amp.shape
    return pl.pallas_call(
        turn_kernel,
        out_shape=jax.ShapeDtypeStruct((depth // 128, two * width, 128), f32),
        in_specs=[pl.BlockSpec(memory_space=pltpu.VMEM)],
        out_specs=pl.BlockSpec(memory_space=pltpu.VMEM),
        name="turn",
    )(amp)


def dense(info_ref, held, order, high_refs, low_refs):
    width = held.shape[1] // 8
    for h in range(2):
        base = info_ref[order + h] * 4
        for k in range(4):
            block = held.at[base + k]
            for a in range(0, width, 2):
                value = jnp.concatenate([block[pl.ds(a + b, 8, stride=width), :] for b in range(2)], axis=0)
                high, low = split(value)
                high_refs[h][a * 8 : a * 8 + 16, k * 128 : k * 128 + 128] = high
                low_refs[h][a * 8 : a * 8 + 16, k * 128 : k * 128 + 128] = low


def three(high, low, whigh, wlow):
    total = jnp.dot(high, whigh, preferred_element_type=f32)
    total += jnp.dot(high, wlow, preferred_element_type=f32)
    return total + jnp.dot(low, whigh, preferred_element_type=f32)


def pull(info_ref, held, sems, pieces):
    copies = []
    for n, (ref, start, rows, slot, offset) in enumerate(pieces):
        row = pl.multiple_of(info_ref[slot] * (2 * HALF) + offset, 8)
        copies.append(pltpu.make_async_copy(ref.at[:, pl.ds(start, rows)], held.at[:, pl.ds(row, rows)], sems.at[n]))
    return copies


def pull_w(info_ref, held, sems, refs):
    return [pltpu.make_async_copy(ref, held.at[info_ref[8 + n]], sems.at[n]) for n, ref in enumerate(refs)]


def early_kernel(info_ref, x, xx, s1, xp, xxp, xm, xxm, s2, w, wp, wm, w2,
                 part_ref, ahigh_ref, alow_ref, whigh_ref, wlow_ref, held, wheld, high, low, sems, wsems):
    chunk = pl.program_id(0)
    both = 2 * HALF
    sets = [
        [(x, 0, both, 0, 0), (xx, 0, both, 1, 0), (s1, 0, both, 2, 0), (s1, both, both, 3, 0)],
        [(xp, 0, both, 0, 0), (xxp, 0, both, 1, 0), (s1, 2 * both, both, 2, 0), (s2, 0, both, 3, 0)],
        [(xm, 0, both, 0, 0), (xxm, 0, both, 1, 0), (s1, 3 * both, both, 2, 0), (s2, both, both, 3, 0)],
    ]
    copies = [pull(info_ref, held.at[j], sems.at[j], sets[j]) for j in range(3)]
    wcopies = pull_w(info_ref, wheld, wsems, [w, wp, wm, w2])

    @pl.when(chunk == 0)
    def _():
        for copy in copies[0] + wcopies + copies[1] + copies[2]:
            copy.start()
        for copy in wcopies:
            copy.wait()
        for n in range(4):
            h, l = split(wheld[n])
            whigh_ref[n * 128 : n * 128 + 128] = h
            wlow_ref[n * 128 : n * 128 + 128] = l

    for j in range(3):
        @pl.when(chunk == j)
        def _():
            for copy in copies[j]:
                copy.wait()

    dense(info_ref, held.at[chunk], 12, [high, ahigh_ref], [low, alow_ref])
    for n in range(0, part_ref.shape[1], 256):
        part_ref[:, n : n + 256] = three(high[...], low[...], whigh_ref[:, n : n + 256], wlow_ref[:, n : n + 256])


def early(info, sources, weights):
    columns = weights[0].shape[1]
    rows = 8 * HALF
    depth = 4 * 128
    return pl.pallas_call(
        early_kernel,
        out_shape=[
            jax.ShapeDtypeStruct((3 * rows, columns), f32),
            jax.ShapeDtypeStruct((3 * rows, depth), bf16),
            jax.ShapeDtypeStruct((3 * rows, depth), bf16),
            jax.ShapeDtypeStruct((depth, columns), bf16),
            jax.ShapeDtypeStruct((depth, columns), bf16),
        ],
        grid_spec=pltpu.PrefetchScalarGridSpec(
            num_scalar_prefetch=1,
            grid=(3,),
            in_specs=[pl.BlockSpec(memory_space=pltpu.HBM)] * 12,
            out_specs=[
                pl.BlockSpec((rows, columns), lambda c, i: (c, 0)),
                pl.BlockSpec((rows, depth), lambda c, i: (c, 0)),
                pl.BlockSpec((rows, depth), lambda c, i: (c, 0)),
                pl.BlockSpec((depth, columns), lambda c, i: (0, 0)),
                pl.BlockSpec((depth, columns), lambda c, i: (0, 0)),
            ],
            scratch_shapes=[
                pltpu.VMEM((3, 8, rows, 128), f32),
                pltpu.VMEM((4, 128, columns), f32),
                pltpu.VMEM((rows, depth), bf16),
                pltpu.VMEM((rows, depth), bf16),
                pltpu.SemaphoreType.DMA((3, 4)),
                pltpu.SemaphoreType.DMA((4,)),
            ],
        ),
        compiler_params=pltpu.CompilerParams(vmem_limit_bytes=60 * MIB),
        cost_estimate=pl.CostEstimate(flops=18 * rows * depth * columns, bytes_accessed=20 * MIB, transcendentals=0),
        name="early",
    )(info, *sources, *weights)


def late_kernel(info_ref, part_ref, ahigh_ref, alow_ref, whigh_ref, wlow_ref, rgap_ref, cgap_ref,
                up, down, s3, wx, wxp, wxm, wx2,
                out_ref, held, wheld, whigh2, wlow2, high, low, high2, low2, sems, wsems):
    chunk = pl.program_id(0)
    last = 3
    columns = whigh_ref.shape[1]
    pieces = []
    for ref, base, slot in ((up, 0, 0), (down, 0, 0), (s3, 0, 2), (s3, 2 * HALF, 2)):
        offset = HALF * (len(pieces) // 2 % 2)
        pieces += [(ref, base, HALF, slot, offset), (ref, base + HALF, HALF, slot + 1, offset)]
    copies = pull(info_ref, held, sems, pieces)
    wcopies = pull_w(info_ref, wheld, wsems, [wx, wxp, wxm, wx2])

    @pl.when(chunk == 0)
    def _():
        for copy in wcopies + copies:
            copy.start()
        for copy in wcopies:
            copy.wait()
        for n in range(4):
            h, l = split(wheld[n])
            whigh2[n * 128 : n * 128 + 128] = h
            wlow2[n * 128 : n * 128 + 128] = l

    tall = rgap_ref[...].reshape(-1, 128)

    def finish(n, total):
        for m in range(0, 256, 128):
            gap = tall + cgap_ref[:, n + m : n + m + 128]
            out_ref[:, 0, :, n + m : n + m + 128] = (total[:, m : m + 128] / gap).reshape(-1, 8, 128)

    @pl.when(chunk < last)
    def _():
        for n in range(0, columns, 256):
            cut = slice(n, n + 256)
            total = part_ref[:, cut] + three(ahigh_ref[...], alow_ref[...], whigh2[:, cut], wlow2[:, cut])
            finish(n, total)

    @pl.when(chunk == last)
    def _():
        for copy in copies:
            copy.wait()
        dense(info_ref, held, 12, [high, high2], [low, low2])
        for n in range(0, columns, 256):
            cut = slice(n, n + 256)
            total = three(high[...], low[...], whigh_ref[:, cut], wlow_ref[:, cut])
            total += three(high2[...], low2[...], whigh2[:, cut], wlow2[:, cut])
            finish(n, total)


def late(info, made, rgap, cgap, sources, weights, virtuals):
    columns = weights[0].shape[1]
    rows = 8 * HALF
    depth = 4 * 128
    block = lambda width: pl.BlockSpec((rows, width), lambda c, i: (jnp.minimum(c, 2), 0))
    fixed = lambda *shape: pl.BlockSpec(shape, lambda c, i: (0, 0))
    return pl.pallas_call(
        late_kernel,
        out_shape=jax.ShapeDtypeStruct((virtuals, 4, 8, columns), f32),
        grid_spec=pltpu.PrefetchScalarGridSpec(
            num_scalar_prefetch=1,
            grid=(4,),
            in_specs=[block(columns), block(depth), block(depth), fixed(depth, columns), fixed(depth, columns)]
            + [pl.BlockSpec((virtuals, 1, 8, 128), lambda c, i: (0, i[4 + c], 0, 0)), fixed(1, columns)]
            + [pl.BlockSpec(memory_space=pltpu.HBM)] * 7,
            out_specs=pl.BlockSpec((virtuals, 1, 8, columns), lambda c, i: (0, i[4 + c], 0, 0)),
            scratch_shapes=[
                pltpu.VMEM((8, rows, 128), f32),
                pltpu.VMEM((4, 128, columns), f32),
                pltpu.VMEM((depth, columns), bf16),
                pltpu.VMEM((depth, columns), bf16),
            ]
            + [pltpu.VMEM((rows, depth), bf16)] * 4
            + [pltpu.SemaphoreType.DMA((8,)), pltpu.SemaphoreType.DMA((4,))],
        ),
        compiler_params=pltpu.CompilerParams(vmem_limit_bytes=60 * MIB),
        cost_estimate=pl.CostEstimate(flops=30 * rows * depth * columns, bytes_accessed=24 * MIB, transcendentals=0),
        name="late",
    )(info, *made, rgap, cgap, *sources, *weights)


def body(amplitudes, integrals, occ_energy, vir_energy):
    virtuals, own = amplitudes.shape[:2]
    depth = amplitudes.shape[2] * amplitudes.shape[3]
    columns = integrals.shape[1]
    y, xl, core, xh, z = (lax.axis_index(a) for a in AXES)

    info = jnp.stack(
        [xl * 2 + core, (1 - xl) * 2 + core, xl * 2 + 1 - core, (1 - xl) * 2 + 1 - core]
        + [y, (y + 3) % 4, (y + 1) % 4, (y + 2) % 4]
        + [z, (z + 3) % 4, (z + 1) % 4, (z + 2) % 4]
        + [xh, 1 - xh]
    ).astype(jnp.int32)
    gap = vir_energy[:, None] - occ_energy[None, :]
    row_gap = lax.dynamic_slice_in_dim(gap, (xh * 4 + z) * virtuals, virtuals)
    rgap = jnp.broadcast_to(row_gap.reshape(virtuals, 4, 8, 1), (virtuals, 4, 8, 128))
    start = ((y * 2 + xl) * 2 + core) * columns
    cgap = lax.dynamic_slice_in_dim(gap.reshape(-1), start, columns).reshape(1, columns)
    info, rgap, cgap = lax.optimization_barrier((info, rgap, cgap))

    join = lambda *values: jnp.concatenate(values, axis=1)
    x = turn(amplitudes.transpose(1, 2, 3, 0).reshape(own, depth, virtuals))
    w = integrals

    wp, wm = hop(w, z=1), hop(w, z=3)
    xp, xm, xx = hop(x, y=1), hop(x, y=3), hop(x, xl=1)
    wp, wm, xp, xm, xx, w, x = lax.optimization_barrier((wp, wm, xp, xm, xx, w, x))
    xxp, xxm, w2, wx = hop(xx, y=1), hop(xx, y=3), hop(w, z=2), hop(w, xh=1)
    s1 = hop(join(x, xx, xp, xm), core=1)
    xxp, xxm, w2, wx, s1 = lax.optimization_barrier((xxp, xxm, w2, wx, s1))
    s2 = hop(join(xxp, xxm), core=1)
    up = hop(join(xp[:, :HALF], xxp[:, :HALF]), y=1)
    down = hop(join(xm[:, HALF:], xxm[:, HALF:]), y=3)
    wxp, wxm, wx2 = hop(wx, z=1), hop(wx, z=3), hop(w2, xh=1)
    made = early(info, [x, xx, s1, xp, xxp, xm, xxm, s2], [w, wp, wm, w2])
    up, down, wxp, wxm, wx2, *made = lax.optimization_barrier((up, down, wxp, wxm, wx2, *made))
    s3 = hop(join(up, down), core=1)
    out = late(info, made, rgap, cgap, [up, down, s3], [wx, wxp, wxm, wx2], virtuals)
    return out.reshape(virtuals * 32, columns)


def solution(mesh):
    fine = Mesh(mesh.devices.reshape(SIZES), AXES)
    in_specs = (P(COL, ROW, None, None), P(COL, ROW), P(), P())
    return jax.shard_map(body, mesh=fine, in_specs=in_specs, out_specs=P(COL, ROW), check_vma=False)
```

time: 218 us -> 96.7 us (0.44)
  waiting for transfers between devices: 114 us -> 27.2 us
  local copies, waits for them, and re-layouts: 56.8 us -> 4.94 us
  Pallas kernels: 0 us -> 35.9 us
  matrix products: 31.9 us -> 0 us
  starting transfers between devices: 0.04 us -> 25.1 us
  between operations: 13.4 us -> 0.45 us
    all_gather x2 -> x0, waiting for transfers between devices: 113 us -> none  [the longest x1 95.3 us: body(): portion = lax.all_gather(amplitudes, 'row', axis=1, tiled=True)]
    pallas_call x0 -> x3, Pallas kernels: none -> 35.9 us  [the longest x1 18.2 us: late(): pl.pallas_call(late_kernel, out_shape=jax.ShapeDtypeStruct((virtuals, 4,...]
    dot_general x1 -> x0, matrix products: 31.9 us -> none  [body(): jnp.dot(flattened, whole_w, preferred_element_type=jnp.float32, precision...]
    all_gather x1 -> x0, local copies, waits for them, and re-layouts: 30.4 us -> none  [body(): portion = lax.all_gather(amplitudes, 'row', axis=1, tiled=True)]
    ppermute x0 -> x17, waiting for transfers between devices: none -> 27.2 us  [hop(): return lax.ppermute(value, AXES, pairs)]
    reshape x1 -> x0, local copies, waits for them, and re-layouts: 26.3 us -> none  [body(): portion.reshape(virtuals * amount, portion.shape[2] * portion.shape[3])]
    ppermute x0 -> x17, starting transfers between devices: none -> 25.1 us  [hop(): return lax.ppermute(value, AXES, pairs)]
    concatenate x0 -> x5, other arithmetic: none -> 2.78 us  [body(): join = lambda *values: jnp.concatenate(values, axis=1)]
  transfers between devices with their start and end apart: 2 -> 17, of which waited for: 2 -> 9; matrix products, arithmetic and copies ran while one was open for 27% -> 3% of each run, Pallas kernels for 0% -> 16%
where the time goes in v2:
time: 96.7 us; the launch traced here: 96.5 us
  Pallas kernels  35.9 us (37%)
  waiting for transfers between devices  27.2 us (28%)
  starting transfers between devices  25.1 us (26%)
  local copies, waits for them, and re-layouts  4.94 us (5%)
  other arithmetic  2.86 us (3%)
    ppermute x17, waiting for transfers between devices, hop(): return lax.ppermute(value, AXES, pairs)  27.2 us
    ppermute x17, starting transfers between devices, hop(): return lax.ppermute(value, AXES, pairs)  25.1 us
    pallas_call x1, Pallas kernels, late(): pl.pallas_call(late_kernel, out_shape=jax.ShapeDtypeStruct((virtuals, 4,...  18.2 us
    pallas_call x1, Pallas kernels, early(): pl.pallas_call(early_kernel, out_shape=[jax.ShapeDtypeStruct((3 * rows, c...  15.3 us
    concatenate x5, other arithmetic, body(): join = lambda *values: jnp.concatenate(values, axis=1)  2.78 us
    pallas_call x1, Pallas kernels, turn(): pl.pallas_call(turn_kernel, out_shape=jax.ShapeDtypeStruct((depth // 128,...  2.37 us
  transfers between devices with their start and end apart: 17, of which 9 were waited for; matrix products, arithmetic and copies ran while one was open for 3% of the time, Pallas kernels for 16%

profile of v2, /device:TPU:1, one launch (start us, length us, event | category | flops | bytes accessed | tf_op | source)
XLA Modules:
  0.0 96.5 jit_solution(14575554356268699804)
XLA Ops:
  0.0 2.4 %turn.1.x = f32[8,128,128]{2,1,0:T(8,128)} custom-call(f32[2,1024,64]{2,1,0:T(8,128)} %bitcast.21), custom_call_target="tpu_custom_call" | custom-call | tf_op jit(solution)/shard_map/turn/pallas_call | solution.py:49
  2.4 2.0 %collective-permute-start.4 = (f32[8,128,128]{2,1,0:T(8,128)}, f32[8,128,128]{2,1,0:T(8,128)S(1)}, u32[]{:S(2)}, u32[]{:S(2)}) collective-permute-start(f32[8,128,128]{2,1,0:T(8,128)} %turn.1.x), channel_id=1, source_target_pairs={{0,16},{1,17},{2,18},{3,19},{4,20},{5,21},{6,22},{7,23},{8,24},{9,... | collective-permute-start | bytes 1572872 | tf_op jit(solution)/shard_map/ppermute | solution.py:28
  4.4 2.7 %collective-permute-start.3 = (f32[8,128,128]{2,1,0:T(8,128)}, f32[8,128,128]{2,1,0:T(8,128)S(1)}, u32[]{:S(2)}, u32[]{:S(2)}) collective-permute-start(f32[8,128,128]{2,1,0:T(8,128)} %turn.1.x), channel_id=1, source_target_pairs={{0,96},{1,97},{2,98},{3,99},{4,100},{5,101},{6,102},{7,103},{8,104... | collective-permute-start | bytes 1572872 | tf_op jit(solution)/shard_map/ppermute | solution.py:28
  7.2 0.0 collective-permute-start.2
  7.2 1.6 %collective-permute-start = (f32[128,1024]{1,0:T(8,128)}, f32[128,1024]{1,0:T(8,128)S(1)}, u32[]{:S(2)}, u32[]{:S(2)}) collective-permute-start(f32[128,1024]{1,0:T(8,128)} %w), channel_id=1, source_target_pairs={{0,1},{1,2},{2,3},{3,0},{4,5},{5,6},{6,7},{7,4},{8,9},{9,10},{10,1... | collective-permute-start | bytes 1572872 | tf_op jit(solution)/shard_map/ppermute | solution.py:28
  8.8 2.1 %collective-permute-start.1 = (f32[128,1024]{1,0:T(8,128)}, f32[128,1024]{1,0:T(8,128)}, u32[]{:S(2)}, u32[]{:S(2)}) collective-permute-start(f32[128,1024]{1,0:T(8,128)} %w), channel_id=1, source_target_pairs={{0,3},{1,0},{2,1},{3,2},{4,7},{5,4},{6,5},{7,6},{8,11},{9,8},{10,9... | collective-permute-start | bytes 1572872 | tf_op jit(solution)/shard_map/ppermute | solution.py:28
  10.9 5.0 %collective-permute-done.4.xx = f32[8,128,128]{2,1,0:T(8,128)S(1)} collective-permute-done((f32[8,128,128]{2,1,0:T(8,128)}, f32[8,128,128]{2,1,0:T(8,128)S(1)}, u32[]{:S(2)}, u32[]{:S(2)}) %collective-permute-start.4) | collective-permute-done | bytes 524320 | tf_op jit(solution)/shard_map/ppermute | solution.py:28
  15.9 1.9 %collective-permute-done.3.xm = f32[8,128,128]{2,1,0:T(8,128)S(1)} collective-permute-done((f32[8,128,128]{2,1,0:T(8,128)}, f32[8,128,128]{2,1,0:T(8,128)S(1)}, u32[]{:S(2)}, u32[]{:S(2)}) %collective-permute-start.3) | collective-permute-done | bytes 524320 | tf_op jit(solution)/shard_map/ppermute | solution.py:28
  17.7 3.0 %collective-permute-done.2.xp = f32[8,128,128]{2,1,0:T(8,128)S(1)} collective-permute-done((f32[8,128,128]{2,1,0:T(8,128)}, f32[8,128,128]{2,1,0:T(8,128)S(1)}, u32[]{:S(2)}, u32[]{:S(2)}) %collective-permute-start.2) | collective-permute-done | bytes 524320 | tf_op jit(solution)/shard_map/ppermute | solution.py:28
  20.8 1.4 %collective-permute-done.wp = f32[128,1024]{1,0:T(8,128)S(1)} collective-permute-done((f32[128,1024]{1,0:T(8,128)}, f32[128,1024]{1,0:T(8,128)S(1)}, u32[]{:S(2)}, u32[]{:S(2)}) %collective-permute-start) | collective-permute-done | bytes 524320 | tf_op jit(solution)/shard_map/ppermute | solution.py:28
  22.1 0.8 copy-done.10
  22.9 0.0 collective-permute-done.1.wm
  22.9 1.2 %pad_maximum_fusion = f32[8,512,128]{2,1,0:T(8,128)S(1)} fusion(f32[8,128,128]{2,1,0:T(8,128)S(1)} %collective-permute-done.3.xm, f32[8,128,128]{2,1,0:T(8,128)S(1)} %collective-permute-done.2.xp, f32[8,128,128]{2,1,0:T(8,128)S(1)} %collective-permute-done.4.xx, f32[8,128,128]{2,1,0:T(8,128)} %turn.1.x), kind=kLoop, calls=%fused_computation | loop fusion | flops 1572864 | bytes 4194304 | tf_op jit(solution)/shard_map/concatenate | solution.py:262
  24.1 0.0 copy-start.6
  24.1 0.0 copy-start.7
  24.1 1.9 %collective-permute-start.9 = (f32[8,512,128]{2,1,0:T(8,128)S(1)}, f32[8,512,128]{2,1,0:T(8,128)}, u32[]{:S(2)}, u32[]{:S(2)}) collective-permute-start(f32[8,512,128]{2,1,0:T(8,128)S(1)} %pad_maximum_fusion), channel_id=1, source_target_pairs={{0,8},{1,9},{2,10},{3,11},{4,12},{5,13},{6,14},{7,15},{8,0},{9,1},... | collective-permute-start | bytes 6291464 | tf_op jit(solution)/shard_map/ppermute | solution.py:28
  26.1 0.0 copy-done.9
  26.1 2.5 %collective-permute-start.8 = (f32[128,1024]{1,0:T(8,128)S(1)}, f32[128,1024]{1,0:T(8,128)}, u32[]{:S(2)}, u32[]{:S(2)}) collective-permute-start(f32[128,1024]{1,0:T(8,128)S(1)} %copy-done.9), channel_id=1, source_target_pairs={{0,4},{1,5},{2,6},{3,7},{4,0},{5,1},{6,2},{7,3},{8,12},{9,13},{10,... | collective-permute-start | bytes 1572872 | tf_op jit(solution)/shard_map/ppermute | solution.py:28
  28.6 2.6 %collective-permute-start.7 = (f32[128,1024]{1,0:T(8,128)S(1)}, f32[128,1024]{1,0:T(8,128)}, u32[]{:S(2)}, u32[]{:S(2)}) collective-permute-start(f32[128,1024]{1,0:T(8,128)S(1)} %copy-done.9), channel_id=1, source_target_pairs={{0,2},{1,3},{2,0},{3,1},{4,6},{5,7},{6,4},{7,5},{8,10},{9,11},{10,... | collective-permute-start | bytes 1572872 | tf_op jit(solution)/shard_map/ppermute | solution.py:28
  31.1 2.1 %collective-permute-start.6 = (f32[8,128,128]{2,1,0:T(8,128)S(1)}, f32[8,128,128]{2,1,0:T(8,128)S(1)}, u32[]{:S(2)}, u32[]{:S(2)}) collective-permute-start(f32[8,128,128]{2,1,0:T(8,128)S(1)} %collective-permute-done.4.xx), channel_id=1, source_target_pairs={{0,96},{1,97},{2,98},{3,99},{4,100},{5,101},{6,102},{7,103},{8,104... | collective-permute-start | bytes 1572872 | tf_op jit(solution)/shard_map/ppermute | solution.py:28
  33.2 0.0 copy-done.5
  33.2 0.0 collective-permute-start.5
  33.2 8.0 %collective-permute-done.8.wx = f32[128,1024]{1,0:T(8,128)} collective-permute-done((f32[128,1024]{1,0:T(8,128)S(1)}, f32[128,1024]{1,0:T(8,128)}, u32[]{:S(2)}, u32[]{:S(2)}) %collective-permute-start.8) | collective-permute-done | bytes 524320 | tf_op jit(solution)/shard_map/ppermute | solution.py:28
  41.2 2.1 %collective-permute-done.7.w2 = f32[128,1024]{1,0:T(8,128)} collective-permute-done((f32[128,1024]{1,0:T(8,128)S(1)}, f32[128,1024]{1,0:T(8,128)}, u32[]{:S(2)}, u32[]{:S(2)}) %collective-permute-start.7) | collective-permute-done | bytes 524320 | tf_op jit(solution)/shard_map/ppermute | solution.py:28
  43.3 0.7 collective-permute-done.6.xxm
  44.1 2.9 %collective-permute-done.5.xxp = f32[8,128,128]{2,1,0:T(8,128)S(1)} collective-permute-done((f32[8,128,128]{2,1,0:T(8,128)S(1)}, f32[8,128,128]{2,1,0:T(8,128)S(1)}, u32[]{:S(2)}, u32[]{:S(2)}) %collective-permute-start.5) | collective-permute-done | bytes 524320 | tf_op jit(solution)/shard_map/ppermute | solution.py:28
  46.9 0.0 collective-permute-done.9.s1
  46.9 0.1 pad_maximum_fusion.1
  47.0 1.9 %collective-permute-start.15 = (f32[8,256,128]{2,1,0:T(8,128)S(1)}, f32[8,256,128]{2,1,0:T(8,128)}, u32[]{:S(2)}, u32[]{:S(2)}) collective-permute-start(f32[8,256,128]{2,1,0:T(8,128)S(1)} %pad_maximum_fusion.1), channel_id=1, source_target_pairs={{0,8},{1,9},{2,10},{3,11},{4,12},{5,13},{6,14},{7,15},{8,0},{9,1},... | collective-permute-start | bytes 3145736 | tf_op jit(solution)/shard_map/ppermute | solution.py:28
  48.9 0.0 copy-done.6
  48.9 0.0 copy-done.7
  48.9 0.1 broadcast_subtract_fusion
  49.0 0.1 copy.6
  49.1 0.0 copy-done.3
  49.1 0.0 copy-done.2
  49.1 0.0 slice-start
  49.2 0.0 copy-done
  49.2 0.0 copy-done.1
  49.3 0.8 collective-permute-start.13
  50.0 0.7 collective-permute-start.12
  50.8 0.1 collective-permute-start.11
  50.9 0.0 slice-done
  51.0 1.5 %collective-permute-start.10 = (f32[8,128,128]{2,1,0:T(8,128)S(1)}, f32[8,128,128]{2,1,0:T(8,128)S(1)}, u32[]{:S(2)}, u32[]{:S(2)}) collective-permute-start(f32[8,128,128]{2,1,0:T(8,128)S(1)} %pad_maximum_fusion.3), channel_id=1, source_target_pairs={{0,32},{1,33},{2,34},{3,35},{4,36},{5,37},{6,38},{7,39},{8,40},{9,... | collective-permute-start | bytes 1572872 | tf_op jit(solution)/shard_map/ppermute | solution.py:28
  52.5 0.0 collective-permute-done.15.s2
  52.5 0.5 collective-permute-start.14
  53.0 0.1 dynamic-slice_bitcast_fusion
  53.1 0.1 copy.5
  53.2 0.1 sub.37
  53.4 0.6 dynamic_slice.7
  54.0 0.7 stack.59.info_ref
  54.7 1.3 %broadcast_in_dim.10.rgap_ref = f32[64,4,8,128]{3,2,1,0:T(8,128)} broadcast(f32[64,4,8]{2,1,0:T(4,128)S(1)} %copy.5), dimensions={0,1,2} | broadcast | bytes 1056768 | tf_op jit(solution)/shard_map/broadcast_in_dim | solution.py:257
  56.0 15.3 %early.1 = (f32[1536,1024]{1,0:T(8,128)}, bf16[1536,512]{1,0:T(8,128)(2,1)}, bf16[1536,512]{1,0:T(8,128)(2,1)}, bf16[512,1024]{1,0:T(8,128)(2,1)}, bf16[512,1024]{1,0:T(8,128)(2,1)}) custom-call(s32[14]{0:T(128)} %stack.59.info_ref, f32[8,128,128]{2,1,0:T(8,128)} %turn.1.x, f32[8,128,128]{2,1,0:T(8,128)} %copy-done.5, ...), custom_call_target="tpu_custom_call" | custom-call | flops 4831838208 | bytes 20971520 | tf_op jit(solution)/shard_map/early/pallas_call | solution.py:127
  71.3 0.0 collective-permute-done.11.down
  71.3 0.0 collective-permute-done.10.up
  71.4 0.0 copy-start.4
  71.4 0.0 collective-permute-done.14.wx2
  71.4 0.0 copy-start.11
  71.4 0.0 collective-permute-done.13.wxm
  71.4 0.0 collective-permute-done.12.wxp
  71.4 1.5 %pad_maximum_fusion.2 = f32[8,256,128]{2,1,0:T(8,128)S(1)} fusion(f32[8,128,128]{2,1,0:T(8,128)} %collective-permute-done.11.down, f32[8,128,128]{2,1,0:T(8,128)S(1)} %collective-permute-done.10.up), kind=kLoop, calls=%fused_computation.2 | loop fusion | flops 262144 | bytes 2097152 | tf_op jit(solution)/shard_map/concatenate | solution.py:262
  72.9 2.0 %collective-permute-start.16 = (f32[8,256,128]{2,1,0:T(8,128)S(1)}, f32[8,256,128]{2,1,0:T(8,128)S(1)}, u32[]{:S(2)}, u32[]{:S(2)}) collective-permute-start(f32[8,256,128]{2,1,0:T(8,128)S(1)} %pad_maximum_fusion.2), channel_id=1, source_target_pairs={{0,8},{1,9},{2,10},{3,11},{4,12},{5,13},{6,14},{7,15},{8,0},{9,1},... | collective-permute-start | bytes 3145736 | tf_op jit(solution)/shard_map/ppermute | solution.py:28
  74.8 2.3 %collective-permute-done.16.s3 = f32[8,256,128]{2,1,0:T(8,128)S(1)} collective-permute-done((f32[8,256,128]{2,1,0:T(8,128)S(1)}, f32[8,256,128]{2,1,0:T(8,128)S(1)}, u32[]{:S(2)}, u32[]{:S(2)}) %collective-permute-start.16) | collective-permute-done | bytes 1048608 | tf_op jit(solution)/shard_map/ppermute | solution.py:28
  77.1 1.0 %copy-done.8 = f32[8,256,128]{2,1,0:T(8,128)} copy-done((f32[8,256,128]{2,1,0:T(8,128)}, f32[8,256,128]{2,1,0:T(8,128)S(1)}, u32[]{:S(2)}) %copy-start.8) | copy-done | bytes 1048600
  78.1 18.2 %late.1 = f32[64,4,8,1024]{3,2,1,0:T(8,128)} custom-call(s32[14]{0:T(128)} %stack.59.info_ref, f32[1536,1024]{1,0:T(8,128)} %get-tuple-element.53.part_ref, bf16[1536,512]{1,0:T(8,128)(2,1)} %get-tuple-element.54.ahigh_ref, bf16[1536,512]{1,0:T(8,128)(2,1)} %get-tuple-element.55.alow_ref, bf16[512,1024]{1,0:T(8,128)(2,1)} %get-tuple-element.56.whigh_ref, ...), custom_call_target="tpu_custom_call" | custom-call | flops 8053063680 | bytes 25165824 | tf_op jit(solution)/shard_map/late/pallas_call | solution.py:218
  (15 shorter events, 0.1 us)
Async XLA Ops:
  2.4 23.7 %copy-start.9 = (f32[128,1024]{1,0:T(8,128)S(1)}, f32[128,1024]{1,0:T(8,128)}, u32[]{:S(2)}) copy-start(f32[128,1024]{1,0:T(8,128)} %w) | copy-start | bytes 1572868
  2.4 13.5 %collective-permute-start.4 = (f32[8,128,128]{2,1,0:T(8,128)}, f32[8,128,128]{2,1,0:T(8,128)S(1)}, u32[]{:S(2)}, u32[]{:S(2)}) collective-permute-start(f32[8,128,128]{2,1,0:T(8,128)} %turn.1.x), channel_id=1, source_target_pairs={{0,16},{1,17},{2,18},{3,19},{4,20},{5,21},{6,22},{7,23},{8,24},{9,... | collective-permute-start | bytes 1572872 | tf_op jit(solution)/shard_map/ppermute | solution.py:28
  4.4 13.3 %collective-permute-start.3 = (f32[8,128,128]{2,1,0:T(8,128)}, f32[8,128,128]{2,1,0:T(8,128)S(1)}, u32[]{:S(2)}, u32[]{:S(2)}) collective-permute-start(f32[8,128,128]{2,1,0:T(8,128)} %turn.1.x), channel_id=1, source_target_pairs={{0,96},{1,97},{2,98},{3,99},{4,100},{5,101},{6,102},{7,103},{8,104... | collective-permute-start | bytes 1572872 | tf_op jit(solution)/shard_map/ppermute | solution.py:28
  7.2 13.6 %collective-permute-start.2 = (f32[8,128,128]{2,1,0:T(8,128)}, f32[8,128,128]{2,1,0:T(8,128)S(1)}, u32[]{:S(2)}, u32[]{:S(2)}) collective-permute-start(f32[8,128,128]{2,1,0:T(8,128)} %turn.1.x), channel_id=1, source_target_pairs={{0,32},{1,33},{2,34},{3,35},{4,36},{5,37},{6,38},{7,39},{8,40},{9,... | collective-permute-start | bytes 1572872 | tf_op jit(solution)/shard_map/ppermute | solution.py:28
  7.2 15.0 %collective-permute-start = (f32[128,1024]{1,0:T(8,128)}, f32[128,1024]{1,0:T(8,128)S(1)}, u32[]{:S(2)}, u32[]{:S(2)}) collective-permute-start(f32[128,1024]{1,0:T(8,128)} %w), channel_id=1, source_target_pairs={{0,1},{1,2},{2,3},{3,0},{4,5},{5,6},{6,7},{7,4},{8,9},{9,10},{10,1... | collective-permute-start | bytes 1572872 | tf_op jit(solution)/shard_map/ppermute | solution.py:28
  8.8 14.1 %collective-permute-start.1 = (f32[128,1024]{1,0:T(8,128)}, f32[128,1024]{1,0:T(8,128)}, u32[]{:S(2)}, u32[]{:S(2)}) collective-permute-start(f32[128,1024]{1,0:T(8,128)} %w), channel_id=1, source_target_pairs={{0,3},{1,0},{2,1},{3,2},{4,7},{5,4},{6,5},{7,6},{8,11},{9,8},{10,9... | collective-permute-start | bytes 1572872 | tf_op jit(solution)/shard_map/ppermute | solution.py:28
  15.9 17.3 %copy-start.5 = (f32[8,128,128]{2,1,0:T(8,128)}, f32[8,128,128]{2,1,0:T(8,128)S(1)}, u32[]{:S(2)}) copy-start(f32[8,128,128]{2,1,0:T(8,128)S(1)} %collective-permute-done.4.xx) | copy-start | bytes 1572868
  17.7 31.4 %copy-start.2 = (f32[8,128,128]{2,1,0:T(8,128)}, f32[8,128,128]{2,1,0:T(8,128)S(1)}, u32[]{:S(2)}) copy-start(f32[8,128,128]{2,1,0:T(8,128)S(1)} %collective-permute-done.3.xm) | copy-start | bytes 1572868
  20.8 28.4 %copy-start.3 = (f32[8,128,128]{2,1,0:T(8,128)}, f32[8,128,128]{2,1,0:T(8,128)S(1)}, u32[]{:S(2)}) copy-start(f32[8,128,128]{2,1,0:T(8,128)S(1)} %collective-permute-done.2.xp) | copy-start | bytes 1572868
  22.1 0.8 copy-start.10
  24.1 24.8 %copy-start.6 = (f32[512]{0:T(512)S(1)}, f32[512]{0:T(512)}, u32[]{:S(2)}) copy-start(f32[512]{0:T(512)} %param.7) | copy-start | bytes 6148
  24.1 24.8 %copy-start.7 = (f32[32]{0:T(128)S(1)}, f32[32]{0:T(128)}, u32[]{:S(2)}) copy-start(f32[32]{0:T(128)} %param.6) | copy-start | bytes 388
  24.1 22.8 %collective-permute-start.9 = (f32[8,512,128]{2,1,0:T(8,128)S(1)}, f32[8,512,128]{2,1,0:T(8,128)}, u32[]{:S(2)}, u32[]{:S(2)}) collective-permute-start(f32[8,512,128]{2,1,0:T(8,128)S(1)} %pad_maximum_fusion), channel_id=1, source_target_pairs={{0,8},{1,9},{2,10},{3,11},{4,12},{5,13},{6,14},{7,15},{8,0},{9,1},... | collective-permute-start | bytes 6291464 | tf_op jit(solution)/shard_map/ppermute | solution.py:28
  26.1 15.1 %collective-permute-start.8 = (f32[128,1024]{1,0:T(8,128)S(1)}, f32[128,1024]{1,0:T(8,128)}, u32[]{:S(2)}, u32[]{:S(2)}) collective-permute-start(f32[128,1024]{1,0:T(8,128)S(1)} %copy-done.9), channel_id=1, source_target_pairs={{0,4},{1,5},{2,6},{3,7},{4,0},{5,1},{6,2},{7,3},{8,12},{9,13},{10,... | collective-permute-start | bytes 1572872 | tf_op jit(solution)/shard_map/ppermute | solution.py:28
  28.6 14.8 %collective-permute-start.7 = (f32[128,1024]{1,0:T(8,128)S(1)}, f32[128,1024]{1,0:T(8,128)}, u32[]{:S(2)}, u32[]{:S(2)}) collective-permute-start(f32[128,1024]{1,0:T(8,128)S(1)} %copy-done.9), channel_id=1, source_target_pairs={{0,2},{1,3},{2,0},{3,1},{4,6},{5,7},{6,4},{7,5},{8,10},{9,11},{10,... | collective-permute-start | bytes 1572872 | tf_op jit(solution)/shard_map/ppermute | solution.py:28
  31.1 12.9 %collective-permute-start.6 = (f32[8,128,128]{2,1,0:T(8,128)S(1)}, f32[8,128,128]{2,1,0:T(8,128)S(1)}, u32[]{:S(2)}, u32[]{:S(2)}) collective-permute-start(f32[8,128,128]{2,1,0:T(8,128)S(1)} %collective-permute-done.4.xx), channel_id=1, source_target_pairs={{0,96},{1,97},{2,98},{3,99},{4,100},{5,101},{6,102},{7,103},{8,104... | collective-permute-start | bytes 1572872 | tf_op jit(solution)/shard_map/ppermute | solution.py:28
  33.2 13.7 %collective-permute-start.5 = (f32[8,128,128]{2,1,0:T(8,128)S(1)}, f32[8,128,128]{2,1,0:T(8,128)S(1)}, u32[]{:S(2)}, u32[]{:S(2)}) collective-permute-start(f32[8,128,128]{2,1,0:T(8,128)S(1)} %collective-permute-done.4.xx), channel_id=1, source_target_pairs={{0,32},{1,33},{2,34},{3,35},{4,36},{5,37},{6,38},{7,39},{8,40},{9,... | collective-permute-start | bytes 1572872 | tf_op jit(solution)/shard_map/ppermute | solution.py:28
  44.1 5.2 %copy-start = (f32[8,128,128]{2,1,0:T(8,128)}, f32[8,128,128]{2,1,0:T(8,128)S(1)}, u32[]{:S(2)}) copy-start(f32[8,128,128]{2,1,0:T(8,128)S(1)} %collective-permute-done.6.xxm) | copy-start | bytes 1572868
  46.9 2.3 %copy-start.1 = (f32[8,128,128]{2,1,0:T(8,128)}, f32[8,128,128]{2,1,0:T(8,128)S(1)}, u32[]{:S(2)}) copy-start(f32[8,128,128]{2,1,0:T(8,128)S(1)} %collective-permute-done.5.xxp) | copy-start | bytes 1572868
  47.0 5.5 %collective-permute-start.15 = (f32[8,256,128]{2,1,0:T(8,128)S(1)}, f32[8,256,128]{2,1,0:T(8,128)}, u32[]{:S(2)}, u32[]{:S(2)}) collective-permute-start(f32[8,256,128]{2,1,0:T(8,128)S(1)} %pad_maximum_fusion.1), channel_id=1, source_target_pairs={{0,8},{1,9},{2,10},{3,11},{4,12},{5,13},{6,14},{7,15},{8,0},{9,1},... | collective-permute-start | bytes 3145736 | tf_op jit(solution)/shard_map/ppermute | solution.py:28
  49.1 1.8 %slice-start = ((f32[8,128,128]{2,1,0:T(8,128)}), f32[8,64,128]{2,1,0:T(8,128)S(1)}, s32[]{:S(2)}) async-start(f32[8,128,128]{2,1,0:T(8,128)} %copy-done.3), calls=%async_computation | async-start | bytes 524288 | tf_op jit(solution)/shard_map/slice | solution.py:273
  49.3 22.1 %collective-permute-start.13 = (f32[128,1024]{1,0:T(8,128)}, f32[128,1024]{1,0:T(8,128)}, u32[]{:S(2)}, u32[]{:S(2)}) collective-permute-start(f32[128,1024]{1,0:T(8,128)} %collective-permute-done.8.wx), channel_id=1, source_target_pairs={{0,3},{1,0},{2,1},{3,2},{4,7},{5,4},{6,5},{7,6},{8,11},{9,8},{10,9... | collective-permute-start | bytes 1572872 | tf_op jit(solution)/shard_map/ppermute | solution.py:28
  50.0 21.4 %collective-permute-start.12 = (f32[128,1024]{1,0:T(8,128)}, f32[128,1024]{1,0:T(8,128)}, u32[]{:S(2)}, u32[]{:S(2)}) collective-permute-start(f32[128,1024]{1,0:T(8,128)} %collective-permute-done.8.wx), channel_id=1, source_target_pairs={{0,1},{1,2},{2,3},{3,0},{4,5},{5,6},{6,7},{7,4},{8,9},{9,10},{10,1... | collective-permute-start | bytes 1572872 | tf_op jit(solution)/shard_map/ppermute | solution.py:28
  50.8 20.5 %collective-permute-start.11 = (f32[8,128,128]{2,1,0:T(8,128)S(1)}, f32[8,128,128]{2,1,0:T(8,128)}, u32[]{:S(2)}, u32[]{:S(2)}) collective-permute-start(f32[8,128,128]{2,1,0:T(8,128)S(1)} %pad_maximum_fusion.4), channel_id=1, source_target_pairs={{0,96},{1,97},{2,98},{3,99},{4,100},{5,101},{6,102},{7,103},{8,104... | collective-permute-start | bytes 1572872 | tf_op jit(solution)/shard_map/ppermute | solution.py:28
  51.0 20.4 %collective-permute-start.10 = (f32[8,128,128]{2,1,0:T(8,128)S(1)}, f32[8,128,128]{2,1,0:T(8,128)S(1)}, u32[]{:S(2)}, u32[]{:S(2)}) collective-permute-start(f32[8,128,128]{2,1,0:T(8,128)S(1)} %pad_maximum_fusion.3), channel_id=1, source_target_pairs={{0,32},{1,33},{2,34},{3,35},{4,36},{5,37},{6,38},{7,39},{8,40},{9,... | collective-permute-start | bytes 1572872 | tf_op jit(solution)/shard_map/ppermute | solution.py:28
  52.5 18.9 %collective-permute-start.14 = (f32[128,1024]{1,0:T(8,128)}, f32[128,1024]{1,0:T(8,128)S(1)}, u32[]{:S(2)}, u32[]{:S(2)}) collective-permute-start(f32[128,1024]{1,0:T(8,128)} %collective-permute-done.7.w2), channel_id=1, source_target_pairs={{0,4},{1,5},{2,6},{3,7},{4,0},{5,1},{6,2},{7,3},{8,12},{9,13},{10,... | collective-permute-start | bytes 1572872 | tf_op jit(solution)/shard_map/ppermute | solution.py:28
  71.4 5.8 %copy-start.4 = (f32[8,128,128]{2,1,0:T(8,128)}, f32[8,128,128]{2,1,0:T(8,128)S(1)}, u32[]{:S(2)}) copy-start(f32[8,128,128]{2,1,0:T(8,128)S(1)} %collective-permute-done.10.up) | copy-start | bytes 1572868
  71.4 5.7 %copy-start.11 = (f32[128,1024]{1,0:T(8,128)}, f32[128,1024]{1,0:T(8,128)S(1)}, u32[]{:S(2)}) copy-start(f32[128,1024]{1,0:T(8,128)S(1)} %collective-permute-done.14.wx2) | copy-start | bytes 1572868
  72.9 4.2 %collective-permute-start.16 = (f32[8,256,128]{2,1,0:T(8,128)S(1)}, f32[8,256,128]{2,1,0:T(8,128)S(1)}, u32[]{:S(2)}, u32[]{:S(2)}) collective-permute-start(f32[8,256,128]{2,1,0:T(8,128)S(1)} %pad_maximum_fusion.2), channel_id=1, source_target_pairs={{0,8},{1,9},{2,10},{3,11},{4,12},{5,13},{6,14},{7,15},{8,0},{9,1},... | collective-permute-start | bytes 3145736 | tf_op jit(solution)/shard_map/ppermute | solution.py:28
  77.1 1.0 %copy-start.8 = (f32[8,256,128]{2,1,0:T(8,128)}, f32[8,256,128]{2,1,0:T(8,128)S(1)}, u32[]{:S(2)}) copy-start(f32[8,256,128]{2,1,0:T(8,128)S(1)} %collective-permute-done.16.s3) | copy-start | bytes 3145732

commit v3 on v2

--- a/solution.py
+++ b/solution.py
@@ -115,9 +115,9 @@
             for copy in copies[j]:
                 copy.wait()
 
-    dense(info_ref, held.at[chunk], 12, [high, ahigh_ref], [low, alow_ref])
-    for n in range(0, part_ref.shape[1], 256):
-        part_ref[:, n : n + 256] = three(high[...], low[...], whigh_ref[:, n : n + 256], wlow_ref[:, n : n + 256])
+    dense(info_ref, held.at[chunk], 12, [high, ahigh_ref.at[chunk]], [low, alow_ref.at[chunk]])
+    for n in range(0, part_ref.shape[2], 256):
+        part_ref[chunk, :, n : n + 256] = three(high[...], low[...], whigh_ref[:, n : n + 256], wlow_ref[:, n : n + 256])
 
 
 def early(info, sources, weights):
@@ -127,23 +127,17 @@
     return pl.pallas_call(
         early_kernel,
         out_shape=[
-            jax.ShapeDtypeStruct((3 * rows, columns), f32),
-            jax.ShapeDtypeStruct((3 * rows, depth), bf16),
-            jax.ShapeDtypeStruct((3 * rows, depth), bf16),
-            jax.ShapeDtypeStruct((depth, columns), bf16),
-            jax.ShapeDtypeStruct((depth, columns), bf16),
+            pltpu.VMEM((3, rows, columns), f32),
+            pltpu.VMEM((3, rows, depth), bf16),
+            pltpu.VMEM((3, rows, depth), bf16),
+            pltpu.VMEM((depth, columns), bf16),
+            pltpu.VMEM((depth, columns), bf16),
         ],
         grid_spec=pltpu.PrefetchScalarGridSpec(
             num_scalar_prefetch=1,
             grid=(3,),
             in_specs=[pl.BlockSpec(memory_space=pltpu.HBM)] * 12,
-            out_specs=[
-                pl.BlockSpec((rows, columns), lambda c, i: (c, 0)),
-                pl.BlockSpec((rows, depth), lambda c, i: (c, 0)),
-                pl.BlockSpec((rows, depth), lambda c, i: (c, 0)),
-                pl.BlockSpec((depth, columns), lambda c, i: (0, 0)),
-                pl.BlockSpec((depth, columns), lambda c, i: (0, 0)),
-            ],
+            out_specs=[pl.BlockSpec(memory_space=pltpu.VMEM)] * 5,
             scratch_shapes=[
                 pltpu.VMEM((3, 8, rows, 128), f32),
                 pltpu.VMEM((4, 128, columns), f32),
@@ -153,7 +147,7 @@
                 pltpu.SemaphoreType.DMA((4,)),
             ],
         ),
-        compiler_params=pltpu.CompilerParams(vmem_limit_bytes=60 * MIB),
+        compiler_params=pltpu.CompilerParams(vmem_limit_bytes=46 * MIB),
         cost_estimate=pl.CostEstimate(flops=18 * rows * depth * columns, bytes_accessed=20 * MIB, transcendentals=0),
         name="early",
     )(info, *sources, *weights)
@@ -194,7 +188,7 @@
     def _():
         for n in range(0, columns, 256):
             cut = slice(n, n + 256)
-            total = part_ref[:, cut] + three(ahigh_ref[...], alow_ref[...], whigh2[:, cut], wlow2[:, cut])
+            total = part_ref[chunk, :, cut] + three(ahigh_ref[chunk], alow_ref[chunk], whigh2[:, cut], wlow2[:, cut])
             finish(n, total)
 
     @pl.when(chunk == last)
@@ -213,7 +207,6 @@
     columns = weights[0].shape[1]
     rows = 8 * HALF
     depth = 4 * 128
-    block = lambda width: pl.BlockSpec((rows, width), lambda c, i: (jnp.minimum(c, 2), 0))
     fixed = lambda *shape: pl.BlockSpec(shape, lambda c, i: (0, 0))
     return pl.pallas_call(
         late_kernel,
@@ -221,9 +214,9 @@
         grid_spec=pltpu.PrefetchScalarGridSpec(
             num_scalar_prefetch=1,
             grid=(4,),
-            in_specs=[block(columns), block(depth), block(depth), fixed(depth, columns), fixed(depth, columns)]
+            in_specs=[pl.BlockSpec(memory_space=pltpu.VMEM)] * 5
             + [pl.BlockSpec((virtuals, 1, 8, 128), lambda c, i: (0, i[4 + c], 0, 0)), fixed(1, columns)]
-            + [pl.BlockSpec(memory_space=pltpu.HBM)] * 7,
+            + [pl.BlockSpec(memory_space=pl.ANY)] * 7,
             out_specs=pl.BlockSpec((virtuals, 1, 8, columns), lambda c, i: (0, i[4 + c], 0, 0)),
             scratch_shapes=[
                 pltpu.VMEM((8, rows, 128), f32),
@@ -234,10 +227,10 @@
             + [pltpu.VMEM((rows, depth), bf16)] * 4
             + [pltpu.SemaphoreType.DMA((8,)), pltpu.SemaphoreType.DMA((4,))],
         ),
-        compiler_params=pltpu.CompilerParams(vmem_limit_bytes=60 * MIB),
+        compiler_params=pltpu.CompilerParams(vmem_limit_bytes=30 * MIB),
         cost_estimate=pl.CostEstimate(flops=30 * rows * depth * columns, bytes_accessed=24 * MIB, transcendentals=0),
         name="late",
-    )(info, *made, rgap, cgap, *sources, *weights)
+    )(info, *(pltpu.with_memory_space_constraint(v, pltpu.VMEM) for v in made), rgap, cgap, *sources, *weights)
 
 
 def body(amplitudes, integrals, occ_energy, vir_energy):
@@ -257,7 +250,6 @@
     rgap = jnp.broadcast_to(row_gap.reshape(virtuals, 4, 8, 1), (virtuals, 4, 8, 128))
     start = ((y * 2 + xl) * 2 + core) * columns
     cgap = lax.dynamic_slice_in_dim(gap.reshape(-1), start, columns).reshape(1, columns)
-    info, rgap, cgap = lax.optimization_barrier((info, rgap, cgap))
 
     join = lambda *values: jnp.concatenate(values, axis=1)
     x = turn(amplitudes.transpose(1, 2, 3, 0).reshape(own, depth, virtuals))
@@ -265,17 +257,20 @@
 
     wp, wm = hop(w, z=1), hop(w, z=3)
     xp, xm, xx = hop(x, y=1), hop(x, y=3), hop(x, xl=1)
-    wp, wm, xp, xm, xx, w, x = lax.optimization_barrier((wp, wm, xp, xm, xx, w, x))
-    xxp, xxm, w2, wx = hop(xx, y=1), hop(xx, y=3), hop(w, z=2), hop(w, xh=1)
+    xx, wp, wm, info, rgap, cgap = lax.optimization_barrier((xx, wp, wm, info, rgap, cgap))
+    xxp, xxm = hop(xx, y=1), hop(xx, y=3)
+    w2, wx = hop(after(w, wp, wm), z=2), hop(after(w, xx), xh=1)
     s1 = hop(join(x, xx, xp, xm), core=1)
     xxp, xxm, w2, wx, s1 = lax.optimization_barrier((xxp, xxm, w2, wx, s1))
     s2 = hop(join(xxp, xxm), core=1)
     up = hop(join(xp[:, :HALF], xxp[:, :HALF]), y=1)
     down = hop(join(xm[:, HALF:], xxm[:, HALF:]), y=3)
     wxp, wxm, wx2 = hop(wx, z=1), hop(wx, z=3), hop(w2, xh=1)
-    made = early(info, [x, xx, s1, xp, xxp, xm, xxm, s2], [w, wp, wm, w2])
-    up, down, wxp, wxm, wx2, *made = lax.optimization_barrier((up, down, wxp, wxm, wx2, *made))
+
+    *made, wlow = early(info, [x, xx, s1, xp, xxp, xm, xxm, s2], [w, wp, wm, w2])
+    up, down, wxp, wxm, wx2, wlow = lax.optimization_barrier((up, down, wxp, wxm, wx2, wlow))
     s3 = hop(join(up, down), core=1)
+    made += [wlow]
     out = late(info, made, rgap, cgap, [up, down, s3], [wx, wxp, wxm, wx2], virtuals)
     return out.reshape(virtuals * 32, columns)
 

time: 96.7 us -> 83.2 us (0.86)
  Pallas kernels: 35.9 us -> 28.5 us
  other arithmetic: 2.86 us -> 1.12 us
  local copies, waits for them, and re-layouts: 4.94 us -> 3.26 us
  waiting for transfers between devices: 27.2 us -> 25.7 us
  starting transfers between devices: 25.1 us -> 24 us
    pallas_call x1, Pallas kernels: 18.2 us -> 12.7 us  [late(): pl.pallas_call(late_kernel, out_shape=jax.ShapeDtypeStruct((virtuals, 4,...]
    concatenate x5, other arithmetic: 2.78 us -> 0.35 us  [body(): join = lambda *values: jnp.concatenate(values, axis=1)]
    pallas_call x1, Pallas kernels: 15.3 us -> 13.4 us  [early(): pl.pallas_call(early_kernel, out_shape=[pltpu.VMEM((3, rows, columns), f3...]
    ppermute x17, waiting for transfers between devices: 27.2 us -> 25.7 us  [hop(): return lax.ppermute(value, AXES, pairs)]
    ppermute x17, starting transfers between devices: 25.1 us -> 24 us  [hop(): return lax.ppermute(value, AXES, pairs)]
    broadcast_in_dim x3, local copies, waits for them, and re-layouts: 1.53 us -> 0.52 us  [body(): jnp.broadcast_to(row_gap.reshape(virtuals, 4, 8, 1), (virtuals, 4, 8, 128))]
  transfers between devices with their start and end apart: 17 -> 17, of which waited for: 9 -> 8; matrix products, arithmetic and copies ran while one was open for 3% -> 3% of each run, Pallas kernels for 16% -> 16%
where the time goes in v3:
time: 83.2 us; the launch traced here: 83 us
  Pallas kernels  28.5 us (34%)
  waiting for transfers between devices  25.7 us (31%)
  starting transfers between devices  24 us (29%)
  local copies, waits for them, and re-layouts  3.26 us (4%)
  other arithmetic  1.12 us (1%)
    ppermute x17, waiting for transfers between devices, hop(): return lax.ppermute(value, AXES, pairs)  25.7 us
    ppermute x17, starting transfers between devices, hop(): return lax.ppermute(value, AXES, pairs)  24 us
    pallas_call x1, Pallas kernels, early(): pl.pallas_call(early_kernel, out_shape=[pltpu.VMEM((3, rows, columns), f3...  13.4 us
    pallas_call x1, Pallas kernels, late(): pl.pallas_call(late_kernel, out_shape=jax.ShapeDtypeStruct((virtuals, 4,...  12.7 us
    pallas_call x1, Pallas kernels, turn(): pl.pallas_call(turn_kernel, out_shape=jax.ShapeDtypeStruct((depth // 128,...  2.4 us
  transfers between devices with their start and end apart: 17, of which 8 were waited for; matrix products, arithmetic and copies ran while one was open for 3% of the time, Pallas kernels for 16%

profile of v3, /device:TPU:1, one launch (start us, length us, event | category | flops | bytes accessed | tf_op | source)
XLA Modules:
  0.0 83.0 jit_solution(8739083808618587866)
XLA Ops:
  0.0 2.4 %turn.1.x = f32[8,128,128]{2,1,0:T(8,128)} custom-call(f32[2,1024,64]{2,1,0:T(8,128)} %bitcast.22), custom_call_target="tpu_custom_call" | custom-call | tf_op jit(solution)/shard_map/turn/pallas_call | solution.py:49
  2.4 2.0 %collective-permute-start = (f32[8,128,128]{2,1,0:T(8,128)}, f32[8,128,128]{2,1,0:T(8,128)S(1)}, u32[]{:S(2)}, u32[]{:S(2)}) collective-permute-start(f32[8,128,128]{2,1,0:T(8,128)} %turn.1.x), channel_id=1, source_target_pairs={{0,16},{1,17},{2,18},{3,19},{4,20},{5,21},{6,22},{7,23},{8,24},{9,... | collective-permute-start | bytes 1572872 | tf_op jit(solution)/shard_map/ppermute | solution.py:28
  4.4 3.8 %collective-permute-start.2 = (f32[128,1024]{1,0:T(8,128)}, f32[128,1024]{1,0:T(8,128)S(1)}, u32[]{:S(2)}, u32[]{:S(2)}) collective-permute-start(f32[128,1024]{1,0:T(8,128)} %w.1), channel_id=1, source_target_pairs={{0,3},{1,0},{2,1},{3,2},{4,7},{5,4},{6,5},{7,6},{8,11},{9,8},{10,9... | collective-permute-start | bytes 1572872 | tf_op jit(solution)/shard_map/ppermute | solution.py:28
  8.2 0.0 collective-permute-start.1
  8.2 2.7 %collective-permute-start.8 = (f32[8,128,128]{2,1,0:T(8,128)}, f32[8,128,128]{2,1,0:T(8,128)S(1)}, u32[]{:S(2)}, u32[]{:S(2)}) collective-permute-start(f32[8,128,128]{2,1,0:T(8,128)} %turn.1.x), channel_id=1, source_target_pairs={{0,96},{1,97},{2,98},{3,99},{4,100},{5,101},{6,102},{7,103},{8,104... | collective-permute-start | bytes 1572872 | tf_op jit(solution)/shard_map/ppermute | solution.py:28
  10.9 0.0 collective-permute-start.7
  10.9 0.8 broadcast_subtract_fusion
  11.7 0.1 copy.6
  11.8 0.1 dynamic-slice_bitcast_fusion
  11.9 0.1 copy.5
  12.0 0.1 sub.37
  12.2 0.7 stack.59.info_ref
  12.9 3.1 %collective-permute-done.xx = f32[8,128,128]{2,1,0:T(8,128)S(1)} collective-permute-done((f32[8,128,128]{2,1,0:T(8,128)}, f32[8,128,128]{2,1,0:T(8,128)S(1)}, u32[]{:S(2)}, u32[]{:S(2)}) %collective-permute-start) | collective-permute-done | bytes 524320 | tf_op jit(solution)/shard_map/ppermute | solution.py:28
  16.0 0.0 copy-start.6
  16.0 2.7 %collective-permute-done.2.wm = f32[128,1024]{1,0:T(8,128)S(1)} collective-permute-done((f32[128,1024]{1,0:T(8,128)}, f32[128,1024]{1,0:T(8,128)S(1)}, u32[]{:S(2)}, u32[]{:S(2)}) %collective-permute-start.2) | collective-permute-done | bytes 524320 | tf_op jit(solution)/shard_map/ppermute | solution.py:28
  18.8 3.1 %collective-permute-done.1.wp = f32[128,1024]{1,0:T(8,128)} collective-permute-done((f32[128,1024]{1,0:T(8,128)}, f32[128,1024]{1,0:T(8,128)}, u32[]{:S(2)}, u32[]{:S(2)}) %collective-permute-start.1) | collective-permute-done | bytes 524320 | tf_op jit(solution)/shard_map/ppermute | solution.py:28
  21.9 0.0 copy-done.10
  21.9 0.3 broadcast_in_dim.10.rgap_ref
  22.2 0.0 copy-start.9
  22.3 0.0 collective-permute-done.8.xm
  22.3 0.0 copy-start.4
  22.3 2.0 %collective-permute-done.7.xp = f32[8,128,128]{2,1,0:T(8,128)S(1)} collective-permute-done((f32[8,128,128]{2,1,0:T(8,128)}, f32[8,128,128]{2,1,0:T(8,128)S(1)}, u32[]{:S(2)}, u32[]{:S(2)}) %collective-permute-start.7) | collective-permute-done | bytes 524320 | tf_op jit(solution)/shard_map/ppermute | solution.py:28
  24.3 0.0 copy-done.1
  24.3 0.1 pad_maximum_fusion
  24.4 2.5 %collective-permute-start.9 = (f32[8,512,128]{2,1,0:T(8,128)S(1)}, f32[8,512,128]{2,1,0:T(8,128)S(1)}, u32[]{:S(2)}, u32[]{:S(2)}) collective-permute-start(f32[8,512,128]{2,1,0:T(8,128)S(1)} %pad_maximum_fusion), channel_id=1, source_target_pairs={{0,8},{1,9},{2,10},{3,11},{4,12},{5,13},{6,14},{7,15},{8,0},{9,1},... | collective-permute-start | bytes 6291464 | tf_op jit(solution)/shard_map/ppermute | solution.py:28
  26.9 0.0 copy-done.9
  26.9 2.5 %collective-permute-start.6 = (f32[128,1024]{1,0:T(8,128)S(1)}, f32[128,1024]{1,0:T(8,128)S(1)}, u32[]{:S(2)}, u32[]{:S(2)}) collective-permute-start(f32[128,1024]{1,0:T(8,128)S(1)} %copy-done.9), channel_id=1, source_target_pairs={{0,4},{1,5},{2,6},{3,7},{4,0},{5,1},{6,2},{7,3},{8,12},{9,13},{10,... | collective-permute-start | bytes 1572872 | tf_op jit(solution)/shard_map/ppermute | solution.py:28
  29.4 1.3 %collective-permute-start.5 = (f32[128,1024]{1,0:T(8,128)S(1)}, f32[128,1024]{1,0:T(8,128)}, u32[]{:S(2)}, u32[]{:S(2)}) collective-permute-start(f32[128,1024]{1,0:T(8,128)S(1)} %copy-done.9), channel_id=1, source_target_pairs={{0,2},{1,3},{2,0},{3,1},{4,6},{5,7},{6,4},{7,5},{8,10},{9,11},{10,... | collective-permute-start | bytes 1572872 | tf_op jit(solution)/shard_map/ppermute | solution.py:28
  30.7 0.0 collective-permute-start.4
  30.7 0.0 copy-done.6
  30.7 1.4 %collective-permute-start.3 = (f32[8,128,128]{2,1,0:T(8,128)S(1)}, f32[8,128,128]{2,1,0:T(8,128)S(1)}, u32[]{:S(2)}, u32[]{:S(2)}) collective-permute-start(f32[8,128,128]{2,1,0:T(8,128)S(1)} %collective-permute-done.xx), channel_id=1, source_target_pairs={{0,32},{1,33},{2,34},{3,35},{4,36},{5,37},{6,38},{7,39},{8,40},{9,... | collective-permute-start | bytes 1572872 | tf_op jit(solution)/shard_map/ppermute | solution.py:28
  32.2 9.9 %collective-permute-done.6.wx = f32[128,1024]{1,0:T(8,128)S(1)} collective-permute-done((f32[128,1024]{1,0:T(8,128)S(1)}, f32[128,1024]{1,0:T(8,128)S(1)}, u32[]{:S(2)}, u32[]{:S(2)}) %collective-permute-start.6) | collective-permute-done | bytes 524320 | tf_op jit(solution)/shard_map/ppermute | solution.py:28
  42.0 2.1 %collective-permute-done.5.w2 = f32[128,1024]{1,0:T(8,128)} collective-permute-done((f32[128,1024]{1,0:T(8,128)S(1)}, f32[128,1024]{1,0:T(8,128)}, u32[]{:S(2)}, u32[]{:S(2)}) %collective-permute-start.5) | collective-permute-done | bytes 524320 | tf_op jit(solution)/shard_map/ppermute | solution.py:28
  44.2 0.0 collective-permute-done.4.xxm
  44.2 0.4 collective-permute-done.3.xxp
  44.6 0.0 collective-permute-done.9.s1
  44.6 0.1 pad_maximum_fusion.1
  44.6 1.8 %collective-permute-start.10 = (f32[8,256,128]{2,1,0:T(8,128)S(1)}, f32[8,256,128]{2,1,0:T(8,128)S(1)}, u32[]{:S(2)}, u32[]{:S(2)}) collective-permute-start(f32[8,256,128]{2,1,0:T(8,128)S(1)} %pad_maximum_fusion.1), channel_id=1, source_target_pairs={{0,8},{1,9},{2,10},{3,11},{4,12},{5,13},{6,14},{7,15},{8,0},{9,1},... | collective-permute-start | bytes 3145736 | tf_op jit(solution)/shard_map/ppermute | solution.py:28
  46.4 0.0 copy-done.4
  46.5 0.0 copy-done.5
  46.5 0.0 slice-start
  46.5 0.0 copy-done.2
  46.6 0.0 copy-done.3
  46.6 0.0 copy-done.7
  46.6 0.1 collective-permute-start.12
  46.7 0.7 slice-done
  47.5 0.8 collective-permute-start.11
  48.3 0.5 collective-permute-start.15
  48.8 1.9 %collective-permute-start.14 = (f32[128,1024]{1,0:T(8,128)S(1)}, f32[128,1024]{1,0:T(8,128)S(1)}, u32[]{:S(2)}, u32[]{:S(2)}) collective-permute-start(f32[128,1024]{1,0:T(8,128)S(1)} %collective-permute-done.6.wx), channel_id=1, source_target_pairs={{0,3},{1,0},{2,1},{3,2},{4,7},{5,4},{6,5},{7,6},{8,11},{9,8},{10,9... | collective-permute-start | bytes 1572872 | tf_op jit(solution)/shard_map/ppermute | solution.py:28
  50.7 0.0 collective-permute-done.10.s2
  50.7 1.0 %copy-done.8 = f32[8,256,128]{2,1,0:T(8,128)} copy-done((f32[8,256,128]{2,1,0:T(8,128)}, f32[8,256,128]{2,1,0:T(8,128)S(1)}, u32[]{:S(2)}) %copy-start.8) | copy-done | bytes 1048600
  51.7 0.0 collective-permute-start.13
  51.7 13.4 %early.1 = (f32[3,512,1024]{2,1,0:T(8,128)S(1)}, bf16[3,512,512]{2,1,0:T(8,128)(2,1)S(1)}, bf16[3,512,512]{2,1,0:T(8,128)(2,1)S(1)}, bf16[512,1024]{1,0:T(8,128)(2,1)S(1)}, bf16[512,1024]{1,0:T(8,128)(2,1)S(1)}) custom-call(s32[14]{0:T(128)} %stack.59.info_ref, f32[8,128,128]{2,1,0:T(8,128)} %turn.1.x, f32[8,128,128]{2,1,0:T(8,128)} %copy-done.6, ...), custom_call_target="tpu_custom_call" | custom-call | flops 4831838208 | bytes 20971520 | tf_op jit(solution)/shard_map/early/pallas_call | solution.py:127
  65.1 0.0 copy-start
  65.1 0.0 collective-permute-done.12.down
  65.1 0.0 collective-permute-done.11.up
  65.1 0.0 collective-permute-done.15.wx2
  65.1 0.0 collective-permute-done.14.wxm
  65.2 0.0 collective-permute-done.13.wxp
  65.2 0.1 pad_maximum_fusion.2
  65.2 2.6 %collective-permute-start.16 = (f32[8,256,128]{2,1,0:T(8,128)S(1)}, f32[8,256,128]{2,1,0:T(8,128)S(1)}, u32[]{:S(2)}, u32[]{:S(2)}) collective-permute-start(f32[8,256,128]{2,1,0:T(8,128)S(1)} %pad_maximum_fusion.2), channel_id=1, source_target_pairs={{0,8},{1,9},{2,10},{3,11},{4,12},{5,13},{6,14},{7,15},{8,0},{9,1},... | collective-permute-start | bytes 3145736 | tf_op jit(solution)/shard_map/ppermute | solution.py:28
  67.8 2.3 %collective-permute-done.16.s3 = f32[8,256,128]{2,1,0:T(8,128)S(1)} collective-permute-done((f32[8,256,128]{2,1,0:T(8,128)S(1)}, f32[8,256,128]{2,1,0:T(8,128)S(1)}, u32[]{:S(2)}, u32[]{:S(2)}) %collective-permute-start.16) | collective-permute-done | bytes 1048608 | tf_op jit(solution)/shard_map/ppermute | solution.py:28
  70.1 0.0 copy-done
  70.1 12.7 %late.1 = f32[64,4,8,1024]{3,2,1,0:T(8,128)} custom-call(s32[14]{0:T(128)S(1)} %copy-done, f32[3,512,1024]{2,1,0:T(8,128)S(1)} %get-tuple-element.39.part_ref, bf16[3,512,512]{2,1,0:T(8,128)(2,1)S(1)} %get-tuple-element.40.ahigh_ref, bf16[3,512,512]{2,1,0:T(8,128)(2,1)S(1)} %get-tuple-element.41.alow_ref, bf16[512,1024]{1,0:T(8,128)(2,1)S(1)} %get-tuple-element.42.whigh_ref, ...), custom_call_target="tpu_custom_call" | custom-call | flops 8053063680 | bytes 25165824 | tf_op jit(solution)/shard_map/late/pallas_call | solution.py:211
  (13 shorter events, 0.1 us)
Async XLA Ops:
  2.4 21.9 %copy-start.1 = (f32[8,128,128]{2,1,0:T(8,128)S(1)}, f32[8,128,128]{2,1,0:T(8,128)}, u32[]{:S(2)}) copy-start(f32[8,128,128]{2,1,0:T(8,128)} %turn.1.x) | copy-start | bytes 1572868
  2.4 13.6 %collective-permute-start = (f32[8,128,128]{2,1,0:T(8,128)}, f32[8,128,128]{2,1,0:T(8,128)S(1)}, u32[]{:S(2)}, u32[]{:S(2)}) collective-permute-start(f32[8,128,128]{2,1,0:T(8,128)} %turn.1.x), channel_id=1, source_target_pairs={{0,16},{1,17},{2,18},{3,19},{4,20},{5,21},{6,22},{7,23},{8,24},{9,... | collective-permute-start | bytes 1572872 | tf_op jit(solution)/shard_map/ppermute | solution.py:28
  4.4 14.3 %collective-permute-start.2 = (f32[128,1024]{1,0:T(8,128)}, f32[128,1024]{1,0:T(8,128)S(1)}, u32[]{:S(2)}, u32[]{:S(2)}) collective-permute-start(f32[128,1024]{1,0:T(8,128)} %w.1), channel_id=1, source_target_pairs={{0,3},{1,0},{2,1},{3,2},{4,7},{5,4},{6,5},{7,6},{8,11},{9,8},{10,9... | collective-permute-start | bytes 1572872 | tf_op jit(solution)/shard_map/ppermute | solution.py:28
  8.2 13.7 %collective-permute-start.1 = (f32[128,1024]{1,0:T(8,128)}, f32[128,1024]{1,0:T(8,128)}, u32[]{:S(2)}, u32[]{:S(2)}) collective-permute-start(f32[128,1024]{1,0:T(8,128)} %w.1), channel_id=1, source_target_pairs={{0,1},{1,2},{2,3},{3,0},{4,5},{5,6},{6,7},{7,4},{8,9},{9,10},{10,1... | collective-permute-start | bytes 1572872 | tf_op jit(solution)/shard_map/ppermute | solution.py:28
  8.2 14.0 %collective-permute-start.8 = (f32[8,128,128]{2,1,0:T(8,128)}, f32[8,128,128]{2,1,0:T(8,128)S(1)}, u32[]{:S(2)}, u32[]{:S(2)}) collective-permute-start(f32[8,128,128]{2,1,0:T(8,128)} %turn.1.x), channel_id=1, source_target_pairs={{0,96},{1,97},{2,98},{3,99},{4,100},{5,101},{6,102},{7,103},{8,104... | collective-permute-start | bytes 1572872 | tf_op jit(solution)/shard_map/ppermute | solution.py:28
  10.9 13.3 %collective-permute-start.7 = (f32[8,128,128]{2,1,0:T(8,128)}, f32[8,128,128]{2,1,0:T(8,128)S(1)}, u32[]{:S(2)}, u32[]{:S(2)}) collective-permute-start(f32[8,128,128]{2,1,0:T(8,128)} %turn.1.x), channel_id=1, source_target_pairs={{0,32},{1,33},{2,34},{3,35},{4,36},{5,37},{6,38},{7,39},{8,40},{9,... | collective-permute-start | bytes 1572872 | tf_op jit(solution)/shard_map/ppermute | solution.py:28
  16.0 14.7 %copy-start.6 = (f32[8,128,128]{2,1,0:T(8,128)}, f32[8,128,128]{2,1,0:T(8,128)S(1)}, u32[]{:S(2)}) copy-start(f32[8,128,128]{2,1,0:T(8,128)S(1)} %collective-permute-done.xx) | copy-start | bytes 1572868
  18.8 3.1 %copy-start.10 = (f32[128,1024]{1,0:T(8,128)}, f32[128,1024]{1,0:T(8,128)S(1)}, u32[]{:S(2)}) copy-start(f32[128,1024]{1,0:T(8,128)S(1)} %collective-permute-done.2.wm) | copy-start | bytes 1572868
  22.2 4.7 %copy-start.9 = (f32[128,1024]{1,0:T(8,128)S(1)}, f32[128,1024]{1,0:T(8,128)}, u32[]{:S(2)}) copy-start(f32[128,1024]{1,0:T(8,128)} %w.1) | copy-start | bytes 1572868
  22.3 24.2 %copy-start.4 = (f32[8,128,128]{2,1,0:T(8,128)}, f32[8,128,128]{2,1,0:T(8,128)S(1)}, u32[]{:S(2)}) copy-start(f32[8,128,128]{2,1,0:T(8,128)S(1)} %collective-permute-done.8.xm) | copy-start | bytes 1572868
  24.3 22.2 %copy-start.5 = (f32[8,128,128]{2,1,0:T(8,128)}, f32[8,128,128]{2,1,0:T(8,128)S(1)}, u32[]{:S(2)}) copy-start(f32[8,128,128]{2,1,0:T(8,128)S(1)} %collective-permute-done.7.xp) | copy-start | bytes 1572868
  24.4 20.1 %collective-permute-start.9 = (f32[8,512,128]{2,1,0:T(8,128)S(1)}, f32[8,512,128]{2,1,0:T(8,128)S(1)}, u32[]{:S(2)}, u32[]{:S(2)}) collective-permute-start(f32[8,512,128]{2,1,0:T(8,128)S(1)} %pad_maximum_fusion), channel_id=1, source_target_pairs={{0,8},{1,9},{2,10},{3,11},{4,12},{5,13},{6,14},{7,15},{8,0},{9,1},... | collective-permute-start | bytes 6291464 | tf_op jit(solution)/shard_map/ppermute | solution.py:28
  26.9 15.1 %collective-permute-start.6 = (f32[128,1024]{1,0:T(8,128)S(1)}, f32[128,1024]{1,0:T(8,128)S(1)}, u32[]{:S(2)}, u32[]{:S(2)}) collective-permute-start(f32[128,1024]{1,0:T(8,128)S(1)} %copy-done.9), channel_id=1, source_target_pairs={{0,4},{1,5},{2,6},{3,7},{4,0},{5,1},{6,2},{7,3},{8,12},{9,13},{10,... | collective-permute-start | bytes 1572872 | tf_op jit(solution)/shard_map/ppermute | solution.py:28
  29.4 14.8 %collective-permute-start.5 = (f32[128,1024]{1,0:T(8,128)S(1)}, f32[128,1024]{1,0:T(8,128)}, u32[]{:S(2)}, u32[]{:S(2)}) collective-permute-start(f32[128,1024]{1,0:T(8,128)S(1)} %copy-done.9), channel_id=1, source_target_pairs={{0,2},{1,3},{2,0},{3,1},{4,6},{5,7},{6,4},{7,5},{8,10},{9,11},{10,... | collective-permute-start | bytes 1572872 | tf_op jit(solution)/shard_map/ppermute | solution.py:28
  30.7 13.5 %collective-permute-start.4 = (f32[8,128,128]{2,1,0:T(8,128)S(1)}, f32[8,128,128]{2,1,0:T(8,128)S(1)}, u32[]{:S(2)}, u32[]{:S(2)}) collective-permute-start(f32[8,128,128]{2,1,0:T(8,128)S(1)} %collective-permute-done.xx), channel_id=1, source_target_pairs={{0,96},{1,97},{2,98},{3,99},{4,100},{5,101},{6,102},{7,103},{8,104... | collective-permute-start | bytes 1572872 | tf_op jit(solution)/shard_map/ppermute | solution.py:28
  30.7 13.8 %collective-permute-start.3 = (f32[8,128,128]{2,1,0:T(8,128)S(1)}, f32[8,128,128]{2,1,0:T(8,128)S(1)}, u32[]{:S(2)}, u32[]{:S(2)}) collective-permute-start(f32[8,128,128]{2,1,0:T(8,128)S(1)} %collective-permute-done.xx), channel_id=1, source_target_pairs={{0,32},{1,33},{2,34},{3,35},{4,36},{5,37},{6,38},{7,39},{8,40},{9,... | collective-permute-start | bytes 1572872 | tf_op jit(solution)/shard_map/ppermute | solution.py:28
  44.2 2.4 %copy-start.2 = (f32[8,128,128]{2,1,0:T(8,128)}, f32[8,128,128]{2,1,0:T(8,128)S(1)}, u32[]{:S(2)}) copy-start(f32[8,128,128]{2,1,0:T(8,128)S(1)} %collective-permute-done.4.xxm) | copy-start | bytes 1572868
  44.6 2.0 %copy-start.3 = (f32[8,128,128]{2,1,0:T(8,128)}, f32[8,128,128]{2,1,0:T(8,128)S(1)}, u32[]{:S(2)}) copy-start(f32[8,128,128]{2,1,0:T(8,128)S(1)} %collective-permute-done.3.xxp) | copy-start | bytes 1572868
  44.6 2.0 %copy-start.7 = (f32[8,512,128]{2,1,0:T(8,128)}, f32[8,512,128]{2,1,0:T(8,128)S(1)}, u32[]{:S(2)}) copy-start(f32[8,512,128]{2,1,0:T(8,128)S(1)} %collective-permute-done.9.s1) | copy-start | bytes 6291460
  44.6 6.1 %collective-permute-start.10 = (f32[8,256,128]{2,1,0:T(8,128)S(1)}, f32[8,256,128]{2,1,0:T(8,128)S(1)}, u32[]{:S(2)}, u32[]{:S(2)}) collective-permute-start(f32[8,256,128]{2,1,0:T(8,128)S(1)} %pad_maximum_fusion.1), channel_id=1, source_target_pairs={{0,8},{1,9},{2,10},{3,11},{4,12},{5,13},{6,14},{7,15},{8,0},{9,1},... | collective-permute-start | bytes 3145736 | tf_op jit(solution)/shard_map/ppermute | solution.py:28
  46.5 1.0 %slice-start = ((f32[8,128,128]{2,1,0:T(8,128)}), f32[8,64,128]{2,1,0:T(8,128)S(1)}, s32[]{:S(2)}) async-start(f32[8,128,128]{2,1,0:T(8,128)} %copy-done.5), calls=%async_computation | async-start | bytes 524288 | tf_op jit(solution)/shard_map/slice | solution.py:266
  46.6 18.5 %collective-permute-start.12 = (f32[8,128,128]{2,1,0:T(8,128)S(1)}, f32[8,128,128]{2,1,0:T(8,128)S(1)}, u32[]{:S(2)}, u32[]{:S(2)}) collective-permute-start(f32[8,128,128]{2,1,0:T(8,128)S(1)} %pad_maximum_fusion.4), channel_id=1, source_target_pairs={{0,96},{1,97},{2,98},{3,99},{4,100},{5,101},{6,102},{7,103},{8,104... | collective-permute-start | bytes 1572872 | tf_op jit(solution)/shard_map/ppermute | solution.py:28
  47.5 17.7 %collective-permute-start.11 = (f32[8,128,128]{2,1,0:T(8,128)S(1)}, f32[8,128,128]{2,1,0:T(8,128)S(1)}, u32[]{:S(2)}, u32[]{:S(2)}) collective-permute-start(f32[8,128,128]{2,1,0:T(8,128)S(1)} %pad_maximum_fusion.3), channel_id=1, source_target_pairs={{0,32},{1,33},{2,34},{3,35},{4,36},{5,37},{6,38},{7,39},{8,40},{9,... | collective-permute-start | bytes 1572872 | tf_op jit(solution)/shard_map/ppermute | solution.py:28
  48.3 16.9 %collective-permute-start.15 = (f32[128,1024]{1,0:T(8,128)}, f32[128,1024]{1,0:T(8,128)S(1)}, u32[]{:S(2)}, u32[]{:S(2)}) collective-permute-start(f32[128,1024]{1,0:T(8,128)} %collective-permute-done.5.w2), channel_id=1, source_target_pairs={{0,4},{1,5},{2,6},{3,7},{4,0},{5,1},{6,2},{7,3},{8,12},{9,13},{10,... | collective-permute-start | bytes 1572872 | tf_op jit(solution)/shard_map/ppermute | solution.py:28
  48.8 16.4 %collective-permute-start.14 = (f32[128,1024]{1,0:T(8,128)S(1)}, f32[128,1024]{1,0:T(8,128)S(1)}, u32[]{:S(2)}, u32[]{:S(2)}) collective-permute-start(f32[128,1024]{1,0:T(8,128)S(1)} %collective-permute-done.6.wx), channel_id=1, source_target_pairs={{0,3},{1,0},{2,1},{3,2},{4,7},{5,4},{6,5},{7,6},{8,11},{9,8},{10,9... | collective-permute-start | bytes 1572872 | tf_op jit(solution)/shard_map/ppermute | solution.py:28
  50.7 1.0 %copy-start.8 = (f32[8,256,128]{2,1,0:T(8,128)}, f32[8,256,128]{2,1,0:T(8,128)S(1)}, u32[]{:S(2)}) copy-start(f32[8,256,128]{2,1,0:T(8,128)S(1)} %collective-permute-done.10.s2) | copy-start | bytes 3145732
  51.7 13.5 %collective-permute-start.13 = (f32[128,1024]{1,0:T(8,128)S(1)}, f32[128,1024]{1,0:T(8,128)S(1)}, u32[]{:S(2)}, u32[]{:S(2)}) collective-permute-start(f32[128,1024]{1,0:T(8,128)S(1)} %collective-permute-done.6.wx), channel_id=1, source_target_pairs={{0,1},{1,2},{2,3},{3,0},{4,5},{5,6},{6,7},{7,4},{8,9},{9,10},{10,1... | collective-permute-start | bytes 1572872 | tf_op jit(solution)/shard_map/ppermute | solution.py:28
  65.1 5.0 %copy-start = (s32[14]{0:T(128)S(1)}, s32[14]{0:T(128)}, u32[]{:S(2)}) copy-start(s32[14]{0:T(128)} %stack.59.info_ref) | copy-start | bytes 172
  65.2 4.9 %collective-permute-start.16 = (f32[8,256,128]{2,1,0:T(8,128)S(1)}, f32[8,256,128]{2,1,0:T(8,128)S(1)}, u32[]{:S(2)}, u32[]{:S(2)}) collective-permute-start(f32[8,256,128]{2,1,0:T(8,128)S(1)} %pad_maximum_fusion.2), channel_id=1, source_target_pairs={{0,8},{1,9},{2,10},{3,11},{4,12},{5,13},{6,14},{7,15},{8,0},{9,1},... | collective-permute-start | bytes 3145736 | tf_op jit(solution)/shard_map/ppermute | solution.py:28

commit v4 on v3

v4 whole, which is shorter than its diff:
```python
import functools

import jax
import jax.numpy as jnp
import numpy as np
from jax import lax
from jax.experimental import pallas as pl
from jax.experimental.pallas import tpu as pltpu
from jax.sharding import Mesh, PartitionSpec as P

ROW = ("y", "xl", "core")
COL = ("xh", "z")
AXES = ROW + COL
SIZES = (4, 2, 2, 2, 4)
f32, bf16 = jnp.float32, jnp.bfloat16
MIB = 1 << 20
READY, EARLY, LATE, LAST = 40, 42, 24, 24
TURN_FLOPS = 1 << 20
HALF = 64


def hop(value, **move):
    pairs = []
    for source in range(int(np.prod(SIZES))):
        place = list(np.unravel_index(source, SIZES))
        for axis, step in move.items():
            k = AXES.index(axis)
            place[k] = (place[k] + step) % SIZES[k]
        pairs.append((source, int(np.ravel_multi_index(place, SIZES))))
    return lax.ppermute(value, AXES, pairs)


def after(value, *needed):
    return lax.optimization_barrier((value,) + needed)[0]


def split(value):
    high = value.astype(bf16)
    return high, (value - high.astype(f32)).astype(bf16)


def turn_kernel(amp_ref, out_ref):
    for n in range(out_ref.shape[0]):
        lanes = slice(n * 128, n * 128 + 128)
        both = jnp.concatenate([amp_ref[0, lanes], amp_ref[1, lanes]], axis=1)
        out_ref[n] = both.T


def turn(amp):
    two, depth, width = amp.shape
    return pl.pallas_call(
        turn_kernel,
        out_shape=jax.ShapeDtypeStruct((depth // 128, two * width, 128), f32),
        in_specs=[pl.BlockSpec(memory_space=pltpu.VMEM)],
        out_specs=pl.BlockSpec(memory_space=pltpu.VMEM),
        cost_estimate=pl.CostEstimate(flops=TURN_FLOPS, bytes_accessed=2 * MIB, transcendentals=0),
        name="turn",
    )(amp)


def dense(info_ref, held, high_refs, low_refs, rows=slice(0, 64)):
    width = held.shape[1] // 8
    for h in range(2):
        base = info_ref[12 + h] * 4
        for k in range(4):
            block = held.at[base + info_ref[8 + k]]
            for a in range(rows.start, rows.stop, 2):
                value = jnp.concatenate([block[pl.ds(a + b, 8, stride=width), :] for b in range(2)], axis=0)
                high, low = split(value)
                high_refs[h][a * 8 : a * 8 + 16, k * 128 : k * 128 + 128] = high
                low_refs[h][a * 8 : a * 8 + 16, k * 128 : k * 128 + 128] = low


def three(high, low, whigh, wlow):
    total = jnp.dot(high, whigh, preferred_element_type=f32)
    total += jnp.dot(high, wlow, preferred_element_type=f32)
    return total + jnp.dot(low, whigh, preferred_element_type=f32)


def pull(info_ref, held, sems, pieces):
    copies = []
    for n, (ref, start, rows, slot, offset) in enumerate(pieces):
        row = pl.multiple_of(info_ref[slot] * (2 * HALF) + offset, 8)
        copies.append(pltpu.make_async_copy(ref.at[:, pl.ds(start, rows)], held.at[:, pl.ds(row, rows)], sems.at[n]))
    return copies


def start_all(copies):
    for copy in copies:
        copy.start()


def wait_all(copies):
    for copy in copies:
        copy.wait()


def split_into(high_ref, low_ref, pieces, first=0):
    for n, ref in enumerate(pieces):
        row = (first + n) * 128
        high_ref[row : row + 128], low_ref[row : row + 128] = split(ref[...])


WHOLE = pl.BlockSpec(memory_space=pltpu.VMEM)
APART = pl.BlockSpec(memory_space=pltpu.HBM)
ANYWHERE = pl.BlockSpec(memory_space=pl.ANY)
ROWS = 8 * HALF
DEEP = 512
near = lambda value: pltpu.with_memory_space_constraint(value, pltpu.VMEM)


def ready_kernel(info_ref, x, xx, s1, w, wp, wm, high, low, high2, low2, whigh, wlow, held, sems):
    both = 2 * HALF
    copies = pull(info_ref, held, sems, [(x, 0, both, 0, 0), (xx, 0, both, 1, 0), (s1, 0, both, 2, 0), (s1, both, both, 3, 0)])
    start_all(copies)
    split_into(whigh, wlow, [w, wp, wm])
    wait_all(copies)
    dense(info_ref, held, [high, high2], [low, low2])


def ready(info, sources, weights):
    columns = weights[0].shape[1]
    return pl.pallas_call(
        ready_kernel,
        out_shape=[pltpu.VMEM((ROWS, DEEP), bf16)] * 4 + [pltpu.VMEM((384, columns), bf16)] * 2,
        in_specs=[pl.BlockSpec(memory_space=pltpu.SMEM)] + [APART] * 3 + [WHOLE] * 3,
        out_specs=[WHOLE] * 6,
        scratch_shapes=[pltpu.VMEM((8, ROWS, 128), f32), pltpu.SemaphoreType.DMA((4,))],
        compiler_params=pltpu.CompilerParams(vmem_limit_bytes=READY * MIB),
        cost_estimate=pl.CostEstimate(flops=4 * ROWS * DEEP, bytes_accessed=10 * MIB, transcendentals=0),
        name="ready",
    )(info, *sources, *weights)


def early_kernel(info_ref, s2, xp, xxp, xm, xxm, w2, high, low, whigh3, wlow3,
                 part_ref, ahigh_ref, alow_ref, whigh, wlow, held, bhigh, blow, sems):
    both = 2 * HALF
    copies = [
        pull(info_ref, held.at[j], sems.at[j], [
            (near_ref, 0, both, 0, 0), (far_ref, 0, both, 1, 0), (s2, 2 * j * both, both, 2, 0), (s2, (2 * j + 1) * both, both, 3, 0)
        ])
        for j, (near_ref, far_ref) in enumerate(((xp, xxp), (xm, xxm)))
    ]
    start_all(copies[0] + copies[1])
    whigh[0:384] = whigh3[...]
    wlow[0:384] = wlow3[...]
    split_into(whigh, wlow, [w2], 3)
    for j in range(3):
        if j:
            wait_all(copies[j - 1])
            dense(info_ref, held.at[j - 1], [bhigh.at[j - 1], ahigh_ref.at[j - 1]], [blow.at[j - 1], alow_ref.at[j - 1]])
        h, l = (high, low) if j == 0 else (bhigh.at[j - 1], blow.at[j - 1])
        for n in range(0, part_ref.shape[2], 256):
            part_ref[j, :, n : n + 256] = three(h[...], l[...], whigh[:, n : n + 256], wlow[:, n : n + 256])


def early(info, sources, w2, made):
    columns = w2.shape[1]
    return pl.pallas_call(
        early_kernel,
        out_shape=[
            pltpu.VMEM((3, ROWS, columns), f32),
            pltpu.VMEM((2, ROWS, DEEP), bf16),
            pltpu.VMEM((2, ROWS, DEEP), bf16),
            pltpu.VMEM((DEEP, columns), bf16),
            pltpu.VMEM((DEEP, columns), bf16),
        ],
        in_specs=[pl.BlockSpec(memory_space=pltpu.SMEM)] + [APART] * 5 + [WHOLE] * 5,
        out_specs=[WHOLE] * 5,
        scratch_shapes=[
            pltpu.VMEM((2, 8, ROWS, 128), f32),
            pltpu.VMEM((2, ROWS, DEEP), bf16),
            pltpu.VMEM((2, ROWS, DEEP), bf16),
            pltpu.SemaphoreType.DMA((2, 4)),
        ],
        compiler_params=pltpu.CompilerParams(vmem_limit_bytes=EARLY * MIB),
        cost_estimate=pl.CostEstimate(flops=18 * ROWS * DEEP * columns, bytes_accessed=20 * MIB, transcendentals=0),
        name="early",
    )(info, *sources, w2, *(near(v) for v in made))


def finish(out_ref, rgap_ref, cgap_ref, n, total):
    tall = rgap_ref[...].reshape(-1, 128)
    for m in range(0, 256, 128):
        gap = tall + cgap_ref[:, n + m : n + m + 128]
        out_ref[:, 0, :, n + m : n + m + 128] = (total[:, m : m + 128] / gap).reshape(-1, 8, 128)


def late_kernel(info_ref, part_ref, high2, low2, ahigh_ref, alow_ref, wx, wxp, wxm, wx2, rgap_ref, cgap_ref,
                out_ref, whigh2, wlow2):
    chunk = pl.program_id(0)

    @pl.when(chunk == 0)
    def _():
        split_into(whigh2, wlow2, [wx, wxp, wxm, wx2])

    def work(h, l):
        for n in range(0, whigh2.shape[1], 256):
            cut = slice(n, n + 256)
            finish(out_ref, rgap_ref, cgap_ref, n, part_ref[chunk, :, cut] + three(h[...], l[...], whigh2[:, cut], wlow2[:, cut]))

    pl.when(chunk == 0)(lambda: work(high2, low2))
    pl.when(chunk > 0)(lambda: work(ahigh_ref.at[chunk - 1], alow_ref.at[chunk - 1]))


def late(info, part, own, others, weights, rgap, cgap, virtuals):
    columns = weights[0].shape[1]
    rows = lambda *shape: pl.BlockSpec((virtuals, 1, 8) + shape, lambda c, i: (0, i[4 + c], 0, 0))
    return pl.pallas_call(
        late_kernel,
        out_shape=[jax.ShapeDtypeStruct((virtuals, 4, 8, columns), f32)] + [pltpu.VMEM((DEEP, columns), bf16)] * 2,
        grid_spec=pltpu.PrefetchScalarGridSpec(
            num_scalar_prefetch=1,
            grid=(3,),
            in_specs=[WHOLE] * 9 + [rows(128), WHOLE],
            out_specs=[rows(columns), WHOLE, WHOLE],
        ),
        compiler_params=pltpu.CompilerParams(vmem_limit_bytes=LATE * MIB),
        cost_estimate=pl.CostEstimate(flops=18 * ROWS * DEEP * columns, bytes_accessed=24 * MIB, transcendentals=0),
        name="late",
    )(info, *(near(v) for v in (part, *own, *others)), *weights, rgap, cgap)


def last_kernel(info_ref, rest_ref, up, down, s3, whigh, wlow, whigh2, wlow2, rgap_ref, cgap_ref,
                out_ref, held, high, low, high2, low2, sems):
    del rest_ref
    step = pl.program_id(0)
    pieces = []
    for ref, base, slot in ((up, 0, 0), (down, 0, 0), (s3, 0, 2), (s3, 2 * HALF, 2)):
        offset = HALF * (len(pieces) // 2 % 2)
        pieces += [(ref, base, HALF, slot, offset), (ref, base + HALF, HALF, slot + 1, offset)]
    copies = pull(info_ref, held, sems, pieces)

    @pl.when(step == 0)
    def _():
        start_all(copies)
        wait_all(copies)
        dense(info_ref, held, [high, high2], [low, low2])

    part = pl.ds(pl.multiple_of(step * out_ref.shape[0] * 8, 16), out_ref.shape[0] * 8)
    for n in range(0, whigh.shape[1], 256):
        cut = slice(n, n + 256)
        total = three(high[part], low[part], whigh[:, cut], wlow[:, cut])
        total += three(high2[part], low2[part], whigh2[:, cut], wlow2[:, cut])
        finish(out_ref, rgap_ref, cgap_ref, n, total)


def last(info, rest, sources, weights, rgap, cgap, virtuals):
    columns = weights[0].shape[1]
    steps = 2
    rows = lambda *shape: pl.BlockSpec((virtuals // steps, 1, 8) + shape, lambda c, i: (c, i[7], 0, 0))
    return pl.pallas_call(
        last_kernel,
        out_shape=jax.ShapeDtypeStruct((virtuals, 4, 8, columns), f32),
        grid_spec=pltpu.PrefetchScalarGridSpec(
            num_scalar_prefetch=1,
            grid=(steps,),
            in_specs=[APART] + [ANYWHERE] * 3 + [WHOLE] * 4 + [rows(128), WHOLE],
            out_specs=rows(columns),
            scratch_shapes=[pltpu.VMEM((8, ROWS, 128), f32)]
            + [pltpu.VMEM((ROWS, DEEP), bf16)] * 4
            + [pltpu.SemaphoreType.DMA((8,))],
        ),
        input_output_aliases={1: 0},
        compiler_params=pltpu.CompilerParams(vmem_limit_bytes=LAST * MIB),
        cost_estimate=pl.CostEstimate(flops=12 * ROWS * DEEP * columns, bytes_accessed=8 * MIB, transcendentals=0),
        name="last",
    )(info, rest, *sources, *(near(v) for v in weights), rgap, cgap)


def body(amplitudes, integrals, occ_energy, vir_energy):
    virtuals, own = amplitudes.shape[:2]
    depth = amplitudes.shape[2] * amplitudes.shape[3]
    columns = integrals.shape[1]
    y, xl, core, xh, z = (lax.axis_index(a) for a in AXES)

    info = jnp.stack(
        [xl * 2 + core, (1 - xl) * 2 + core, xl * 2 + 1 - core, (1 - xl) * 2 + 1 - core]
        + [y, (y + 3) % 4, (y + 1) % 4, (y + 2) % 4]
        + [z, (z + 3) % 4, (z + 1) % 4, (z + 2) % 4]
        + [xh, 1 - xh]
    ).astype(jnp.int32)
    gap = vir_energy[:, None] - occ_energy[None, :]
    row_gap = lax.dynamic_slice_in_dim(gap, (xh * 4 + z) * virtuals, virtuals)
    rgap = jnp.broadcast_to(row_gap.reshape(virtuals, 4, 8, 1), (virtuals, 4, 8, 128))
    start = ((y * 2 + xl) * 2 + core) * columns
    cgap = lax.dynamic_slice_in_dim(gap.reshape(-1), start, columns).reshape(1, columns)

    join = lambda *values: jnp.concatenate(values, axis=1)
    x = turn(amplitudes.transpose(1, 2, 3, 0).reshape(own, depth, virtuals))
    w = integrals

    wp, wm = hop(w, z=1), hop(w, z=3)
    xp, xm, xx = hop(x, y=1), hop(x, y=3), hop(x, xl=1)
    xx, wp, wm, info, rgap, cgap = lax.optimization_barrier((xx, wp, wm, info, rgap, cgap))
    xxp, xxm = hop(xx, y=1), hop(xx, y=3)
    w2, wx = hop(after(w, wp, wm), z=2), hop(after(w, xx), xh=1)
    s1 = hop(after(join(x, xx), xp, xm), core=1)
    high, low, high2, low2, whigh, wlow = ready(info, [x, xx, s1], [w, wp, wm])
    xxp, xxm, w2, wx, wlow = lax.optimization_barrier((xxp, xxm, w2, wx, wlow))
    s2 = hop(join(xp, xxp, xm, xxm), core=1)
    up = hop(join(xp[:, :HALF], xxp[:, :HALF]), y=1)
    down = hop(join(xm[:, HALF:], xxm[:, HALF:]), y=3)
    wxp, wxm, wx2 = hop(wx, z=1), hop(wx, z=3), hop(w2, xh=1)

    part, ahigh, alow, whigh, wlow = early(info, [s2, xp, xxp, xm, xxm], w2, [high, low, whigh, wlow])
    up, down, wxp, wxm, wx2, wlow = lax.optimization_barrier((up, down, wxp, wxm, wx2, wlow))
    s3 = hop(join(up, down), core=1)
    out, whigh2, wlow2 = late(info, part, [high2, low2], [ahigh, alow], [wx, wxp, wxm, wx2], rgap, cgap, virtuals)
    out = last(info, out, [up, down, s3], [whigh, wlow, whigh2, wlow2], rgap, cgap, virtuals)
    return out.reshape(virtuals * 32, columns)


def solution(mesh):
    fine = Mesh(mesh.devices.reshape(SIZES), AXES)
    in_specs = (P(COL, ROW, None, None), P(COL, ROW), P(), P())
    return jax.shard_map(body, mesh=fine, in_specs=in_specs, out_specs=P(COL, ROW), check_vma=False)
```

time: 83.2 us -> 83.3 us (level)
  waiting for transfers between devices: 25.7 us -> 21 us
  local copies, waits for them, and re-layouts: 3.26 us -> 5.31 us
  other arithmetic: 1.12 us -> 2.36 us
    ppermute x17, waiting for transfers between devices: 25.7 us -> 21 us  [hop(): return lax.ppermute(value, AXES, pairs)]
    broadcast_in_dim x3, local copies, waits for them, and re-layouts: 0.52 us -> 1.85 us  [body(): jnp.broadcast_to(row_gap.reshape(virtuals, 4, 8, 1), (virtuals, 4, 8, 128))]
    concatenate x5, other arithmetic: 0.35 us -> 1.59 us  [body(): join = lambda *values: jnp.concatenate(values, axis=1)]
    pallas_call x2 -> x4, Pallas kernels: 26.1 us -> 26.8 us  [the longest x1 10.1 us: early(): pl.pallas_call(early_kernel, out_shape=[pltpu.VMEM((3, ROWS, columns), f3...]
  transfers between devices with their start and end apart: 17 -> 17, of which waited for: 8 -> 9; matrix products, arithmetic and copies ran while one was open for 3% -> 7% of each run, Pallas kernels for 16% -> 24%
where the time goes in v4:
time: 83.3 us; the launch traced here: 82.9 us
  Pallas kernels  29.2 us (35%)
  starting transfers between devices  24.7 us (30%)
  waiting for transfers between devices  21 us (25%)
  local copies, waits for them, and re-layouts  5.31 us (6%)
  other arithmetic  2.36 us (3%)
    ppermute x17, starting transfers between devices, hop(): return lax.ppermute(value, AXES, pairs)  24.7 us
    ppermute x17, waiting for transfers between devices, hop(): return lax.ppermute(value, AXES, pairs)  21 us
    pallas_call x1, Pallas kernels, early(): pl.pallas_call(early_kernel, out_shape=[pltpu.VMEM((3, ROWS, columns), f3...  10.1 us
    pallas_call x1, Pallas kernels, late(): pl.pallas_call(late_kernel, out_shape=[jax.ShapeDtypeStruct((virtuals, 4,...  7.53 us
    pallas_call x1, Pallas kernels, last(): pl.pallas_call(last_kernel, out_shape=jax.ShapeDtypeStruct((virtuals, 4,...  6.8 us
    pallas_call x1, Pallas kernels, turn(): pl.pallas_call(turn_kernel, out_shape=jax.ShapeDtypeStruct((depth // 128,...  2.37 us
    pallas_call x1, Pallas kernels, ready(): pl.pallas_call(ready_kernel, out_shape=[pltpu.VMEM((ROWS, DEEP), bf16)] *...  2.37 us
    broadcast_in_dim x3, local copies, waits for them, and re-layouts, body(): jnp.broadcast_to(row_gap.reshape(virtuals, 4, 8, 1), (virtuals, 4, 8, 128))  1.85 us
  transfers between devices with their start and end apart: 17, of which 9 were waited for; matrix products, arithmetic and copies ran while one was open for 7% of the time, Pallas kernels for 24%

profile of v4, /device:TPU:1, one launch (start us, length us, event | category | flops | bytes accessed | tf_op | source)
XLA Modules:
  0.0 82.9 jit_solution(7197447612382966854)
XLA Ops:
  0.0 2.4 %turn.1.x = f32[8,128,128]{2,1,0:T(8,128)} custom-call(f32[2,1024,64]{2,1,0:T(8,128)} %bitcast.23), custom_call_target="tpu_custom_call" | custom-call | flops 1048576 | bytes 2097152 | tf_op jit(solution)/shard_map/turn/pallas_call | solution.py:51
  2.4 0.0 copy-start
  2.4 2.0 %collective-permute-start = (f32[8,128,128]{2,1,0:T(8,128)}, f32[8,128,128]{2,1,0:T(8,128)S(1)}, u32[]{:S(2)}, u32[]{:S(2)}) collective-permute-start(f32[8,128,128]{2,1,0:T(8,128)} %turn.1.x), channel_id=1, source_target_pairs={{0,16},{1,17},{2,18},{3,19},{4,20},{5,21},{6,22},{7,23},{8,24},{9,... | collective-permute-start | bytes 1572872 | tf_op jit(solution)/shard_map/ppermute | solution.py:30
  4.4 3.8 %collective-permute-start.2 = (f32[128,1024]{1,0:T(8,128)}, f32[128,1024]{1,0:T(8,128)S(1)}, u32[]{:S(2)}, u32[]{:S(2)}) collective-permute-start(f32[128,1024]{1,0:T(8,128)} %w.1), channel_id=1, source_target_pairs={{0,3},{1,0},{2,1},{3,2},{4,7},{5,4},{6,5},{7,6},{8,11},{9,8},{10,9... | collective-permute-start | bytes 1572872 | tf_op jit(solution)/shard_map/ppermute | solution.py:30
  8.2 0.0 collective-permute-start.1
  8.2 2.7 %collective-permute-start.8 = (f32[8,128,128]{2,1,0:T(8,128)}, f32[8,128,128]{2,1,0:T(8,128)S(1)}, u32[]{:S(2)}, u32[]{:S(2)}) collective-permute-start(f32[8,128,128]{2,1,0:T(8,128)} %turn.1.x), channel_id=1, source_target_pairs={{0,96},{1,97},{2,98},{3,99},{4,100},{5,101},{6,102},{7,103},{8,104... | collective-permute-start | bytes 1572872 | tf_op jit(solution)/shard_map/ppermute | solution.py:30
  10.9 0.0 collective-permute-start.3
  10.9 0.8 broadcast_subtract_fusion
  11.7 0.1 copy.7
  11.8 0.7 dynamic-slice_bitcast_fusion
  12.5 0.8 copy.6
  13.3 0.8 sub.37
  14.1 0.7 dynamic_slice.7
  14.8 0.1 stack.59.info_ref
  14.9 0.0 copy-start.2
  14.9 1.0 %collective-permute-done.xx = f32[8,128,128]{2,1,0:T(8,128)S(1)} collective-permute-done((f32[8,128,128]{2,1,0:T(8,128)}, f32[8,128,128]{2,1,0:T(8,128)S(1)}, u32[]{:S(2)}, u32[]{:S(2)}) %collective-permute-start) | collective-permute-done | bytes 524320 | tf_op jit(solution)/shard_map/ppermute | solution.py:30
  15.9 2.9 %collective-permute-done.2.wm = f32[128,1024]{1,0:T(8,128)S(1)} collective-permute-done((f32[128,1024]{1,0:T(8,128)}, f32[128,1024]{1,0:T(8,128)S(1)}, u32[]{:S(2)}, u32[]{:S(2)}) %collective-permute-start.2) | collective-permute-done | bytes 524320 | tf_op jit(solution)/shard_map/ppermute | solution.py:30
  18.8 3.1 %collective-permute-done.1.wp = f32[128,1024]{1,0:T(8,128)S(1)} collective-permute-done((f32[128,1024]{1,0:T(8,128)}, f32[128,1024]{1,0:T(8,128)S(1)}, u32[]{:S(2)}, u32[]{:S(2)}) %collective-permute-start.1) | collective-permute-done | bytes 524320 | tf_op jit(solution)/shard_map/ppermute | solution.py:30
  21.9 0.3 broadcast_in_dim.10.rgap_ref
  22.2 0.0 copy-done
  22.2 0.1 pad_maximum_fusion.1
  22.3 0.0 collective-permute-done.8.xm
  22.3 0.0 copy-start.4
  22.3 2.0 %collective-permute-done.3.xp = f32[8,128,128]{2,1,0:T(8,128)} collective-permute-done((f32[8,128,128]{2,1,0:T(8,128)}, f32[8,128,128]{2,1,0:T(8,128)}, u32[]{:S(2)}, u32[]{:S(2)}) %collective-permute-start.3) | collective-permute-done | bytes 524320 | tf_op jit(solution)/shard_map/ppermute | solution.py:30
  24.3 2.4 %collective-permute-start.9 = (f32[8,256,128]{2,1,0:T(8,128)S(1)}, f32[8,256,128]{2,1,0:T(8,128)S(1)}, u32[]{:S(2)}, u32[]{:S(2)}) collective-permute-start(f32[8,256,128]{2,1,0:T(8,128)S(1)} %pad_maximum_fusion.1), channel_id=1, source_target_pairs={{0,8},{1,9},{2,10},{3,11},{4,12},{5,13},{6,14},{7,15},{8,0},{9,1},... | collective-permute-start | bytes 3145736 | tf_op jit(solution)/shard_map/ppermute | solution.py:30
  26.8 0.0 copy-done.1
  26.8 2.5 %collective-permute-start.7 = (f32[128,1024]{1,0:T(8,128)S(1)}, f32[128,1024]{1,0:T(8,128)S(1)}, u32[]{:S(2)}, u32[]{:S(2)}) collective-permute-start(f32[128,1024]{1,0:T(8,128)S(1)} %copy-done.1), channel_id=1, source_target_pairs={{0,4},{1,5},{2,6},{3,7},{4,0},{5,1},{6,2},{7,3},{8,12},{9,13},{10,... | collective-permute-start | bytes 1572872 | tf_op jit(solution)/shard_map/ppermute | solution.py:30
  29.2 1.3 %collective-permute-start.6 = (f32[128,1024]{1,0:T(8,128)S(1)}, f32[128,1024]{1,0:T(8,128)S(1)}, u32[]{:S(2)}, u32[]{:S(2)}) collective-permute-start(f32[128,1024]{1,0:T(8,128)S(1)} %copy-done.1), channel_id=1, source_target_pairs={{0,2},{1,3},{2,0},{3,1},{4,6},{5,7},{6,4},{7,5},{8,10},{9,11},{10,... | collective-permute-start | bytes 1572872 | tf_op jit(solution)/shard_map/ppermute | solution.py:30
  30.5 0.0 collective-permute-start.5
  30.5 1.5 %collective-permute-start.4 = (f32[8,128,128]{2,1,0:T(8,128)S(1)}, f32[8,128,128]{2,1,0:T(8,128)S(1)}, u32[]{:S(2)}, u32[]{:S(2)}) collective-permute-start(f32[8,128,128]{2,1,0:T(8,128)S(1)} %collective-permute-done.xx), channel_id=1, source_target_pairs={{0,32},{1,33},{2,34},{3,35},{4,36},{5,37},{6,38},{7,39},{8,40},{9,... | collective-permute-start | bytes 1572872 | tf_op jit(solution)/shard_map/ppermute | solution.py:30
  32.0 0.0 collective-permute-done.9.s1
  32.0 2.4 %ready.1 = (bf16[512,512]{1,0:T(8,128)(2,1)S(1)}, bf16[512,512]{1,0:T(8,128)(2,1)S(1)}, bf16[512,512]{1,0:T(8,128)(2,1)S(1)}, bf16[512,512]{1,0:T(8,128)(2,1)S(1...) custom-call(s32[14]{0:T(128)S(1)} %stack.59.info_ref, f32[8,128,128]{2,1,0:T(8,128)S(1)} %copy-done, ...), custom_call_target="tpu_custom_call" | custom-call | flops 1048576 | bytes 10485760 | tf_op jit(solution)/shard_map/ready/pallas_call | solution.py:123
  34.4 0.0 copy-done.2
  34.4 7.4 %collective-permute-done.7.wx = f32[128,1024]{1,0:T(8,128)S(1)} collective-permute-done((f32[128,1024]{1,0:T(8,128)S(1)}, f32[128,1024]{1,0:T(8,128)S(1)}, u32[]{:S(2)}, u32[]{:S(2)}) %collective-permute-start.7) | collective-permute-done | bytes 524320 | tf_op jit(solution)/shard_map/ppermute | solution.py:30
  41.8 2.1 %collective-permute-done.6.w2 = f32[128,1024]{1,0:T(8,128)S(1)} collective-permute-done((f32[128,1024]{1,0:T(8,128)S(1)}, f32[128,1024]{1,0:T(8,128)S(1)}, u32[]{:S(2)}, u32[]{:S(2)}) %collective-permute-start.6) | collective-permute-done | bytes 524320 | tf_op jit(solution)/shard_map/ppermute | solution.py:30
  44.0 0.0 collective-permute-done.5.xxm
  44.0 0.4 collective-permute-done.4.xxp
  44.4 1.4 %pad_maximum_fusion = f32[8,512,128]{2,1,0:T(8,128)S(1)} fusion(f32[8,128,128]{2,1,0:T(8,128)S(1)} %collective-permute-done.5.xxm, f32[8,128,128]{2,1,0:T(8,128)S(1)} %collective-permute-done.8.xm, f32[8,128,128]{2,1,0:T(8,128)S(1)} %collective-permute-done.4.xxp, f32[8,128,128]{2,1,0:T(8,128)} %collective-permute-done.3.xp), kind=kLoop, calls=%fused_computation | loop fusion | flops 1572864 | bytes 4194304 | tf_op jit(solution)/shard_map/concatenate | solution.py:289
  45.7 1.8 %collective-permute-start.10 = (f32[8,512,128]{2,1,0:T(8,128)S(1)}, f32[8,512,128]{2,1,0:T(8,128)S(1)}, u32[]{:S(2)}, u32[]{:S(2)}) collective-permute-start(f32[8,512,128]{2,1,0:T(8,128)S(1)} %pad_maximum_fusion), channel_id=1, source_target_pairs={{0,8},{1,9},{2,10},{3,11},{4,12},{5,13},{6,14},{7,15},{8,0},{9,1},... | collective-permute-start | bytes 6291464 | tf_op jit(solution)/shard_map/ppermute | solution.py:30
  47.6 0.0 copy-done.4
  47.6 1.0 %slice.16 = f32[8,64,128]{2,1,0:T(8,128)S(1)} slice(f32[8,128,128]{2,1,0:T(8,128)} %collective-permute-done.3.xp), slice={[0:8], [0:64], [0:128]} | slice | bytes 524288 | tf_op jit(solution)/shard_map/slice | solution.py:302
  48.6 0.0 copy-done.6
  48.6 0.0 copy-done.5
  48.7 0.3 collective-permute-start.12
  49.0 1.3 %collective-permute-start.11 = (f32[8,128,128]{2,1,0:T(8,128)S(1)}, f32[8,128,128]{2,1,0:T(8,128)S(1)}, u32[]{:S(2)}, u32[]{:S(2)}) collective-permute-start(f32[8,128,128]{2,1,0:T(8,128)S(1)} %pad_maximum_fusion.3), channel_id=1, source_target_pairs={{0,32},{1,33},{2,34},{3,35},{4,36},{5,37},{6,38},{7,39},{8,40},{9,... | collective-permute-start | bytes 1572872 | tf_op jit(solution)/shard_map/ppermute | solution.py:30
  50.3 0.0 copy-done.8
  50.3 0.5 collective-permute-start.15
  50.8 1.9 %collective-permute-start.14 = (f32[128,1024]{1,0:T(8,128)S(1)}, f32[128,1024]{1,0:T(8,128)S(1)}, u32[]{:S(2)}, u32[]{:S(2)}) collective-permute-start(f32[128,1024]{1,0:T(8,128)S(1)} %collective-permute-done.7.wx), channel_id=1, source_target_pairs={{0,3},{1,0},{2,1},{3,2},{4,7},{5,4},{6,5},{7,6},{8,11},{9,8},{10,9... | collective-permute-start | bytes 1572872 | tf_op jit(solution)/shard_map/ppermute | solution.py:30
  52.7 0.0 collective-permute-done.10.s2
  52.7 0.6 collective-permute-start.13
  53.3 0.8 copy-done.7
  54.1 10.1 %early.1 = (f32[3,512,1024]{2,1,0:T(8,128)S(1)}, bf16[2,512,512]{2,1,0:T(8,128)(2,1)S(1)}, bf16[2,512,512]{2,1,0:T(8,128)(2,1)S(1)}, bf16[512,1024]{1,0:T(8,128)(2,1)S(1)}, bf16[512,1024]{1,0:T(8,128)(2,1)S(1)}) custom-call(s32[14]{0:T(128)} %copy-done.2, f32[8,512,128]{2,1,0:T(8,128)} %copy-done.7, f32[8,128,128]{2,1,0:T(8,128)} %collective-permute-done.3.xp, ...), custom_call_target="tpu_custom_call" | custom-call | flops 4831838208 | bytes 20971520 | tf_op jit(solution)/shard_map/early/pallas_call | solution.py:159
  64.2 0.0 copy-start.3
  64.2 0.0 collective-permute-done.12.down
  64.2 0.0 collective-permute-done.11.up
  64.2 0.5 collective-permute-done.15.wx2
  64.7 0.0 collective-permute-done.14.wxm
  64.7 1.5 %collective-permute-done.13.wxp = f32[128,1024]{1,0:T(8,128)S(1)} collective-permute-done((f32[128,1024]{1,0:T(8,128)S(1)}, f32[128,1024]{1,0:T(8,128)S(1)}, u32[]{:S(2)}, u32[]{:S(2)}) %collective-permute-start.13) | collective-permute-done | bytes 524320 | tf_op jit(solution)/shard_map/ppermute | solution.py:30
  66.2 0.1 pad_maximum_fusion.2
  66.3 2.1 %collective-permute-start.16 = (f32[8,256,128]{2,1,0:T(8,128)S(1)}, f32[8,256,128]{2,1,0:T(8,128)S(1)}, u32[]{:S(2)}, u32[]{:S(2)}) collective-permute-start(f32[8,256,128]{2,1,0:T(8,128)S(1)} %pad_maximum_fusion.2), channel_id=1, source_target_pairs={{0,8},{1,9},{2,10},{3,11},{4,12},{5,13},{6,14},{7,15},{8,0},{9,1},... | collective-permute-start | bytes 3145736 | tf_op jit(solution)/shard_map/ppermute | solution.py:30
  68.4 0.0 copy-done.3
  68.5 7.5 %late.1 = (f32[64,4,8,1024]{3,2,1,0:T(8,128)}, bf16[512,1024]{1,0:T(8,128)(2,1)S(1)}, bf16[512,1024]{1,0:T(8,128)(2,1)S(1)}) custom-call(s32[14]{0:T(128)S(1)} %copy-done.3, f32[3,512,1024]{2,1,0:T(8,128)S(1)} %get-tuple-element.54.part_ref, bf16[512,512]{1,0:T(8,128)(2,1)S(1)} %get-tuple-element.55.high2, bf16[512,512]{1,0:T(8,128)(2,1)S(1)} %get-tuple-element.56.low2, ...), custom_call_target="tpu_custom_call" | custom-call | flops 4831838208 | bytes 25165824 | tf_op jit(solution)/shard_map/late/pallas_call | solution.py:209
  76.0 0.0 collective-permute-done.16.s3
  76.0 6.8 %last.1 = f32[64,4,8,1024]{3,2,1,0:T(8,128)} custom-call(s32[14]{0:T(128)S(1)} %copy-done.3, f32[64,4,8,1024]{3,2,1,0:T(8,128)} %get-tuple-element.66.rest_ref, f32[8,128,128]{2,1,0:T(8,128)S(1)} %collective-permute-done.11.up, f32[8,128,128]{2,1,0:T(8,128)S(1)} %collective-permute-done.12.down, ...), custom_call_target="tpu_custom_call", output_to_operand_aliasing={{}: (1, {})} | custom-call | flops 3221225472 | bytes 8388608 | tf_op jit(solution)/shard_map/last/pallas_call | solution.py:252
  (10 shorter events, 0.1 us)
Async XLA Ops:
  2.4 19.8 %copy-start = (f32[8,128,128]{2,1,0:T(8,128)S(1)}, f32[8,128,128]{2,1,0:T(8,128)}, u32[]{:S(2)}) copy-start(f32[8,128,128]{2,1,0:T(8,128)} %turn.1.x) | copy-start | bytes 1572868
  2.4 13.5 %collective-permute-start = (f32[8,128,128]{2,1,0:T(8,128)}, f32[8,128,128]{2,1,0:T(8,128)S(1)}, u32[]{:S(2)}, u32[]{:S(2)}) collective-permute-start(f32[8,128,128]{2,1,0:T(8,128)} %turn.1.x), channel_id=1, source_target_pairs={{0,16},{1,17},{2,18},{3,19},{4,20},{5,21},{6,22},{7,23},{8,24},{9,... | collective-permute-start | bytes 1572872 | tf_op jit(solution)/shard_map/ppermute | solution.py:30
  4.4 14.3 %collective-permute-start.2 = (f32[128,1024]{1,0:T(8,128)}, f32[128,1024]{1,0:T(8,128)S(1)}, u32[]{:S(2)}, u32[]{:S(2)}) collective-permute-start(f32[128,1024]{1,0:T(8,128)} %w.1), channel_id=1, source_target_pairs={{0,3},{1,0},{2,1},{3,2},{4,7},{5,4},{6,5},{7,6},{8,11},{9,8},{10,9... | collective-permute-start | bytes 1572872 | tf_op jit(solution)/shard_map/ppermute | solution.py:30
  8.2 13.7 %collective-permute-start.1 = (f32[128,1024]{1,0:T(8,128)}, f32[128,1024]{1,0:T(8,128)S(1)}, u32[]{:S(2)}, u32[]{:S(2)}) collective-permute-start(f32[128,1024]{1,0:T(8,128)} %w.1), channel_id=1, source_target_pairs={{0,1},{1,2},{2,3},{3,0},{4,5},{5,6},{6,7},{7,4},{8,9},{9,10},{10,1... | collective-permute-start | bytes 1572872 | tf_op jit(solution)/shard_map/ppermute | solution.py:30
  8.2 14.1 %collective-permute-start.8 = (f32[8,128,128]{2,1,0:T(8,128)}, f32[8,128,128]{2,1,0:T(8,128)S(1)}, u32[]{:S(2)}, u32[]{:S(2)}) collective-permute-start(f32[8,128,128]{2,1,0:T(8,128)} %turn.1.x), channel_id=1, source_target_pairs={{0,96},{1,97},{2,98},{3,99},{4,100},{5,101},{6,102},{7,103},{8,104... | collective-permute-start | bytes 1572872 | tf_op jit(solution)/shard_map/ppermute | solution.py:30
  10.9 13.4 %collective-permute-start.3 = (f32[8,128,128]{2,1,0:T(8,128)}, f32[8,128,128]{2,1,0:T(8,128)}, u32[]{:S(2)}, u32[]{:S(2)}) collective-permute-start(f32[8,128,128]{2,1,0:T(8,128)} %turn.1.x), channel_id=1, source_target_pairs={{0,32},{1,33},{2,34},{3,35},{4,36},{5,37},{6,38},{7,39},{8,40},{9,... | collective-permute-start | bytes 1572872 | tf_op jit(solution)/shard_map/ppermute | solution.py:30
  11.7 15.1 %copy-start.1 = (f32[128,1024]{1,0:T(8,128)S(1)}, f32[128,1024]{1,0:T(8,128)}, u32[]{:S(2)}) copy-start(f32[128,1024]{1,0:T(8,128)} %w.1) | copy-start | bytes 1572868
  14.9 19.5 %copy-start.2 = (s32[14]{0:T(128)}, s32[14]{0:T(128)S(1)}, u32[]{:S(2)}) copy-start(s32[14]{0:T(128)S(1)} %stack.59.info_ref) | copy-start | bytes 172
  22.3 25.2 %copy-start.4 = (f32[8,128,128]{2,1,0:T(8,128)}, f32[8,128,128]{2,1,0:T(8,128)S(1)}, u32[]{:S(2)}) copy-start(f32[8,128,128]{2,1,0:T(8,128)S(1)} %collective-permute-done.8.xm) | copy-start | bytes 1572868
  24.3 7.7 %collective-permute-start.9 = (f32[8,256,128]{2,1,0:T(8,128)S(1)}, f32[8,256,128]{2,1,0:T(8,128)S(1)}, u32[]{:S(2)}, u32[]{:S(2)}) collective-permute-start(f32[8,256,128]{2,1,0:T(8,128)S(1)} %pad_maximum_fusion.1), channel_id=1, source_target_pairs={{0,8},{1,9},{2,10},{3,11},{4,12},{5,13},{6,14},{7,15},{8,0},{9,1},... | collective-permute-start | bytes 3145736 | tf_op jit(solution)/shard_map/ppermute | solution.py:30
  26.8 15.1 %collective-permute-start.7 = (f32[128,1024]{1,0:T(8,128)S(1)}, f32[128,1024]{1,0:T(8,128)S(1)}, u32[]{:S(2)}, u32[]{:S(2)}) collective-permute-start(f32[128,1024]{1,0:T(8,128)S(1)} %copy-done.1), channel_id=1, source_target_pairs={{0,4},{1,5},{2,6},{3,7},{4,0},{5,1},{6,2},{7,3},{8,12},{9,13},{10,... | collective-permute-start | bytes 1572872 | tf_op jit(solution)/shard_map/ppermute | solution.py:30
  29.2 14.7 %collective-permute-start.6 = (f32[128,1024]{1,0:T(8,128)S(1)}, f32[128,1024]{1,0:T(8,128)S(1)}, u32[]{:S(2)}, u32[]{:S(2)}) collective-permute-start(f32[128,1024]{1,0:T(8,128)S(1)} %copy-done.1), channel_id=1, source_target_pairs={{0,2},{1,3},{2,0},{3,1},{4,6},{5,7},{6,4},{7,5},{8,10},{9,11},{10,... | collective-permute-start | bytes 1572872 | tf_op jit(solution)/shard_map/ppermute | solution.py:30
  30.5 13.4 %collective-permute-start.5 = (f32[8,128,128]{2,1,0:T(8,128)S(1)}, f32[8,128,128]{2,1,0:T(8,128)S(1)}, u32[]{:S(2)}, u32[]{:S(2)}) collective-permute-start(f32[8,128,128]{2,1,0:T(8,128)S(1)} %collective-permute-done.xx), channel_id=1, source_target_pairs={{0,96},{1,97},{2,98},{3,99},{4,100},{5,101},{6,102},{7,103},{8,104... | collective-permute-start | bytes 1572872 | tf_op jit(solution)/shard_map/ppermute | solution.py:30
  30.5 13.8 %collective-permute-start.4 = (f32[8,128,128]{2,1,0:T(8,128)S(1)}, f32[8,128,128]{2,1,0:T(8,128)S(1)}, u32[]{:S(2)}, u32[]{:S(2)}) collective-permute-start(f32[8,128,128]{2,1,0:T(8,128)S(1)} %collective-permute-done.xx), channel_id=1, source_target_pairs={{0,32},{1,33},{2,34},{3,35},{4,36},{5,37},{6,38},{7,39},{8,40},{9,... | collective-permute-start | bytes 1572872 | tf_op jit(solution)/shard_map/ppermute | solution.py:30
  44.0 6.3 %copy-start.8 = (f32[128,1024]{1,0:T(8,128)}, f32[128,1024]{1,0:T(8,128)S(1)}, u32[]{:S(2)}) copy-start(f32[128,1024]{1,0:T(8,128)S(1)} %collective-permute-done.6.w2) | copy-start | bytes 1572868
  44.0 4.6 %copy-start.5 = (f32[8,128,128]{2,1,0:T(8,128)}, f32[8,128,128]{2,1,0:T(8,128)S(1)}, u32[]{:S(2)}) copy-start(f32[8,128,128]{2,1,0:T(8,128)S(1)} %collective-permute-done.5.xxm) | copy-start | bytes 1572868
  44.4 4.2 %copy-start.6 = (f32[8,128,128]{2,1,0:T(8,128)}, f32[8,128,128]{2,1,0:T(8,128)S(1)}, u32[]{:S(2)}) copy-start(f32[8,128,128]{2,1,0:T(8,128)S(1)} %collective-permute-done.4.xxp) | copy-start | bytes 1572868
  45.7 7.0 %collective-permute-start.10 = (f32[8,512,128]{2,1,0:T(8,128)S(1)}, f32[8,512,128]{2,1,0:T(8,128)S(1)}, u32[]{:S(2)}, u32[]{:S(2)}) collective-permute-start(f32[8,512,128]{2,1,0:T(8,128)S(1)} %pad_maximum_fusion), channel_id=1, source_target_pairs={{0,8},{1,9},{2,10},{3,11},{4,12},{5,13},{6,14},{7,15},{8,0},{9,1},... | collective-permute-start | bytes 6291464 | tf_op jit(solution)/shard_map/ppermute | solution.py:30
  48.7 15.5 %collective-permute-start.12 = (f32[8,128,128]{2,1,0:T(8,128)S(1)}, f32[8,128,128]{2,1,0:T(8,128)S(1)}, u32[]{:S(2)}, u32[]{:S(2)}) collective-permute-start(f32[8,128,128]{2,1,0:T(8,128)S(1)} %pad_maximum_fusion.4), channel_id=1, source_target_pairs={{0,96},{1,97},{2,98},{3,99},{4,100},{5,101},{6,102},{7,103},{8,104... | collective-permute-start | bytes 1572872 | tf_op jit(solution)/shard_map/ppermute | solution.py:30
  49.0 15.2 %collective-permute-start.11 = (f32[8,128,128]{2,1,0:T(8,128)S(1)}, f32[8,128,128]{2,1,0:T(8,128)S(1)}, u32[]{:S(2)}, u32[]{:S(2)}) collective-permute-start(f32[8,128,128]{2,1,0:T(8,128)S(1)} %pad_maximum_fusion.3), channel_id=1, source_target_pairs={{0,32},{1,33},{2,34},{3,35},{4,36},{5,37},{6,38},{7,39},{8,40},{9,... | collective-permute-start | bytes 1572872 | tf_op jit(solution)/shard_map/ppermute | solution.py:30
  50.3 14.4 %collective-permute-start.15 = (f32[128,1024]{1,0:T(8,128)S(1)}, f32[128,1024]{1,0:T(8,128)S(1)}, u32[]{:S(2)}, u32[]{:S(2)}) collective-permute-start(f32[128,1024]{1,0:T(8,128)S(1)} %collective-permute-done.6.w2), channel_id=1, source_target_pairs={{0,4},{1,5},{2,6},{3,7},{4,0},{5,1},{6,2},{7,3},{8,12},{9,13},{10,... | collective-permute-start | bytes 1572872 | tf_op jit(solution)/shard_map/ppermute | solution.py:30
  50.8 13.9 %collective-permute-start.14 = (f32[128,1024]{1,0:T(8,128)S(1)}, f32[128,1024]{1,0:T(8,128)S(1)}, u32[]{:S(2)}, u32[]{:S(2)}) collective-permute-start(f32[128,1024]{1,0:T(8,128)S(1)} %collective-permute-done.7.wx), channel_id=1, source_target_pairs={{0,3},{1,0},{2,1},{3,2},{4,7},{5,4},{6,5},{7,6},{8,11},{9,8},{10,9... | collective-permute-start | bytes 1572872 | tf_op jit(solution)/shard_map/ppermute | solution.py:30
  52.7 1.3 %copy-start.7 = (f32[8,512,128]{2,1,0:T(8,128)}, f32[8,512,128]{2,1,0:T(8,128)S(1)}, u32[]{:S(2)}) copy-start(f32[8,512,128]{2,1,0:T(8,128)S(1)} %collective-permute-done.10.s2) | copy-start | bytes 6291460
  52.7 13.5 %collective-permute-start.13 = (f32[128,1024]{1,0:T(8,128)S(1)}, f32[128,1024]{1,0:T(8,128)S(1)}, u32[]{:S(2)}, u32[]{:S(2)}) collective-permute-start(f32[128,1024]{1,0:T(8,128)S(1)} %collective-permute-done.7.wx), channel_id=1, source_target_pairs={{0,1},{1,2},{2,3},{3,0},{4,5},{5,6},{6,7},{7,4},{8,9},{9,10},{10,1... | collective-permute-start | bytes 1572872 | tf_op jit(solution)/shard_map/ppermute | solution.py:30
  64.2 4.3 %copy-start.3 = (s32[14]{0:T(128)S(1)}, s32[14]{0:T(128)}, u32[]{:S(2)}) copy-start(s32[14]{0:T(128)} %copy-done.2) | copy-start | bytes 172
  66.3 9.7 %collective-permute-start.16 = (f32[8,256,128]{2,1,0:T(8,128)S(1)}, f32[8,256,128]{2,1,0:T(8,128)S(1)}, u32[]{:S(2)}, u32[]{:S(2)}) collective-permute-start(f32[8,256,128]{2,1,0:T(8,128)S(1)} %pad_maximum_fusion.2), channel_id=1, source_target_pairs={{0,8},{1,9},{2,10},{3,11},{4,12},{5,13},{6,14},{7,15},{8,0},{9,1},... | collective-permute-start | bytes 3145736 | tf_op jit(solution)/shard_map/ppermute | solution.py:30

commit v5 on v4

--- a/solution.py
+++ b/solution.py
@@ -14,7 +14,7 @@
 SIZES = (4, 2, 2, 2, 4)
 f32, bf16 = jnp.float32, jnp.bfloat16
 MIB = 1 << 20
-READY, EARLY, LATE, LAST = 40, 42, 24, 24
+READY, EARLY, LATE, LAST = 20, 24, 24, 24
 TURN_FLOPS = 1 << 20
 HALF = 64
 
@@ -123,7 +123,7 @@
     return pl.pallas_call(
         ready_kernel,
         out_shape=[pltpu.VMEM((ROWS, DEEP), bf16)] * 4 + [pltpu.VMEM((384, columns), bf16)] * 2,
-        in_specs=[pl.BlockSpec(memory_space=pltpu.SMEM)] + [APART] * 3 + [WHOLE] * 3,
+        in_specs=[pl.BlockSpec(memory_space=pltpu.SMEM)] + [ANYWHERE] * 3 + [WHOLE] * 3,
         out_specs=[WHOLE] * 6,
         scratch_shapes=[pltpu.VMEM((8, ROWS, 128), f32), pltpu.SemaphoreType.DMA((4,))],
         compiler_params=pltpu.CompilerParams(vmem_limit_bytes=READY * MIB),
@@ -165,7 +165,7 @@
             pltpu.VMEM((DEEP, columns), bf16),
             pltpu.VMEM((DEEP, columns), bf16),
         ],
-        in_specs=[pl.BlockSpec(memory_space=pltpu.SMEM)] + [APART] * 5 + [WHOLE] * 5,
+        in_specs=[pl.BlockSpec(memory_space=pltpu.SMEM)] + [ANYWHERE] * 5 + [WHOLE] * 5,
         out_specs=[WHOLE] * 5,
         scratch_shapes=[
             pltpu.VMEM((2, 8, ROWS, 128), f32),
@@ -294,10 +294,11 @@
     xp, xm, xx = hop(x, y=1), hop(x, y=3), hop(x, xl=1)
     xx, wp, wm, info, rgap, cgap = lax.optimization_barrier((xx, wp, wm, info, rgap, cgap))
     xxp, xxm = hop(xx, y=1), hop(xx, y=3)
-    w2, wx = hop(after(w, wp, wm), z=2), hop(after(w, xx), xh=1)
-    s1 = hop(after(join(x, xx), xp, xm), core=1)
+    w2, wx = hop(after(w, wp, wm, xp), z=2), hop(after(w, xx, xm), xh=1)
+    s1 = hop(join(x, xx), core=1)
     high, low, high2, low2, whigh, wlow = ready(info, [x, xx, s1], [w, wp, wm])
-    xxp, xxm, w2, wx, wlow = lax.optimization_barrier((xxp, xxm, w2, wx, wlow))
+    xxp, xxm = lax.optimization_barrier((xxp, xxm))
+    wx, w2, xxp, xxm, wlow = lax.optimization_barrier((wx, w2, xxp, xxm, wlow))
     s2 = hop(join(xp, xxp, xm, xxm), core=1)
     up = hop(join(xp[:, :HALF], xxp[:, :HALF]), y=1)
     down = hop(join(xm[:, HALF:], xxm[:, HALF:]), y=3)

time: 83.3 us -> 80.9 us (0.971)
  local copies, waits for them, and re-layouts: 5.31 us -> 2.24 us
  waiting for transfers between devices: 21 us -> 23.6 us
  other arithmetic: 2.36 us -> 1.12 us
    ppermute x17, waiting for transfers between devices: 21 us -> 23.6 us  [hop(): return lax.ppermute(value, AXES, pairs)]
    pallas_call x1, Pallas kernels: 10.1 us -> 8.63 us  [early(): pl.pallas_call(early_kernel, out_shape=[pltpu.VMEM((3, ROWS, columns), f3...]
    broadcast_in_dim x3, local copies, waits for them, and re-layouts: 1.85 us -> 0.52 us  [body(): jnp.broadcast_to(row_gap.reshape(virtuals, 4, 8, 1), (virtuals, 4, 8, 128))]
    concatenate x5, other arithmetic: 1.59 us -> 0.35 us  [body(): join = lambda *values: jnp.concatenate(values, axis=1)]
    slice x2 -> x3, local copies, waits for them, and re-layouts: 0.99 us -> 0.02 us  [body(): up = hop(join(xp[:, :HALF], xxp[:, :HALF]), y=1)]
  transfers between devices with their start and end apart: 17 -> 17, of which waited for: 9 -> 8; matrix products, arithmetic and copies ran while one was open for 7% -> 4% of each run, Pallas kernels for 24% -> 24%
where the time goes in v5:
time: 80.9 us; the launch traced here: 80.6 us
  Pallas kernels  28.4 us (35%)
  starting transfers between devices  24.9 us (31%)
  waiting for transfers between devices  23.6 us (29%)
  local copies, waits for them, and re-layouts  2.24 us (3%)
  other arithmetic  1.12 us (1%)
    ppermute x17, starting transfers between devices, hop(): return lax.ppermute(value, AXES, pairs)  24.9 us
    ppermute x17, waiting for transfers between devices, hop(): return lax.ppermute(value, AXES, pairs)  23.6 us
    pallas_call x1, Pallas kernels, early(): pl.pallas_call(early_kernel, out_shape=[pltpu.VMEM((3, ROWS, columns), f3...  8.63 us
    pallas_call x1, Pallas kernels, late(): pl.pallas_call(late_kernel, out_shape=[jax.ShapeDtypeStruct((virtuals, 4,...  7.66 us
    pallas_call x1, Pallas kernels, last(): pl.pallas_call(last_kernel, out_shape=jax.ShapeDtypeStruct((virtuals, 4,...  6.85 us
    pallas_call x1, Pallas kernels, ready(): pl.pallas_call(ready_kernel, out_shape=[pltpu.VMEM((ROWS, DEEP), bf16)] *...  2.88 us
    pallas_call x1, Pallas kernels, turn(): pl.pallas_call(turn_kernel, out_shape=jax.ShapeDtypeStruct((depth // 128,...  2.37 us
  transfers between devices with their start and end apart: 17, of which 8 were waited for; matrix products, arithmetic and copies ran while one was open for 4% of the time, Pallas kernels for 24%

profile of v5, /device:TPU:1, one launch (start us, length us, event | category | flops | bytes accessed | tf_op | source)
XLA Modules:
  0.0 80.6 jit_solution(5963583150841502275)
XLA Ops:
  0.0 2.4 %turn.1.x = f32[8,128,128]{2,1,0:T(8,128)} custom-call(f32[2,1024,64]{2,1,0:T(8,128)} %bitcast.23), custom_call_target="tpu_custom_call" | custom-call | flops 1048576 | bytes 2097152 | tf_op jit(solution)/shard_map/turn/pallas_call | solution.py:51
  2.4 0.0 copy-start
  2.4 2.0 %collective-permute-start = (f32[8,128,128]{2,1,0:T(8,128)}, f32[8,128,128]{2,1,0:T(8,128)S(1)}, u32[]{:S(2)}, u32[]{:S(2)}) collective-permute-start(f32[8,128,128]{2,1,0:T(8,128)} %turn.1.x), channel_id=1, source_target_pairs={{0,16},{1,17},{2,18},{3,19},{4,20},{5,21},{6,22},{7,23},{8,24},{9,... | collective-permute-start | bytes 1572872 | tf_op jit(solution)/shard_map/ppermute | solution.py:30
  4.4 3.8 %collective-permute-start.2 = (f32[128,1024]{1,0:T(8,128)}, f32[128,1024]{1,0:T(8,128)S(1)}, u32[]{:S(2)}, u32[]{:S(2)}) collective-permute-start(f32[128,1024]{1,0:T(8,128)} %w.1), channel_id=1, source_target_pairs={{0,3},{1,0},{2,1},{3,2},{4,7},{5,4},{6,5},{7,6},{8,11},{9,8},{10,9... | collective-permute-start | bytes 1572872 | tf_op jit(solution)/shard_map/ppermute | solution.py:30
  8.2 0.0 collective-permute-start.1
  8.2 2.7 %collective-permute-start.4 = (f32[8,128,128]{2,1,0:T(8,128)}, f32[8,128,128]{2,1,0:T(8,128)S(1)}, u32[]{:S(2)}, u32[]{:S(2)}) collective-permute-start(f32[8,128,128]{2,1,0:T(8,128)} %turn.1.x), channel_id=1, source_target_pairs={{0,96},{1,97},{2,98},{3,99},{4,100},{5,101},{6,102},{7,103},{8,104... | collective-permute-start | bytes 1572872 | tf_op jit(solution)/shard_map/ppermute | solution.py:30
  10.9 0.0 collective-permute-start.3
  10.9 0.8 broadcast_subtract_fusion
  11.7 0.0 copy-start.3
  11.7 0.1 copy.7
  11.8 0.1 dynamic-slice_bitcast_fusion
  11.9 0.1 copy.6
  12.0 0.8 sub.37
  12.8 0.7 dynamic_slice.7
  13.5 0.1 stack.59.info_ref
  13.5 2.5 %collective-permute-done.xx = f32[8,128,128]{2,1,0:T(8,128)S(1)} collective-permute-done((f32[8,128,128]{2,1,0:T(8,128)}, f32[8,128,128]{2,1,0:T(8,128)S(1)}, u32[]{:S(2)}, u32[]{:S(2)}) %collective-permute-start) | collective-permute-done | bytes 524320 | tf_op jit(solution)/shard_map/ppermute | solution.py:30
  16.0 2.7 %collective-permute-done.2.wm = f32[128,1024]{1,0:T(8,128)S(1)} collective-permute-done((f32[128,1024]{1,0:T(8,128)}, f32[128,1024]{1,0:T(8,128)S(1)}, u32[]{:S(2)}, u32[]{:S(2)}) %collective-permute-start.2) | collective-permute-done | bytes 524320 | tf_op jit(solution)/shard_map/ppermute | solution.py:30
  18.8 3.1 %collective-permute-done.1.wp = f32[128,1024]{1,0:T(8,128)} collective-permute-done((f32[128,1024]{1,0:T(8,128)}, f32[128,1024]{1,0:T(8,128)}, u32[]{:S(2)}, u32[]{:S(2)}) %collective-permute-start.1) | collective-permute-done | bytes 524320 | tf_op jit(solution)/shard_map/ppermute | solution.py:30
  21.9 0.3 broadcast_in_dim.10.rgap_ref
  22.2 0.0 copy-done
  22.2 0.1 pad_maximum_fusion.1
  22.3 2.2 %collective-permute-start.9 = (f32[8,256,128]{2,1,0:T(8,128)S(1)}, f32[8,256,128]{2,1,0:T(8,128)S(1)}, u32[]{:S(2)}, u32[]{:S(2)}) collective-permute-start(f32[8,256,128]{2,1,0:T(8,128)S(1)} %pad_maximum_fusion.1), channel_id=1, source_target_pairs={{0,8},{1,9},{2,10},{3,11},{4,12},{5,13},{6,14},{7,15},{8,0},{9,1},... | collective-permute-start | bytes 3145736 | tf_op jit(solution)/shard_map/ppermute | solution.py:30
  24.5 2.7 %collective-permute-start.8 = (f32[8,128,128]{2,1,0:T(8,128)S(1)}, f32[8,128,128]{2,1,0:T(8,128)S(1)}, u32[]{:S(2)}, u32[]{:S(2)}) collective-permute-start(f32[8,128,128]{2,1,0:T(8,128)S(1)} %collective-permute-done.xx), channel_id=1, source_target_pairs={{0,96},{1,97},{2,98},{3,99},{4,100},{5,101},{6,102},{7,103},{8,104... | collective-permute-start | bytes 1572872 | tf_op jit(solution)/shard_map/ppermute | solution.py:30
  27.3 0.0 collective-permute-start.7
  27.3 0.0 collective-permute-done.3.xp
  27.3 0.0 copy-start.1
  27.3 0.0 collective-permute-done.4.xm
  27.3 0.0 copy-done.3
  27.3 2.5 %collective-permute-start.5 = (f32[128,1024]{1,0:T(8,128)S(1)}, f32[128,1024]{1,0:T(8,128)S(1)}, u32[]{:S(2)}, u32[]{:S(2)}) collective-permute-start(f32[128,1024]{1,0:T(8,128)S(1)} %copy-done.3), channel_id=1, source_target_pairs={{0,4},{1,5},{2,6},{3,7},{4,0},{5,1},{6,2},{7,3},{8,12},{9,13},{10,... | collective-permute-start | bytes 1572872 | tf_op jit(solution)/shard_map/ppermute | solution.py:30
  29.8 0.0 collective-permute-start.6
  29.9 8.7 %collective-permute-done.8.xxm = f32[8,128,128]{2,1,0:T(8,128)S(1)} collective-permute-done((f32[8,128,128]{2,1,0:T(8,128)S(1)}, f32[8,128,128]{2,1,0:T(8,128)S(1)}, u32[]{:S(2)}, u32[]{:S(2)}) %collective-permute-start.8) | collective-permute-done | bytes 524320 | tf_op jit(solution)/shard_map/ppermute | solution.py:30
  38.6 3.1 %collective-permute-done.7.xxp = f32[8,128,128]{2,1,0:T(8,128)S(1)} collective-permute-done((f32[8,128,128]{2,1,0:T(8,128)S(1)}, f32[8,128,128]{2,1,0:T(8,128)S(1)}, u32[]{:S(2)}, u32[]{:S(2)}) %collective-permute-start.7) | collective-permute-done | bytes 524320 | tf_op jit(solution)/shard_map/ppermute | solution.py:30
  41.7 0.0 collective-permute-done.9.s1
  41.7 2.9 %ready.1 = (bf16[512,512]{1,0:T(8,128)(2,1)S(1)}, bf16[512,512]{1,0:T(8,128)(2,1)S(1)}, bf16[512,512]{1,0:T(8,128)(2,1)S(1)}, bf16[512,512]{1,0:T(8,128)(2,1)S(1...) custom-call(s32[14]{0:T(128)S(1)} %stack.59.info_ref, f32[8,128,128]{2,1,0:T(8,128)S(1)} %copy-done, ...), custom_call_target="tpu_custom_call" | custom-call | flops 1048576 | bytes 10485760 | tf_op jit(solution)/shard_map/ready/pallas_call | solution.py:123
  44.5 0.0 collective-permute-done.5.wx
  44.6 0.0 collective-permute-done.6.w2
  44.6 0.1 pad_maximum_fusion
  44.7 1.3 %collective-permute-start.10 = (f32[8,512,128]{2,1,0:T(8,128)S(1)}, f32[8,512,128]{2,1,0:T(8,128)S(1)}, u32[]{:S(2)}, u32[]{:S(2)}) collective-permute-start(f32[8,512,128]{2,1,0:T(8,128)S(1)} %pad_maximum_fusion), channel_id=1, source_target_pairs={{0,8},{1,9},{2,10},{3,11},{4,12},{5,13},{6,14},{7,15},{8,0},{9,1},... | collective-permute-start | bytes 6291464 | tf_op jit(solution)/shard_map/ppermute | solution.py:30
  46.0 0.0 copy-done.1
  46.0 0.0 slice-start
  46.0 0.0 copy-start.2
  46.1 2.7 %collective-permute-start.12 = (f32[8,128,128]{2,1,0:T(8,128)S(1)}, f32[8,128,128]{2,1,0:T(8,128)S(1)}, u32[]{:S(2)}, u32[]{:S(2)}) collective-permute-start(f32[8,128,128]{2,1,0:T(8,128)S(1)} %pad_maximum_fusion.4), channel_id=1, source_target_pairs={{0,96},{1,97},{2,98},{3,99},{4,100},{5,101},{6,102},{7,103},{8,104... | collective-permute-start | bytes 1572872 | tf_op jit(solution)/shard_map/ppermute | solution.py:30
  48.8 0.0 slice-done
  48.8 0.1 collective-permute-start.11
  48.9 1.3 %collective-permute-start.15 = (f32[128,1024]{1,0:T(8,128)S(1)}, f32[128,1024]{1,0:T(8,128)S(1)}, u32[]{:S(2)}, u32[]{:S(2)}) collective-permute-start(f32[128,1024]{1,0:T(8,128)S(1)} %collective-permute-done.6.w2), channel_id=1, source_target_pairs={{0,4},{1,5},{2,6},{3,7},{4,0},{5,1},{6,2},{7,3},{8,12},{9,13},{10,... | collective-permute-start | bytes 1572872 | tf_op jit(solution)/shard_map/ppermute | solution.py:30
  50.2 0.0 collective-permute-start.14
  50.2 0.0 collective-permute-done.10.s2
  50.2 1.5 %collective-permute-start.13 = (f32[128,1024]{1,0:T(8,128)S(1)}, f32[128,1024]{1,0:T(8,128)S(1)}, u32[]{:S(2)}, u32[]{:S(2)}) collective-permute-start(f32[128,1024]{1,0:T(8,128)S(1)} %collective-permute-done.5.wx), channel_id=1, source_target_pairs={{0,1},{1,2},{2,3},{3,0},{4,5},{5,6},{6,7},{7,4},{8,9},{9,10},{10,1... | collective-permute-start | bytes 1572872 | tf_op jit(solution)/shard_map/ppermute | solution.py:30
  51.7 0.0 copy-done.2
  51.7 8.6 %early.1 = (f32[3,512,1024]{2,1,0:T(8,128)S(1)}, bf16[2,512,512]{2,1,0:T(8,128)(2,1)S(1)}, bf16[2,512,512]{2,1,0:T(8,128)(2,1)S(1)}, bf16[512,1024]{1,0:T(8,128)(2,1)S(1)}, bf16[512,1024]{1,0:T(8,128)(2,1)S(1)}) custom-call(s32[14]{0:T(128)S(1)} %stack.59.info_ref, f32[8,512,128]{2,1,0:T(8,128)S(1)} %collective-permute-done.10.s2, ...), custom_call_target="tpu_custom_call" | custom-call | flops 4831838208 | bytes 20971520 | tf_op jit(solution)/shard_map/early/pallas_call | solution.py:159
  60.3 0.0 collective-permute-done.12.down
  60.3 3.0 %collective-permute-done.11.up = f32[8,128,128]{2,1,0:T(8,128)S(1)} collective-permute-done((f32[8,128,128]{2,1,0:T(8,128)S(1)}, f32[8,128,128]{2,1,0:T(8,128)S(1)}, u32[]{:S(2)}, u32[]{:S(2)}) %collective-permute-start.11) | collective-permute-done | bytes 524320 | tf_op jit(solution)/shard_map/ppermute | solution.py:30
  63.3 0.4 collective-permute-done.15.wx2
  63.7 0.0 collective-permute-done.14.wxm
  63.7 0.1 collective-permute-done.13.wxp
  63.8 0.1 pad_maximum_fusion.2
  63.9 2.0 %collective-permute-start.16 = (f32[8,256,128]{2,1,0:T(8,128)S(1)}, f32[8,256,128]{2,1,0:T(8,128)S(1)}, u32[]{:S(2)}, u32[]{:S(2)}) collective-permute-start(f32[8,256,128]{2,1,0:T(8,128)S(1)} %pad_maximum_fusion.2), channel_id=1, source_target_pairs={{0,8},{1,9},{2,10},{3,11},{4,12},{5,13},{6,14},{7,15},{8,0},{9,1},... | collective-permute-start | bytes 3145736 | tf_op jit(solution)/shard_map/ppermute | solution.py:30
  65.9 7.7 %late.1 = (f32[64,4,8,1024]{3,2,1,0:T(8,128)}, bf16[512,1024]{1,0:T(8,128)(2,1)S(1)}, bf16[512,1024]{1,0:T(8,128)(2,1)S(1)}) custom-call(s32[14]{0:T(128)S(1)} %stack.59.info_ref, f32[3,512,1024]{2,1,0:T(8,128)S(1)} %get-tuple-element.56.part_ref, bf16[512,512]{1,0:T(8,128)(2,1)S(1)} %get-tuple-element.57.high2, ...), custom_call_target="tpu_custom_call" | custom-call | flops 4831838208 | bytes 25165824 | tf_op jit(solution)/shard_map/late/pallas_call | solution.py:209
  73.6 0.0 collective-permute-done.16.s3
  73.6 6.8 %last.1 = f32[64,4,8,1024]{3,2,1,0:T(8,128)} custom-call(s32[14]{0:T(128)S(1)} %stack.59.info_ref, f32[64,4,8,1024]{3,2,1,0:T(8,128)} %get-tuple-element.68.rest_ref, f32[8,128,128]{2,1,0:T(8,128)S(1)} %collective-permute-done.11.up, f32[8,128,128]{2,1,0:T(8,128)S(1)} %collective-permute-done.12.down, ...), custom_call_target="tpu_custom_call", output_to_operand_aliasing={{}: (1, {})} | custom-call | flops 3221225472 | bytes 8388608 | tf_op jit(solution)/shard_map/last/pallas_call | solution.py:252
  (5 shorter events, 0.1 us)
Async XLA Ops:
  2.4 19.8 %copy-start = (f32[8,128,128]{2,1,0:T(8,128)S(1)}, f32[8,128,128]{2,1,0:T(8,128)}, u32[]{:S(2)}) copy-start(f32[8,128,128]{2,1,0:T(8,128)} %turn.1.x) | copy-start | bytes 1572868
  2.4 13.6 %collective-permute-start = (f32[8,128,128]{2,1,0:T(8,128)}, f32[8,128,128]{2,1,0:T(8,128)S(1)}, u32[]{:S(2)}, u32[]{:S(2)}) collective-permute-start(f32[8,128,128]{2,1,0:T(8,128)} %turn.1.x), channel_id=1, source_target_pairs={{0,16},{1,17},{2,18},{3,19},{4,20},{5,21},{6,22},{7,23},{8,24},{9,... | collective-permute-start | bytes 1572872 | tf_op jit(solution)/shard_map/ppermute | solution.py:30
  4.4 14.3 %collective-permute-start.2 = (f32[128,1024]{1,0:T(8,128)}, f32[128,1024]{1,0:T(8,128)S(1)}, u32[]{:S(2)}, u32[]{:S(2)}) collective-permute-start(f32[128,1024]{1,0:T(8,128)} %w.1), channel_id=1, source_target_pairs={{0,3},{1,0},{2,1},{3,2},{4,7},{5,4},{6,5},{7,6},{8,11},{9,8},{10,9... | collective-permute-start | bytes 1572872 | tf_op jit(solution)/shard_map/ppermute | solution.py:30
  8.2 13.7 %collective-permute-start.1 = (f32[128,1024]{1,0:T(8,128)}, f32[128,1024]{1,0:T(8,128)}, u32[]{:S(2)}, u32[]{:S(2)}) collective-permute-start(f32[128,1024]{1,0:T(8,128)} %w.1), channel_id=1, source_target_pairs={{0,1},{1,2},{2,3},{3,0},{4,5},{5,6},{6,7},{7,4},{8,9},{9,10},{10,1... | collective-permute-start | bytes 1572872 | tf_op jit(solution)/shard_map/ppermute | solution.py:30
  8.2 19.1 %collective-permute-start.4 = (f32[8,128,128]{2,1,0:T(8,128)}, f32[8,128,128]{2,1,0:T(8,128)S(1)}, u32[]{:S(2)}, u32[]{:S(2)}) collective-permute-start(f32[8,128,128]{2,1,0:T(8,128)} %turn.1.x), channel_id=1, source_target_pairs={{0,96},{1,97},{2,98},{3,99},{4,100},{5,101},{6,102},{7,103},{8,104... | collective-permute-start | bytes 1572872 | tf_op jit(solution)/shard_map/ppermute | solution.py:30
  10.9 16.4 %collective-permute-start.3 = (f32[8,128,128]{2,1,0:T(8,128)}, f32[8,128,128]{2,1,0:T(8,128)S(1)}, u32[]{:S(2)}, u32[]{:S(2)}) collective-permute-start(f32[8,128,128]{2,1,0:T(8,128)} %turn.1.x), channel_id=1, source_target_pairs={{0,32},{1,33},{2,34},{3,35},{4,36},{5,37},{6,38},{7,39},{8,40},{9,... | collective-permute-start | bytes 1572872 | tf_op jit(solution)/shard_map/ppermute | solution.py:30
  11.7 15.6 %copy-start.3 = (f32[128,1024]{1,0:T(8,128)S(1)}, f32[128,1024]{1,0:T(8,128)}, u32[]{:S(2)}) copy-start(f32[128,1024]{1,0:T(8,128)} %w.1) | copy-start | bytes 1572868
  22.3 19.4 %collective-permute-start.9 = (f32[8,256,128]{2,1,0:T(8,128)S(1)}, f32[8,256,128]{2,1,0:T(8,128)S(1)}, u32[]{:S(2)}, u32[]{:S(2)}) collective-permute-start(f32[8,256,128]{2,1,0:T(8,128)S(1)} %pad_maximum_fusion.1), channel_id=1, source_target_pairs={{0,8},{1,9},{2,10},{3,11},{4,12},{5,13},{6,14},{7,15},{8,0},{9,1},... | collective-permute-start | bytes 3145736 | tf_op jit(solution)/shard_map/ppermute | solution.py:30
  24.5 14.0 %collective-permute-start.8 = (f32[8,128,128]{2,1,0:T(8,128)S(1)}, f32[8,128,128]{2,1,0:T(8,128)S(1)}, u32[]{:S(2)}, u32[]{:S(2)}) collective-permute-start(f32[8,128,128]{2,1,0:T(8,128)S(1)} %collective-permute-done.xx), channel_id=1, source_target_pairs={{0,96},{1,97},{2,98},{3,99},{4,100},{5,101},{6,102},{7,103},{8,104... | collective-permute-start | bytes 1572872 | tf_op jit(solution)/shard_map/ppermute | solution.py:30
  27.3 14.4 %collective-permute-start.7 = (f32[8,128,128]{2,1,0:T(8,128)S(1)}, f32[8,128,128]{2,1,0:T(8,128)S(1)}, u32[]{:S(2)}, u32[]{:S(2)}) collective-permute-start(f32[8,128,128]{2,1,0:T(8,128)S(1)} %collective-permute-done.xx), channel_id=1, source_target_pairs={{0,32},{1,33},{2,34},{3,35},{4,36},{5,37},{6,38},{7,39},{8,40},{9,... | collective-permute-start | bytes 1572872 | tf_op jit(solution)/shard_map/ppermute | solution.py:30
  27.3 18.7 %copy-start.1 = (f32[8,128,128]{2,1,0:T(8,128)}, f32[8,128,128]{2,1,0:T(8,128)S(1)}, u32[]{:S(2)}) copy-start(f32[8,128,128]{2,1,0:T(8,128)S(1)} %collective-permute-done.3.xp) | copy-start | bytes 1572868
  27.3 17.2 %collective-permute-start.5 = (f32[128,1024]{1,0:T(8,128)S(1)}, f32[128,1024]{1,0:T(8,128)S(1)}, u32[]{:S(2)}, u32[]{:S(2)}) collective-permute-start(f32[128,1024]{1,0:T(8,128)S(1)} %copy-done.3), channel_id=1, source_target_pairs={{0,4},{1,5},{2,6},{3,7},{4,0},{5,1},{6,2},{7,3},{8,12},{9,13},{10,... | collective-permute-start | bytes 1572872 | tf_op jit(solution)/shard_map/ppermute | solution.py:30
  29.8 14.7 %collective-permute-start.6 = (f32[128,1024]{1,0:T(8,128)S(1)}, f32[128,1024]{1,0:T(8,128)S(1)}, u32[]{:S(2)}, u32[]{:S(2)}) collective-permute-start(f32[128,1024]{1,0:T(8,128)S(1)} %copy-done.3), channel_id=1, source_target_pairs={{0,2},{1,3},{2,0},{3,1},{4,6},{5,7},{6,4},{7,5},{8,10},{9,11},{10,... | collective-permute-start | bytes 1572872 | tf_op jit(solution)/shard_map/ppermute | solution.py:30
  44.7 5.5 %collective-permute-start.10 = (f32[8,512,128]{2,1,0:T(8,128)S(1)}, f32[8,512,128]{2,1,0:T(8,128)S(1)}, u32[]{:S(2)}, u32[]{:S(2)}) collective-permute-start(f32[8,512,128]{2,1,0:T(8,128)S(1)} %pad_maximum_fusion), channel_id=1, source_target_pairs={{0,8},{1,9},{2,10},{3,11},{4,12},{5,13},{6,14},{7,15},{8,0},{9,1},... | collective-permute-start | bytes 6291464 | tf_op jit(solution)/shard_map/ppermute | solution.py:30
  46.0 2.8 %slice-start = ((f32[8,128,128]{2,1,0:T(8,128)}), f32[8,64,128]{2,1,0:T(8,128)S(1)}, s32[]{:S(2)}) async-start(f32[8,128,128]{2,1,0:T(8,128)} %copy-done.1), calls=%async_computation | async-start | bytes 524288 | tf_op jit(solution)/shard_map/slice | solution.py:303
  46.0 5.7 %copy-start.2 = (f32[8,128,128]{2,1,0:T(8,128)S(1)}, f32[8,128,128]{2,1,0:T(8,128)}, u32[]{:S(2)}) copy-start(f32[8,128,128]{2,1,0:T(8,128)} %copy-done.1) | copy-start | bytes 1572868
  46.1 14.2 %collective-permute-start.12 = (f32[8,128,128]{2,1,0:T(8,128)S(1)}, f32[8,128,128]{2,1,0:T(8,128)S(1)}, u32[]{:S(2)}, u32[]{:S(2)}) collective-permute-start(f32[8,128,128]{2,1,0:T(8,128)S(1)} %pad_maximum_fusion.4), channel_id=1, source_target_pairs={{0,96},{1,97},{2,98},{3,99},{4,100},{5,101},{6,102},{7,103},{8,104... | collective-permute-start | bytes 1572872 | tf_op jit(solution)/shard_map/ppermute | solution.py:30
  48.8 14.5 %collective-permute-start.11 = (f32[8,128,128]{2,1,0:T(8,128)S(1)}, f32[8,128,128]{2,1,0:T(8,128)S(1)}, u32[]{:S(2)}, u32[]{:S(2)}) collective-permute-start(f32[8,128,128]{2,1,0:T(8,128)S(1)} %pad_maximum_fusion.3), channel_id=1, source_target_pairs={{0,32},{1,33},{2,34},{3,35},{4,36},{5,37},{6,38},{7,39},{8,40},{9,... | collective-permute-start | bytes 1572872 | tf_op jit(solution)/shard_map/ppermute | solution.py:30
  48.9 14.8 %collective-permute-start.15 = (f32[128,1024]{1,0:T(8,128)S(1)}, f32[128,1024]{1,0:T(8,128)S(1)}, u32[]{:S(2)}, u32[]{:S(2)}) collective-permute-start(f32[128,1024]{1,0:T(8,128)S(1)} %collective-permute-done.6.w2), channel_id=1, source_target_pairs={{0,4},{1,5},{2,6},{3,7},{4,0},{5,1},{6,2},{7,3},{8,12},{9,13},{10,... | collective-permute-start | bytes 1572872 | tf_op jit(solution)/shard_map/ppermute | solution.py:30
  50.2 13.5 %collective-permute-start.14 = (f32[128,1024]{1,0:T(8,128)S(1)}, f32[128,1024]{1,0:T(8,128)S(1)}, u32[]{:S(2)}, u32[]{:S(2)}) collective-permute-start(f32[128,1024]{1,0:T(8,128)S(1)} %collective-permute-done.5.wx), channel_id=1, source_target_pairs={{0,3},{1,0},{2,1},{3,2},{4,7},{5,4},{6,5},{7,6},{8,11},{9,8},{10,9... | collective-permute-start | bytes 1572872 | tf_op jit(solution)/shard_map/ppermute | solution.py:30
  50.2 13.6 %collective-permute-start.13 = (f32[128,1024]{1,0:T(8,128)S(1)}, f32[128,1024]{1,0:T(8,128)S(1)}, u32[]{:S(2)}, u32[]{:S(2)}) collective-permute-start(f32[128,1024]{1,0:T(8,128)S(1)} %collective-permute-done.5.wx), channel_id=1, source_target_pairs={{0,1},{1,2},{2,3},{3,0},{4,5},{5,6},{6,7},{7,4},{8,9},{9,10},{10,1... | collective-permute-start | bytes 1572872 | tf_op jit(solution)/shard_map/ppermute | solution.py:30
  63.9 9.7 %collective-permute-start.16 = (f32[8,256,128]{2,1,0:T(8,128)S(1)}, f32[8,256,128]{2,1,0:T(8,128)S(1)}, u32[]{:S(2)}, u32[]{:S(2)}) collective-permute-start(f32[8,256,128]{2,1,0:T(8,128)S(1)} %pad_maximum_fusion.2), channel_id=1, source_target_pairs={{0,8},{1,9},{2,10},{3,11},{4,12},{5,13},{6,14},{7,15},{8,0},{9,1},... | collective-permute-start | bytes 3145736 | tf_op jit(solution)/shard_map/ppermute | solution.py:30

commit v6 on v5

--- a/solution.py
+++ b/solution.py
@@ -58,7 +58,7 @@
     )(amp)
 
 
-def dense(info_ref, held, high_refs, low_refs, rows=slice(0, 64)):
+def dense(info_ref, held, high_refs, low_refs, rows=range(64)):
     width = held.shape[1] // 8
     for h in range(2):
         base = info_ref[12 + h] * 4
@@ -67,8 +67,9 @@
             for a in range(rows.start, rows.stop, 2):
                 value = jnp.concatenate([block[pl.ds(a + b, 8, stride=width), :] for b in range(2)], axis=0)
                 high, low = split(value)
-                high_refs[h][a * 8 : a * 8 + 16, k * 128 : k * 128 + 128] = high
-                low_refs[h][a * 8 : a * 8 + 16, k * 128 : k * 128 + 128] = low
+                row = (a - rows.start) * 8
+                high_refs[h][row : row + 16, k * 128 : k * 128 + 128] = high
+                low_refs[h][row : row + 16, k * 128 : k * 128 + 128] = low
 
 
 def three(high, low, whigh, wlow):
@@ -222,7 +223,9 @@
 
 
 def last_kernel(info_ref, rest_ref, up, down, s3, whigh, wlow, whigh2, wlow2, rgap_ref, cgap_ref,
-                out_ref, held, high, low, high2, low2, sems):
+                out_ref, held, *scratch):
+    *scratch, sems = scratch
+    high, low, high2, low2 = (scratch[n : n + 2] for n in range(0, 8, 2))
     del rest_ref
     step = pl.program_id(0)
     pieces = []
@@ -231,18 +234,29 @@
         pieces += [(ref, base, HALF, slot, offset), (ref, base + HALF, HALF, slot + 1, offset)]
     copies = pull(info_ref, held, sems, pieces)
 
+    half = out_ref.shape[0]
+
+    def work(h):
+        for n in range(0, whigh.shape[1], 256):
+            cut = slice(n, n + 256)
+            total = three(high[h][...], low[h][...], whigh[:, cut], wlow[:, cut])
+            total += three(high2[h][...], low2[h][...], whigh2[:, cut], wlow2[:, cut])
+            finish(out_ref, rgap_ref, cgap_ref, n, total)
+
+    def gather(h):
+        dense(info_ref, held, [high[h], high2[h]], [low[h], low2[h]], range(h * half, h * half + half))
+
     @pl.when(step == 0)
     def _():
         start_all(copies)
         wait_all(copies)
-        dense(info_ref, held, [high, high2], [low, low2])
-
-    part = pl.ds(pl.multiple_of(step * out_ref.shape[0] * 8, 16), out_ref.shape[0] * 8)
-    for n in range(0, whigh.shape[1], 256):
-        cut = slice(n, n + 256)
-        total = three(high[part], low[part], whigh[:, cut], wlow[:, cut])
-        total += three(high2[part], low2[part], whigh2[:, cut], wlow2[:, cut])
-        finish(out_ref, rgap_ref, cgap_ref, n, total)
+        gather(0)
+        gather(1)
+        work(0)
+
+    @pl.when(step == 1)
+    def _():
+        work(1)
 
 
 def last(info, rest, sources, weights, rgap, cgap, virtuals):
@@ -258,7 +272,7 @@
             in_specs=[APART] + [ANYWHERE] * 3 + [WHOLE] * 4 + [rows(128), WHOLE],
             out_specs=rows(columns),
             scratch_shapes=[pltpu.VMEM((8, ROWS, 128), f32)]
-            + [pltpu.VMEM((ROWS, DEEP), bf16)] * 4
+            + [pltpu.VMEM((ROWS // steps, DEEP), bf16)] * 8
             + [pltpu.SemaphoreType.DMA((8,))],
         ),
         input_output_aliases={1: 0},
@@ -294,11 +308,11 @@
     xp, xm, xx = hop(x, y=1), hop(x, y=3), hop(x, xl=1)
     xx, wp, wm, info, rgap, cgap = lax.optimization_barrier((xx, wp, wm, info, rgap, cgap))
     xxp, xxm = hop(xx, y=1), hop(xx, y=3)
-    w2, wx = hop(after(w, wp, wm, xp), z=2), hop(after(w, xx, xm), xh=1)
-    s1 = hop(join(x, xx), core=1)
+    w2, wx = hop(after(w, wp, wm), z=2), hop(after(w, xx), xh=1)
+    s1 = hop(after(join(x, xx), xp, xm), core=1)
     high, low, high2, low2, whigh, wlow = ready(info, [x, xx, s1], [w, wp, wm])
-    xxp, xxm = lax.optimization_barrier((xxp, xxm))
-    wx, w2, xxp, xxm, wlow = lax.optimization_barrier((wx, w2, xxp, xxm, wlow))
+    xxp, xxm, wlow = lax.optimization_barrier((xxp, xxm, wlow))
+    wx, w2, xxp, xxm = lax.optimization_barrier((wx, w2, xxp, xxm))
     s2 = hop(join(xp, xxp, xm, xxm), core=1)
     up = hop(join(xp[:, :HALF], xxp[:, :HALF]), y=1)
     down = hop(join(xm[:, HALF:], xxm[:, HALF:]), y=3)

time: 80.9 us -> 82.3 us (1.017)
  waiting for transfers between devices: 23.6 us -> 25 us
    ppermute x17, waiting for transfers between devices: 23.6 us -> 25 us  [hop(): return lax.ppermute(value, AXES, pairs)]
  transfers between devices with their start and end apart: 17 -> 17, of which waited for: 8 -> 12; matrix products, arithmetic and copies ran while one was open for 4% -> 4% of each run, Pallas kernels for 24% -> 23%
where the time goes in v6:
time: 82.3 us; the launch traced here: 82.1 us
  Pallas kernels  28.2 us (34%)
  starting transfers between devices  25.2 us (31%)
  waiting for transfers between devices  25 us (30%)
  local copies, waits for them, and re-layouts  2.24 us (3%)
  other arithmetic  1.12 us (1%)
    ppermute x17, starting transfers between devices, hop(): return lax.ppermute(value, AXES, pairs)  25.2 us
    ppermute x17, waiting for transfers between devices, hop(): return lax.ppermute(value, AXES, pairs)  25 us
    pallas_call x1, Pallas kernels, early(): pl.pallas_call(early_kernel, out_shape=[pltpu.VMEM((3, ROWS, columns), f3...  8.63 us
    pallas_call x1, Pallas kernels, late(): pl.pallas_call(late_kernel, out_shape=[jax.ShapeDtypeStruct((virtuals, 4,...  7.67 us
    pallas_call x1, Pallas kernels, last(): pl.pallas_call(last_kernel, out_shape=jax.ShapeDtypeStruct((virtuals, 4,...  6.62 us
    pallas_call x1, Pallas kernels, ready(): pl.pallas_call(ready_kernel, out_shape=[pltpu.VMEM((ROWS, DEEP), bf16)] *...  2.88 us
    pallas_call x1, Pallas kernels, turn(): pl.pallas_call(turn_kernel, out_shape=jax.ShapeDtypeStruct((depth // 128,...  2.37 us
  transfers between devices with their start and end apart: 17, of which 12 were waited for; matrix products, arithmetic and copies ran while one was open for 4% of the time, Pallas kernels for 23%

profile of v6, /device:TPU:1, one launch (start us, length us, event | category | flops | bytes accessed | tf_op | source)
XLA Modules:
  0.0 82.1 jit_solution(15179092759214855085)
XLA Ops:
  0.0 2.4 %turn.1.x = f32[8,128,128]{2,1,0:T(8,128)} custom-call(f32[2,1024,64]{2,1,0:T(8,128)} %bitcast.23), custom_call_target="tpu_custom_call" | custom-call | flops 1048576 | bytes 2097152 | tf_op jit(solution)/shard_map/turn/pallas_call | solution.py:51
  2.4 0.0 copy-start
  2.4 2.0 %collective-permute-start = (f32[8,128,128]{2,1,0:T(8,128)}, f32[8,128,128]{2,1,0:T(8,128)S(1)}, u32[]{:S(2)}, u32[]{:S(2)}) collective-permute-start(f32[8,128,128]{2,1,0:T(8,128)} %turn.1.x), channel_id=1, source_target_pairs={{0,16},{1,17},{2,18},{3,19},{4,20},{5,21},{6,22},{7,23},{8,24},{9,... | collective-permute-start | bytes 1572872 | tf_op jit(solution)/shard_map/ppermute | solution.py:30
  4.4 3.8 %collective-permute-start.2 = (f32[128,1024]{1,0:T(8,128)}, f32[128,1024]{1,0:T(8,128)S(1)}, u32[]{:S(2)}, u32[]{:S(2)}) collective-permute-start(f32[128,1024]{1,0:T(8,128)} %w.1), channel_id=1, source_target_pairs={{0,3},{1,0},{2,1},{3,2},{4,7},{5,4},{6,5},{7,6},{8,11},{9,8},{10,9... | collective-permute-start | bytes 1572872 | tf_op jit(solution)/shard_map/ppermute | solution.py:30
  8.2 0.0 collective-permute-start.1
  8.2 2.7 %collective-permute-start.8 = (f32[8,128,128]{2,1,0:T(8,128)}, f32[8,128,128]{2,1,0:T(8,128)S(1)}, u32[]{:S(2)}, u32[]{:S(2)}) collective-permute-start(f32[8,128,128]{2,1,0:T(8,128)} %turn.1.x), channel_id=1, source_target_pairs={{0,96},{1,97},{2,98},{3,99},{4,100},{5,101},{6,102},{7,103},{8,104... | collective-permute-start | bytes 1572872 | tf_op jit(solution)/shard_map/ppermute | solution.py:30
  10.9 0.0 collective-permute-start.3
  10.9 0.8 broadcast_subtract_fusion
  11.7 0.0 copy-start.3
  11.7 0.1 copy.7
  11.8 0.1 dynamic-slice_bitcast_fusion
  11.9 0.1 copy.6
  12.0 0.8 sub.37
  12.8 0.7 dynamic_slice.7
  13.5 0.1 stack.59.info_ref
  13.5 2.5 %collective-permute-done.xx = f32[8,128,128]{2,1,0:T(8,128)S(1)} collective-permute-done((f32[8,128,128]{2,1,0:T(8,128)}, f32[8,128,128]{2,1,0:T(8,128)S(1)}, u32[]{:S(2)}, u32[]{:S(2)}) %collective-permute-start) | collective-permute-done | bytes 524320 | tf_op jit(solution)/shard_map/ppermute | solution.py:30
  16.0 2.7 %collective-permute-done.2.wm = f32[128,1024]{1,0:T(8,128)S(1)} collective-permute-done((f32[128,1024]{1,0:T(8,128)}, f32[128,1024]{1,0:T(8,128)S(1)}, u32[]{:S(2)}, u32[]{:S(2)}) %collective-permute-start.2) | collective-permute-done | bytes 524320 | tf_op jit(solution)/shard_map/ppermute | solution.py:30
  18.8 3.1 %collective-permute-done.1.wp = f32[128,1024]{1,0:T(8,128)} collective-permute-done((f32[128,1024]{1,0:T(8,128)}, f32[128,1024]{1,0:T(8,128)}, u32[]{:S(2)}, u32[]{:S(2)}) %collective-permute-start.1) | collective-permute-done | bytes 524320 | tf_op jit(solution)/shard_map/ppermute | solution.py:30
  21.9 0.3 broadcast_in_dim.10.rgap_ref
  22.2 0.0 copy-done
  22.2 0.1 pad_maximum_fusion.1
  22.3 0.0 collective-permute-done.8.xm
  22.3 1.9 %collective-permute-done.3.xp = f32[8,128,128]{2,1,0:T(8,128)S(1)} collective-permute-done((f32[8,128,128]{2,1,0:T(8,128)}, f32[8,128,128]{2,1,0:T(8,128)S(1)}, u32[]{:S(2)}, u32[]{:S(2)}) %collective-permute-start.3) | collective-permute-done | bytes 524320 | tf_op jit(solution)/shard_map/ppermute | solution.py:30
  24.2 0.0 copy-start.1
  24.2 2.4 %collective-permute-start.9 = (f32[8,256,128]{2,1,0:T(8,128)S(1)}, f32[8,256,128]{2,1,0:T(8,128)S(1)}, u32[]{:S(2)}, u32[]{:S(2)}) collective-permute-start(f32[8,256,128]{2,1,0:T(8,128)S(1)} %pad_maximum_fusion.1), channel_id=1, source_target_pairs={{0,8},{1,9},{2,10},{3,11},{4,12},{5,13},{6,14},{7,15},{8,0},{9,1},... | collective-permute-start | bytes 3145736 | tf_op jit(solution)/shard_map/ppermute | solution.py:30
  26.7 0.6 collective-permute-start.7
  27.3 0.8 %collective-permute-start.6 = (f32[8,128,128]{2,1,0:T(8,128)S(1)}, f32[8,128,128]{2,1,0:T(8,128)S(1)}, u32[]{:S(2)}, u32[]{:S(2)}) collective-permute-start(f32[8,128,128]{2,1,0:T(8,128)S(1)} %collective-permute-done.xx), channel_id=1, source_target_pairs={{0,32},{1,33},{2,34},{3,35},{4,36},{5,37},{6,38},{7,39},{8,40},{9,... | collective-permute-start | bytes 1572872 | tf_op jit(solution)/shard_map/ppermute | solution.py:30
  28.1 0.0 copy-done.3
  28.1 2.5 %collective-permute-start.4 = (f32[128,1024]{1,0:T(8,128)S(1)}, f32[128,1024]{1,0:T(8,128)S(1)}, u32[]{:S(2)}, u32[]{:S(2)}) collective-permute-start(f32[128,1024]{1,0:T(8,128)S(1)} %copy-done.3), channel_id=1, source_target_pairs={{0,4},{1,5},{2,6},{3,7},{4,0},{5,1},{6,2},{7,3},{8,12},{9,13},{10,... | collective-permute-start | bytes 1572872 | tf_op jit(solution)/shard_map/ppermute | solution.py:30
  30.6 1.3 %collective-permute-start.5 = (f32[128,1024]{1,0:T(8,128)S(1)}, f32[128,1024]{1,0:T(8,128)S(1)}, u32[]{:S(2)}, u32[]{:S(2)}) collective-permute-start(f32[128,1024]{1,0:T(8,128)S(1)} %copy-done.3), channel_id=1, source_target_pairs={{0,2},{1,3},{2,0},{3,1},{4,6},{5,7},{6,4},{7,5},{8,10},{9,11},{10,... | collective-permute-start | bytes 1572872 | tf_op jit(solution)/shard_map/ppermute | solution.py:30
  31.9 0.0 collective-permute-done.9.s1
  31.9 2.9 %ready.1 = (bf16[512,512]{1,0:T(8,128)(2,1)S(1)}, bf16[512,512]{1,0:T(8,128)(2,1)S(1)}, bf16[512,512]{1,0:T(8,128)(2,1)S(1)}, bf16[512,512]{1,0:T(8,128)(2,1)S(1...) custom-call(s32[14]{0:T(128)S(1)} %stack.59.info_ref, f32[8,128,128]{2,1,0:T(8,128)S(1)} %copy-done, ...), custom_call_target="tpu_custom_call" | custom-call | flops 1048576 | bytes 10485760 | tf_op jit(solution)/shard_map/ready/pallas_call | solution.py:124
  34.8 5.4 %collective-permute-done.7.xxm = f32[8,128,128]{2,1,0:T(8,128)S(1)} collective-permute-done((f32[8,128,128]{2,1,0:T(8,128)S(1)}, f32[8,128,128]{2,1,0:T(8,128)S(1)}, u32[]{:S(2)}, u32[]{:S(2)}) %collective-permute-start.7) | collective-permute-done | bytes 524320 | tf_op jit(solution)/shard_map/ppermute | solution.py:30
  40.2 1.5 %collective-permute-done.6.xxp = f32[8,128,128]{2,1,0:T(8,128)S(1)} collective-permute-done((f32[8,128,128]{2,1,0:T(8,128)S(1)}, f32[8,128,128]{2,1,0:T(8,128)S(1)}, u32[]{:S(2)}, u32[]{:S(2)}) %collective-permute-start.6) | collective-permute-done | bytes 524320 | tf_op jit(solution)/shard_map/ppermute | solution.py:30
  41.7 0.9 %collective-permute-done.4.wx = f32[128,1024]{1,0:T(8,128)S(1)} collective-permute-done((f32[128,1024]{1,0:T(8,128)S(1)}, f32[128,1024]{1,0:T(8,128)S(1)}, u32[]{:S(2)}, u32[]{:S(2)}) %collective-permute-start.4) | collective-permute-done | bytes 524320 | tf_op jit(solution)/shard_map/ppermute | solution.py:30
  42.6 2.1 %collective-permute-done.5.w2 = f32[128,1024]{1,0:T(8,128)S(1)} collective-permute-done((f32[128,1024]{1,0:T(8,128)S(1)}, f32[128,1024]{1,0:T(8,128)S(1)}, u32[]{:S(2)}, u32[]{:S(2)}) %collective-permute-start.5) | collective-permute-done | bytes 524320 | tf_op jit(solution)/shard_map/ppermute | solution.py:30
  44.7 0.1 pad_maximum_fusion
  44.8 1.8 %collective-permute-start.10 = (f32[8,512,128]{2,1,0:T(8,128)S(1)}, f32[8,512,128]{2,1,0:T(8,128)S(1)}, u32[]{:S(2)}, u32[]{:S(2)}) collective-permute-start(f32[8,512,128]{2,1,0:T(8,128)S(1)} %pad_maximum_fusion), channel_id=1, source_target_pairs={{0,8},{1,9},{2,10},{3,11},{4,12},{5,13},{6,14},{7,15},{8,0},{9,1},... | collective-permute-start | bytes 6291464 | tf_op jit(solution)/shard_map/ppermute | solution.py:30
  46.7 0.0 copy-done.1
  46.7 0.0 slice-start
  46.7 0.0 copy-start.2
  46.8 1.9 %collective-permute-start.12 = (f32[8,128,128]{2,1,0:T(8,128)S(1)}, f32[8,128,128]{2,1,0:T(8,128)S(1)}, u32[]{:S(2)}, u32[]{:S(2)}) collective-permute-start(f32[8,128,128]{2,1,0:T(8,128)S(1)} %pad_maximum_fusion.4), channel_id=1, source_target_pairs={{0,96},{1,97},{2,98},{3,99},{4,100},{5,101},{6,102},{7,103},{8,104... | collective-permute-start | bytes 1572872 | tf_op jit(solution)/shard_map/ppermute | solution.py:30
  48.7 0.0 slice-done
  48.8 0.1 collective-permute-start.11
  48.9 0.6 collective-permute-start.15
  49.5 2.2 %collective-permute-start.14 = (f32[128,1024]{1,0:T(8,128)S(1)}, f32[128,1024]{1,0:T(8,128)S(1)}, u32[]{:S(2)}, u32[]{:S(2)}) collective-permute-start(f32[128,1024]{1,0:T(8,128)S(1)} %collective-permute-done.4.wx), channel_id=1, source_target_pairs={{0,3},{1,0},{2,1},{3,2},{4,7},{5,4},{6,5},{7,6},{8,11},{9,8},{10,9... | collective-permute-start | bytes 1572872 | tf_op jit(solution)/shard_map/ppermute | solution.py:30
  51.7 0.0 collective-permute-done.10.s2
  51.7 0.0 collective-permute-start.13
  51.7 0.0 copy-done.2
  51.7 8.6 %early.1 = (f32[3,512,1024]{2,1,0:T(8,128)S(1)}, bf16[2,512,512]{2,1,0:T(8,128)(2,1)S(1)}, bf16[2,512,512]{2,1,0:T(8,128)(2,1)S(1)}, bf16[512,1024]{1,0:T(8,128)(2,1)S(1)}, bf16[512,1024]{1,0:T(8,128)(2,1)S(1)}) custom-call(s32[14]{0:T(128)S(1)} %stack.59.info_ref, f32[8,512,128]{2,1,0:T(8,128)S(1)} %collective-permute-done.10.s2, ...), custom_call_target="tpu_custom_call" | custom-call | flops 4831838208 | bytes 20971520 | tf_op jit(solution)/shard_map/early/pallas_call | solution.py:160
  60.3 0.1 collective-permute-done.12.down
  60.4 2.9 %collective-permute-done.11.up = f32[8,128,128]{2,1,0:T(8,128)S(1)} collective-permute-done((f32[8,128,128]{2,1,0:T(8,128)S(1)}, f32[8,128,128]{2,1,0:T(8,128)S(1)}, u32[]{:S(2)}, u32[]{:S(2)}) %collective-permute-start.11) | collective-permute-done | bytes 524320 | tf_op jit(solution)/shard_map/ppermute | solution.py:30
  63.3 0.4 collective-permute-done.15.wx2
  63.7 0.0 collective-permute-done.14.wxm
  63.7 1.5 %collective-permute-done.13.wxp = f32[128,1024]{1,0:T(8,128)S(1)} collective-permute-done((f32[128,1024]{1,0:T(8,128)S(1)}, f32[128,1024]{1,0:T(8,128)S(1)}, u32[]{:S(2)}, u32[]{:S(2)}) %collective-permute-start.13) | collective-permute-done | bytes 524320 | tf_op jit(solution)/shard_map/ppermute | solution.py:30
  65.1 0.1 pad_maximum_fusion.2
  65.2 2.4 %collective-permute-start.16 = (f32[8,256,128]{2,1,0:T(8,128)S(1)}, f32[8,256,128]{2,1,0:T(8,128)S(1)}, u32[]{:S(2)}, u32[]{:S(2)}) collective-permute-start(f32[8,256,128]{2,1,0:T(8,128)S(1)} %pad_maximum_fusion.2), channel_id=1, source_target_pairs={{0,8},{1,9},{2,10},{3,11},{4,12},{5,13},{6,14},{7,15},{8,0},{9,1},... | collective-permute-start | bytes 3145736 | tf_op jit(solution)/shard_map/ppermute | solution.py:30
  67.6 7.7 %late.1 = (f32[64,4,8,1024]{3,2,1,0:T(8,128)}, bf16[512,1024]{1,0:T(8,128)(2,1)S(1)}, bf16[512,1024]{1,0:T(8,128)(2,1)S(1)}) custom-call(s32[14]{0:T(128)S(1)} %stack.59.info_ref, f32[3,512,1024]{2,1,0:T(8,128)S(1)} %get-tuple-element.58.part_ref, bf16[512,512]{1,0:T(8,128)(2,1)S(1)} %get-tuple-element.59.high2, ...), custom_call_target="tpu_custom_call" | custom-call | flops 4831838208 | bytes 25165824 | tf_op jit(solution)/shard_map/late/pallas_call | solution.py:210
  75.2 0.0 collective-permute-done.16.s3
  75.3 6.6 %last.1 = f32[64,4,8,1024]{3,2,1,0:T(8,128)} custom-call(s32[14]{0:T(128)S(1)} %stack.59.info_ref, f32[64,4,8,1024]{3,2,1,0:T(8,128)} %get-tuple-element.70.rest_ref, f32[8,128,128]{2,1,0:T(8,128)S(1)} %collective-permute-done.11.up, f32[8,128,128]{2,1,0:T(8,128)S(1)} %collective-permute-done.12.down, ...), custom_call_target="tpu_custom_call", output_to_operand_aliasing={{}: (1, {})} | custom-call | flops 3221225472 | bytes 8388608 | tf_op jit(solution)/shard_map/last/pallas_call | solution.py:266
  (5 shorter events, 0.1 us)
Async XLA Ops:
  2.4 19.8 %copy-start = (f32[8,128,128]{2,1,0:T(8,128)S(1)}, f32[8,128,128]{2,1,0:T(8,128)}, u32[]{:S(2)}) copy-start(f32[8,128,128]{2,1,0:T(8,128)} %turn.1.x) | copy-start | bytes 1572868
  2.4 13.6 %collective-permute-start = (f32[8,128,128]{2,1,0:T(8,128)}, f32[8,128,128]{2,1,0:T(8,128)S(1)}, u32[]{:S(2)}, u32[]{:S(2)}) collective-permute-start(f32[8,128,128]{2,1,0:T(8,128)} %turn.1.x), channel_id=1, source_target_pairs={{0,16},{1,17},{2,18},{3,19},{4,20},{5,21},{6,22},{7,23},{8,24},{9,... | collective-permute-start | bytes 1572872 | tf_op jit(solution)/shard_map/ppermute | solution.py:30
  4.4 14.3 %collective-permute-start.2 = (f32[128,1024]{1,0:T(8,128)}, f32[128,1024]{1,0:T(8,128)S(1)}, u32[]{:S(2)}, u32[]{:S(2)}) collective-permute-start(f32[128,1024]{1,0:T(8,128)} %w.1), channel_id=1, source_target_pairs={{0,3},{1,0},{2,1},{3,2},{4,7},{5,4},{6,5},{7,6},{8,11},{9,8},{10,9... | collective-permute-start | bytes 1572872 | tf_op jit(solution)/shard_map/ppermute | solution.py:30
  8.2 13.7 %collective-permute-start.1 = (f32[128,1024]{1,0:T(8,128)}, f32[128,1024]{1,0:T(8,128)}, u32[]{:S(2)}, u32[]{:S(2)}) collective-permute-start(f32[128,1024]{1,0:T(8,128)} %w.1), channel_id=1, source_target_pairs={{0,1},{1,2},{2,3},{3,0},{4,5},{5,6},{6,7},{7,4},{8,9},{9,10},{10,1... | collective-permute-start | bytes 1572872 | tf_op jit(solution)/shard_map/ppermute | solution.py:30
  8.2 14.1 %collective-permute-start.8 = (f32[8,128,128]{2,1,0:T(8,128)}, f32[8,128,128]{2,1,0:T(8,128)S(1)}, u32[]{:S(2)}, u32[]{:S(2)}) collective-permute-start(f32[8,128,128]{2,1,0:T(8,128)} %turn.1.x), channel_id=1, source_target_pairs={{0,96},{1,97},{2,98},{3,99},{4,100},{5,101},{6,102},{7,103},{8,104... | collective-permute-start | bytes 1572872 | tf_op jit(solution)/shard_map/ppermute | solution.py:30
  10.9 13.3 %collective-permute-start.3 = (f32[8,128,128]{2,1,0:T(8,128)}, f32[8,128,128]{2,1,0:T(8,128)S(1)}, u32[]{:S(2)}, u32[]{:S(2)}) collective-permute-start(f32[8,128,128]{2,1,0:T(8,128)} %turn.1.x), channel_id=1, source_target_pairs={{0,32},{1,33},{2,34},{3,35},{4,36},{5,37},{6,38},{7,39},{8,40},{9,... | collective-permute-start | bytes 1572872 | tf_op jit(solution)/shard_map/ppermute | solution.py:30
  11.7 16.5 %copy-start.3 = (f32[128,1024]{1,0:T(8,128)S(1)}, f32[128,1024]{1,0:T(8,128)}, u32[]{:S(2)}) copy-start(f32[128,1024]{1,0:T(8,128)} %w.1) | copy-start | bytes 1572868
  24.2 22.5 %copy-start.1 = (f32[8,128,128]{2,1,0:T(8,128)}, f32[8,128,128]{2,1,0:T(8,128)S(1)}, u32[]{:S(2)}) copy-start(f32[8,128,128]{2,1,0:T(8,128)S(1)} %collective-permute-done.3.xp) | copy-start | bytes 1572868
  24.2 7.7 %collective-permute-start.9 = (f32[8,256,128]{2,1,0:T(8,128)S(1)}, f32[8,256,128]{2,1,0:T(8,128)S(1)}, u32[]{:S(2)}, u32[]{:S(2)}) collective-permute-start(f32[8,256,128]{2,1,0:T(8,128)S(1)} %pad_maximum_fusion.1), channel_id=1, source_target_pairs={{0,8},{1,9},{2,10},{3,11},{4,12},{5,13},{6,14},{7,15},{8,0},{9,1},... | collective-permute-start | bytes 3145736 | tf_op jit(solution)/shard_map/ppermute | solution.py:30
  26.7 13.6 %collective-permute-start.7 = (f32[8,128,128]{2,1,0:T(8,128)S(1)}, f32[8,128,128]{2,1,0:T(8,128)S(1)}, u32[]{:S(2)}, u32[]{:S(2)}) collective-permute-start(f32[8,128,128]{2,1,0:T(8,128)S(1)} %collective-permute-done.xx), channel_id=1, source_target_pairs={{0,96},{1,97},{2,98},{3,99},{4,100},{5,101},{6,102},{7,103},{8,104... | collective-permute-start | bytes 1572872 | tf_op jit(solution)/shard_map/ppermute | solution.py:30
  27.3 14.4 %collective-permute-start.6 = (f32[8,128,128]{2,1,0:T(8,128)S(1)}, f32[8,128,128]{2,1,0:T(8,128)S(1)}, u32[]{:S(2)}, u32[]{:S(2)}) collective-permute-start(f32[8,128,128]{2,1,0:T(8,128)S(1)} %collective-permute-done.xx), channel_id=1, source_target_pairs={{0,32},{1,33},{2,34},{3,35},{4,36},{5,37},{6,38},{7,39},{8,40},{9,... | collective-permute-start | bytes 1572872 | tf_op jit(solution)/shard_map/ppermute | solution.py:30
  28.1 14.4 %collective-permute-start.4 = (f32[128,1024]{1,0:T(8,128)S(1)}, f32[128,1024]{1,0:T(8,128)S(1)}, u32[]{:S(2)}, u32[]{:S(2)}) collective-permute-start(f32[128,1024]{1,0:T(8,128)S(1)} %copy-done.3), channel_id=1, source_target_pairs={{0,4},{1,5},{2,6},{3,7},{4,0},{5,1},{6,2},{7,3},{8,12},{9,13},{10,... | collective-permute-start | bytes 1572872 | tf_op jit(solution)/shard_map/ppermute | solution.py:30
  30.6 14.1 %collective-permute-start.5 = (f32[128,1024]{1,0:T(8,128)S(1)}, f32[128,1024]{1,0:T(8,128)S(1)}, u32[]{:S(2)}, u32[]{:S(2)}) collective-permute-start(f32[128,1024]{1,0:T(8,128)S(1)} %copy-done.3), channel_id=1, source_target_pairs={{0,2},{1,3},{2,0},{3,1},{4,6},{5,7},{6,4},{7,5},{8,10},{9,11},{10,... | collective-permute-start | bytes 1572872 | tf_op jit(solution)/shard_map/ppermute | solution.py:30
  44.8 6.8 %collective-permute-start.10 = (f32[8,512,128]{2,1,0:T(8,128)S(1)}, f32[8,512,128]{2,1,0:T(8,128)S(1)}, u32[]{:S(2)}, u32[]{:S(2)}) collective-permute-start(f32[8,512,128]{2,1,0:T(8,128)S(1)} %pad_maximum_fusion), channel_id=1, source_target_pairs={{0,8},{1,9},{2,10},{3,11},{4,12},{5,13},{6,14},{7,15},{8,0},{9,1},... | collective-permute-start | bytes 6291464 | tf_op jit(solution)/shard_map/ppermute | solution.py:30
  46.7 2.0 %slice-start = ((f32[8,128,128]{2,1,0:T(8,128)}), f32[8,64,128]{2,1,0:T(8,128)S(1)}, s32[]{:S(2)}) async-start(f32[8,128,128]{2,1,0:T(8,128)} %copy-done.1), calls=%async_computation | async-start | bytes 524288 | tf_op jit(solution)/shard_map/slice | solution.py:317
  46.7 5.0 %copy-start.2 = (f32[8,128,128]{2,1,0:T(8,128)S(1)}, f32[8,128,128]{2,1,0:T(8,128)}, u32[]{:S(2)}) copy-start(f32[8,128,128]{2,1,0:T(8,128)} %copy-done.1) | copy-start | bytes 1572868
  46.8 13.6 %collective-permute-start.12 = (f32[8,128,128]{2,1,0:T(8,128)S(1)}, f32[8,128,128]{2,1,0:T(8,128)S(1)}, u32[]{:S(2)}, u32[]{:S(2)}) collective-permute-start(f32[8,128,128]{2,1,0:T(8,128)S(1)} %pad_maximum_fusion.4), channel_id=1, source_target_pairs={{0,96},{1,97},{2,98},{3,99},{4,100},{5,101},{6,102},{7,103},{8,104... | collective-permute-start | bytes 1572872 | tf_op jit(solution)/shard_map/ppermute | solution.py:30
  48.8 14.5 %collective-permute-start.11 = (f32[8,128,128]{2,1,0:T(8,128)S(1)}, f32[8,128,128]{2,1,0:T(8,128)S(1)}, u32[]{:S(2)}, u32[]{:S(2)}) collective-permute-start(f32[8,128,128]{2,1,0:T(8,128)S(1)} %pad_maximum_fusion.3), channel_id=1, source_target_pairs={{0,32},{1,33},{2,34},{3,35},{4,36},{5,37},{6,38},{7,39},{8,40},{9,... | collective-permute-start | bytes 1572872 | tf_op jit(solution)/shard_map/ppermute | solution.py:30
  48.9 14.8 %collective-permute-start.15 = (f32[128,1024]{1,0:T(8,128)S(1)}, f32[128,1024]{1,0:T(8,128)S(1)}, u32[]{:S(2)}, u32[]{:S(2)}) collective-permute-start(f32[128,1024]{1,0:T(8,128)S(1)} %collective-permute-done.5.w2), channel_id=1, source_target_pairs={{0,4},{1,5},{2,6},{3,7},{4,0},{5,1},{6,2},{7,3},{8,12},{9,13},{10,... | collective-permute-start | bytes 1572872 | tf_op jit(solution)/shard_map/ppermute | solution.py:30
  49.5 14.2 %collective-permute-start.14 = (f32[128,1024]{1,0:T(8,128)S(1)}, f32[128,1024]{1,0:T(8,128)S(1)}, u32[]{:S(2)}, u32[]{:S(2)}) collective-permute-start(f32[128,1024]{1,0:T(8,128)S(1)} %collective-permute-done.4.wx), channel_id=1, source_target_pairs={{0,3},{1,0},{2,1},{3,2},{4,7},{5,4},{6,5},{7,6},{8,11},{9,8},{10,9... | collective-permute-start | bytes 1572872 | tf_op jit(solution)/shard_map/ppermute | solution.py:30
  51.7 13.5 %collective-permute-start.13 = (f32[128,1024]{1,0:T(8,128)S(1)}, f32[128,1024]{1,0:T(8,128)S(1)}, u32[]{:S(2)}, u32[]{:S(2)}) collective-permute-start(f32[128,1024]{1,0:T(8,128)S(1)} %collective-permute-done.4.wx), channel_id=1, source_target_pairs={{0,1},{1,2},{2,3},{3,0},{4,5},{5,6},{6,7},{7,4},{8,9},{9,10},{10,1... | collective-permute-start | bytes 1572872 | tf_op jit(solution)/shard_map/ppermute | solution.py:30
  65.2 10.0 %collective-permute-start.16 = (f32[8,256,128]{2,1,0:T(8,128)S(1)}, f32[8,256,128]{2,1,0:T(8,128)S(1)}, u32[]{:S(2)}, u32[]{:S(2)}) collective-permute-start(f32[8,256,128]{2,1,0:T(8,128)S(1)} %pad_maximum_fusion.2), channel_id=1, source_target_pairs={{0,8},{1,9},{2,10},{3,11},{4,12},{5,13},{6,14},{7,15},{8,0},{9,1},... | collective-permute-start | bytes 3145736 | tf_op jit(solution)/shard_map/ppermute | solution.py:30

commit v7 on v6

--- a/solution.py
+++ b/solution.py
@@ -138,7 +138,7 @@
     both = 2 * HALF
     copies = [
         pull(info_ref, held.at[j], sems.at[j], [
-            (near_ref, 0, both, 0, 0), (far_ref, 0, both, 1, 0), (s2, 2 * j * both, both, 2, 0), (s2, (2 * j + 1) * both, both, 3, 0)
+            (near_ref, 0, both, 0, 0), (far_ref, 0, both, 1, 0), (s2, (2 * j + 2) * both, both, 2, 0), (s2, (2 * j + 3) * both, both, 3, 0)
         ])
         for j, (near_ref, far_ref) in enumerate(((xp, xxp), (xm, xxm)))
     ]
@@ -308,16 +308,15 @@
     xp, xm, xx = hop(x, y=1), hop(x, y=3), hop(x, xl=1)
     xx, wp, wm, info, rgap, cgap = lax.optimization_barrier((xx, wp, wm, info, rgap, cgap))
     xxp, xxm = hop(xx, y=1), hop(xx, y=3)
-    w2, wx = hop(after(w, wp, wm), z=2), hop(after(w, xx), xh=1)
-    s1 = hop(after(join(x, xx), xp, xm), core=1)
-    high, low, high2, low2, whigh, wlow = ready(info, [x, xx, s1], [w, wp, wm])
-    xxp, xxm, wlow = lax.optimization_barrier((xxp, xxm, wlow))
+    w2, wx = hop(after(w, wp, wm, xp), z=2), hop(after(w, xx, xm), xh=1)
+    xxp, xxm = lax.optimization_barrier((xxp, xxm))
     wx, w2, xxp, xxm = lax.optimization_barrier((wx, w2, xxp, xxm))
-    s2 = hop(join(xp, xxp, xm, xxm), core=1)
+    s2 = hop(join(x, xx, xp, xxp, xm, xxm), core=1)
     up = hop(join(xp[:, :HALF], xxp[:, :HALF]), y=1)
     down = hop(join(xm[:, HALF:], xxm[:, HALF:]), y=3)
     wxp, wxm, wx2 = hop(wx, z=1), hop(wx, z=3), hop(w2, xh=1)
 
+    high, low, high2, low2, whigh, wlow = ready(info, [x, xx, s2], [w, wp, wm])
     part, ahigh, alow, whigh, wlow = early(info, [s2, xp, xxp, xm, xxm], w2, [high, low, whigh, wlow])
     up, down, wxp, wxm, wx2, wlow = lax.optimization_barrier((up, down, wxp, wxm, wx2, wlow))
     s3 = hop(join(up, down), core=1)

time: 82.3 us -> 79.3 us (0.964)
  local copies, waits for them, and re-layouts: 2.24 us -> 4.8 us
  starting transfers between devices: 25.2 us -> 22.8 us
  waiting for transfers between devices: 25 us -> 22.7 us
    ppermute x17 -> x16, starting transfers between devices: 25.2 us -> 22.8 us  [hop(): return lax.ppermute(value, AXES, pairs)]
    ppermute x17 -> x16, waiting for transfers between devices: 25 us -> 22.7 us  [hop(): return lax.ppermute(value, AXES, pairs)]
    broadcast_in_dim x3, local copies, waits for them, and re-layouts: 0.52 us -> 1.83 us  [body(): jnp.broadcast_to(row_gap.reshape(virtuals, 4, 8, 1), (virtuals, 4, 8, 128))]
    unnamed x8 -> x9, local copies, waits for them, and re-layouts: 0.02 us -> 1.23 us
  transfers between devices with their start and end apart: 17 -> 16, of which waited for: 12 -> 11; matrix products, arithmetic and copies ran while one was open for 4% -> 7% of each run, Pallas kernels for 23% -> 23%
where the time goes in v7:
time: 79.3 us; the launch traced here: 79.1 us
  Pallas kernels  27.5 us (35%)
  starting transfers between devices  22.8 us (29%)
  waiting for transfers between devices  22.7 us (29%)
  local copies, waits for them, and re-layouts  4.8 us (6%)
  other arithmetic  0.91 us (1%)
    ppermute x16, starting transfers between devices, hop(): return lax.ppermute(value, AXES, pairs)  22.8 us
    ppermute x16, waiting for transfers between devices, hop(): return lax.ppermute(value, AXES, pairs)  22.7 us
    pallas_call x1, Pallas kernels, early(): pl.pallas_call(early_kernel, out_shape=[pltpu.VMEM((3, ROWS, columns), f3...  8.58 us
    pallas_call x1, Pallas kernels, late(): pl.pallas_call(late_kernel, out_shape=[jax.ShapeDtypeStruct((virtuals, 4,...  7.54 us
    pallas_call x1, Pallas kernels, last(): pl.pallas_call(last_kernel, out_shape=jax.ShapeDtypeStruct((virtuals, 4,...  6.55 us
    pallas_call x1, Pallas kernels, turn(): pl.pallas_call(turn_kernel, out_shape=jax.ShapeDtypeStruct((depth // 128,...  2.43 us
    pallas_call x1, Pallas kernels, ready(): pl.pallas_call(ready_kernel, out_shape=[pltpu.VMEM((ROWS, DEEP), bf16)] *...  2.37 us
    broadcast_in_dim x3, local copies, waits for them, and re-layouts, body(): jnp.broadcast_to(row_gap.reshape(virtuals, 4, 8, 1), (virtuals, 4, 8, 128))  1.83 us
  transfers between devices with their start and end apart: 16, of which 11 were waited for; matrix products, arithmetic and copies ran while one was open for 7% of the time, Pallas kernels for 23%

profile of v7, /device:TPU:1, one launch (start us, length us, event | category | flops | bytes accessed | tf_op | source)
XLA Modules:
  0.0 79.1 jit_solution(4239580614386484449)
XLA Ops:
  0.0 0.0 copy-start.1
  0.0 2.4 %turn.1.x = f32[8,128,128]{2,1,0:T(8,128)} custom-call(f32[2,1024,64]{2,1,0:T(8,128)} %bitcast.23), custom_call_target="tpu_custom_call" | custom-call | flops 1048576 | bytes 2097152 | tf_op jit(solution)/shard_map/turn/pallas_call | solution.py:51
  2.4 2.0 %collective-permute-start = (f32[8,128,128]{2,1,0:T(8,128)}, f32[8,128,128]{2,1,0:T(8,128)S(1)}, u32[]{:S(2)}, u32[]{:S(2)}) collective-permute-start(f32[8,128,128]{2,1,0:T(8,128)} %turn.1.x), channel_id=1, source_target_pairs={{0,16},{1,17},{2,18},{3,19},{4,20},{5,21},{6,22},{7,23},{8,24},{9,... | collective-permute-start | bytes 1572872 | tf_op jit(solution)/shard_map/ppermute | solution.py:30
  4.5 3.8 %collective-permute-start.2 = (f32[128,1024]{1,0:T(8,128)}, f32[128,1024]{1,0:T(8,128)S(1)}, u32[]{:S(2)}, u32[]{:S(2)}) collective-permute-start(f32[128,1024]{1,0:T(8,128)} %w.1), channel_id=1, source_target_pairs={{0,3},{1,0},{2,1},{3,2},{4,7},{5,4},{6,5},{7,6},{8,11},{9,8},{10,9... | collective-permute-start | bytes 1572872 | tf_op jit(solution)/shard_map/ppermute | solution.py:30
  8.2 0.0 collective-permute-start.1
  8.2 1.3 %collective-permute-start.3 = (f32[8,128,128]{2,1,0:T(8,128)}, f32[8,128,128]{2,1,0:T(8,128)S(1)}, u32[]{:S(2)}, u32[]{:S(2)}) collective-permute-start(f32[8,128,128]{2,1,0:T(8,128)} %turn.1.x), channel_id=1, source_target_pairs={{0,32},{1,33},{2,34},{3,35},{4,36},{5,37},{6,38},{7,39},{8,40},{9,... | collective-permute-start | bytes 1572872 | tf_op jit(solution)/shard_map/ppermute | solution.py:30
  9.5 1.4 %collective-permute-start.4 = (f32[8,128,128]{2,1,0:T(8,128)}, f32[8,128,128]{2,1,0:T(8,128)S(1)}, u32[]{:S(2)}, u32[]{:S(2)}) collective-permute-start(f32[8,128,128]{2,1,0:T(8,128)} %turn.1.x), channel_id=1, source_target_pairs={{0,96},{1,97},{2,98},{3,99},{4,100},{5,101},{6,102},{7,103},{8,104... | collective-permute-start | bytes 1572872 | tf_op jit(solution)/shard_map/ppermute | solution.py:30
  11.0 0.8 broadcast_subtract_fusion
  11.7 0.1 copy.7
  11.9 0.7 dynamic-slice_bitcast_fusion
  12.6 0.8 %copy.6 = f32[64,4,8]{2,1,0:T(4,128)S(1)} copy(f32[64,4,8]{0,2,1:T(8,128)} %dynamic-slice_bitcast_fusion) | data formatting | bytes 16384 | tf_op jit(solution)/shard_map/broadcast_in_dim | solution.py:299
  13.4 0.7 sub.37
  14.1 0.7 dynamic_slice.7
  14.8 0.1 stack.59.info_ref
  14.9 0.9 %collective-permute-done.xx = f32[8,128,128]{2,1,0:T(8,128)S(1)} collective-permute-done((f32[8,128,128]{2,1,0:T(8,128)}, f32[8,128,128]{2,1,0:T(8,128)S(1)}, u32[]{:S(2)}, u32[]{:S(2)}) %collective-permute-start) | collective-permute-done | bytes 524320 | tf_op jit(solution)/shard_map/ppermute | solution.py:30
  15.8 3.0 %collective-permute-done.2.wm = f32[128,1024]{1,0:T(8,128)S(1)} collective-permute-done((f32[128,1024]{1,0:T(8,128)}, f32[128,1024]{1,0:T(8,128)S(1)}, u32[]{:S(2)}, u32[]{:S(2)}) %collective-permute-start.2) | collective-permute-done | bytes 524320 | tf_op jit(solution)/shard_map/ppermute | solution.py:30
  18.8 3.0 %collective-permute-done.1.wp = f32[128,1024]{1,0:T(8,128)S(1)} collective-permute-done((f32[128,1024]{1,0:T(8,128)}, f32[128,1024]{1,0:T(8,128)S(1)}, u32[]{:S(2)}, u32[]{:S(2)}) %collective-permute-start.1) | collective-permute-done | bytes 524320 | tf_op jit(solution)/shard_map/ppermute | solution.py:30
  21.8 0.3 broadcast_in_dim.10.rgap_ref
  22.2 2.8 %collective-permute-start.8 = (f32[8,128,128]{2,1,0:T(8,128)S(1)}, f32[8,128,128]{2,1,0:T(8,128)S(1)}, u32[]{:S(2)}, u32[]{:S(2)}) collective-permute-start(f32[8,128,128]{2,1,0:T(8,128)S(1)} %collective-permute-done.xx), channel_id=1, source_target_pairs={{0,96},{1,97},{2,98},{3,99},{4,100},{5,101},{6,102},{7,103},{8,104... | collective-permute-start | bytes 1572872 | tf_op jit(solution)/shard_map/ppermute | solution.py:30
  25.0 0.0 collective-permute-start.7
  25.0 0.0 collective-permute-done.3.xp
  25.0 0.0 collective-permute-done.4.xm
  25.0 0.0 copy-done.1
  25.0 2.5 %collective-permute-start.5 = (f32[128,1024]{1,0:T(8,128)S(1)}, f32[128,1024]{1,0:T(8,128)S(1)}, u32[]{:S(2)}, u32[]{:S(2)}) collective-permute-start(f32[128,1024]{1,0:T(8,128)S(1)} %copy-done.1), channel_id=1, source_target_pairs={{0,4},{1,5},{2,6},{3,7},{4,0},{5,1},{6,2},{7,3},{8,12},{9,13},{10,... | collective-permute-start | bytes 1572872 | tf_op jit(solution)/shard_map/ppermute | solution.py:30
  27.5 0.0 collective-permute-start.6
  27.5 1.1 %constant_dynamic-update-slice_fusion.5 = f32[8,768,128]{2,1,0:T(8,128)S(1)} fusion(f32[8,128,128]{2,1,0:T(8,128)} %turn.1.x), kind=kLoop, calls=%fused_computation.10 | loop fusion | bytes 1048576
  28.7 5.3 %collective-permute-done.8.xxm = f32[8,128,128]{2,1,0:T(8,128)S(1)} collective-permute-done((f32[8,128,128]{2,1,0:T(8,128)S(1)}, f32[8,128,128]{2,1,0:T(8,128)S(1)}, u32[]{:S(2)}, u32[]{:S(2)}) %collective-permute-start.8) | collective-permute-done | bytes 524320 | tf_op jit(solution)/shard_map/ppermute | solution.py:30
  34.0 3.1 %collective-permute-done.7.xxp = f32[8,128,128]{2,1,0:T(8,128)S(1)} collective-permute-done((f32[8,128,128]{2,1,0:T(8,128)S(1)}, f32[8,128,128]{2,1,0:T(8,128)S(1)}, u32[]{:S(2)}, u32[]{:S(2)}) %collective-permute-start.7) | collective-permute-done | bytes 524320 | tf_op jit(solution)/shard_map/ppermute | solution.py:30
  37.2 0.4 collective-permute-done.5.wx
  37.5 2.2 %collective-permute-done.6.w2 = f32[128,1024]{1,0:T(8,128)S(1)} collective-permute-done((f32[128,1024]{1,0:T(8,128)S(1)}, f32[128,1024]{1,0:T(8,128)S(1)}, u32[]{:S(2)}, u32[]{:S(2)}) %collective-permute-start.6) | collective-permute-done | bytes 524320 | tf_op jit(solution)/shard_map/ppermute | solution.py:30
  39.8 0.0 copy-start
  39.9 3.7 %collective-permute-start.9 = (f32[8,768,128]{2,1,0:T(8,128)S(1)}, f32[8,768,128]{2,1,0:T(8,128)S(1)}, u32[]{:S(2)}, u32[]{:S(2)}) collective-permute-start(f32[8,768,128]{2,1,0:T(8,128)S(1)} %constant_dynamic-update-slice_fusion), channel_id=1, source_target_pairs={{0,8},{1,9},{2,10},{3,11},{4,12},{5,13},{6,14},{7,15},{8,0},{9,1},... | collective-permute-start | bytes 9437192 | tf_op jit(solution)/shard_map/ppermute | solution.py:30
  43.7 2.7 %collective-permute-start.11 = (f32[8,128,128]{2,1,0:T(8,128)S(1)}, f32[8,128,128]{2,1,0:T(8,128)S(1)}, u32[]{:S(2)}, u32[]{:S(2)}) collective-permute-start(f32[8,128,128]{2,1,0:T(8,128)S(1)} %pad_maximum_fusion.2), channel_id=1, source_target_pairs={{0,96},{1,97},{2,98},{3,99},{4,100},{5,101},{6,102},{7,103},{8,104... | collective-permute-start | bytes 1572872 | tf_op jit(solution)/shard_map/ppermute | solution.py:30
  46.5 0.1 collective-permute-start.10
  46.6 0.6 collective-permute-start.14
  47.2 0.3 collective-permute-start.13
  47.5 1.4 %collective-permute-done.9.s1.s2 = f32[8,768,128]{2,1,0:T(8,128)S(1)} collective-permute-done((f32[8,768,128]{2,1,0:T(8,128)S(1)}, f32[8,768,128]{2,1,0:T(8,128)S(1)}, u32[]{:S(2)}, u32[]{:S(2)}) %collective-permute-start.9) | collective-permute-done | bytes 3145760 | tf_op jit(solution)/shard_map/ppermute | solution.py:30
  48.9 0.0 collective-permute-start.12
  48.9 0.0 copy-done
  48.9 2.4 %ready.1 = (bf16[512,512]{1,0:T(8,128)(2,1)S(1)}, bf16[512,512]{1,0:T(8,128)(2,1)S(1)}, bf16[512,512]{1,0:T(8,128)(2,1)S(1)}, bf16[512,512]{1,0:T(8,128)(2,1)S(1...) custom-call(s32[14]{0:T(128)S(1)} %stack.59.info_ref, f32[8,128,128]{2,1,0:T(8,128)S(1)} %copy-done, ...), custom_call_target="tpu_custom_call" | custom-call | flops 1048576 | bytes 10485760 | tf_op jit(solution)/shard_map/ready/pallas_call | solution.py:124
  51.3 8.6 %early.1 = (f32[3,512,1024]{2,1,0:T(8,128)S(1)}, bf16[2,512,512]{2,1,0:T(8,128)(2,1)S(1)}, bf16[2,512,512]{2,1,0:T(8,128)(2,1)S(1)}, bf16[512,1024]{1,0:T(8,128)(2,1)S(1)}, bf16[512,1024]{1,0:T(8,128)(2,1)S(1)}) custom-call(s32[14]{0:T(128)S(1)} %stack.59.info_ref, f32[8,768,128]{2,1,0:T(8,128)S(1)} %collective-permute-done.9.s1.s2, ...), custom_call_target="tpu_custom_call" | custom-call | flops 4831838208 | bytes 20971520 | tf_op jit(solution)/shard_map/early/pallas_call | solution.py:160
  59.8 0.0 collective-permute-done.11.down
  59.9 1.1 %collective-permute-done.10.up = f32[8,128,128]{2,1,0:T(8,128)S(1)} collective-permute-done((f32[8,128,128]{2,1,0:T(8,128)S(1)}, f32[8,128,128]{2,1,0:T(8,128)S(1)}, u32[]{:S(2)}, u32[]{:S(2)}) %collective-permute-start.10) | collective-permute-done | bytes 524320 | tf_op jit(solution)/shard_map/ppermute | solution.py:30
  61.0 0.4 collective-permute-done.14.wx2
  61.4 0.0 collective-permute-done.13.wxm
  61.4 1.8 %collective-permute-done.12.wxp = f32[128,1024]{1,0:T(8,128)S(1)} collective-permute-done((f32[128,1024]{1,0:T(8,128)S(1)}, f32[128,1024]{1,0:T(8,128)S(1)}, u32[]{:S(2)}, u32[]{:S(2)}) %collective-permute-start.12) | collective-permute-done | bytes 524320 | tf_op jit(solution)/shard_map/ppermute | solution.py:30
  63.2 0.1 pad_maximum_fusion
  63.3 1.5 %collective-permute-start.15 = (f32[8,256,128]{2,1,0:T(8,128)S(1)}, f32[8,256,128]{2,1,0:T(8,128)S(1)}, u32[]{:S(2)}, u32[]{:S(2)}) collective-permute-start(f32[8,256,128]{2,1,0:T(8,128)S(1)} %pad_maximum_fusion), channel_id=1, source_target_pairs={{0,8},{1,9},{2,10},{3,11},{4,12},{5,13},{6,14},{7,15},{8,0},{9,1},... | collective-permute-start | bytes 3145736 | tf_op jit(solution)/shard_map/ppermute | solution.py:30
  64.8 7.5 %late.1 = (f32[64,4,8,1024]{3,2,1,0:T(8,128)}, bf16[512,1024]{1,0:T(8,128)(2,1)S(1)}, bf16[512,1024]{1,0:T(8,128)(2,1)S(1)}) custom-call(s32[14]{0:T(128)S(1)} %stack.59.info_ref, f32[3,512,1024]{2,1,0:T(8,128)S(1)} %get-tuple-element.54.part_ref, bf16[512,512]{1,0:T(8,128)(2,1)S(1)} %get-tuple-element.55.high2, ...), custom_call_target="tpu_custom_call" | custom-call | flops 4831838208 | bytes 25165824 | tf_op jit(solution)/shard_map/late/pallas_call | solution.py:210
  72.3 0.0 collective-permute-done.15.s3
  72.3 6.6 %last.1 = f32[64,4,8,1024]{3,2,1,0:T(8,128)} custom-call(s32[14]{0:T(128)S(1)} %stack.59.info_ref, f32[64,4,8,1024]{3,2,1,0:T(8,128)} %get-tuple-element.66.rest_ref, f32[8,128,128]{2,1,0:T(8,128)S(1)} %collective-permute-done.10.up, f32[8,128,128]{2,1,0:T(8,128)S(1)} %collective-permute-done.11.down, ...), custom_call_target="tpu_custom_call", output_to_operand_aliasing={{}: (1, {})} | custom-call | flops 3221225472 | bytes 8388608 | tf_op jit(solution)/shard_map/last/pallas_call | solution.py:266
  (11 shorter events, 0.3 us)
Async XLA Ops:
  0.0 25.0 %copy-start.1 = (f32[128,1024]{1,0:T(8,128)S(1)}, f32[128,1024]{1,0:T(8,128)}, u32[]{:S(2)}) copy-start(f32[128,1024]{1,0:T(8,128)} %w.1) | copy-start | bytes 1572868
  2.4 13.4 %collective-permute-start = (f32[8,128,128]{2,1,0:T(8,128)}, f32[8,128,128]{2,1,0:T(8,128)S(1)}, u32[]{:S(2)}, u32[]{:S(2)}) collective-permute-start(f32[8,128,128]{2,1,0:T(8,128)} %turn.1.x), channel_id=1, source_target_pairs={{0,16},{1,17},{2,18},{3,19},{4,20},{5,21},{6,22},{7,23},{8,24},{9,... | collective-permute-start | bytes 1572872 | tf_op jit(solution)/shard_map/ppermute | solution.py:30
  4.5 14.3 %collective-permute-start.2 = (f32[128,1024]{1,0:T(8,128)}, f32[128,1024]{1,0:T(8,128)S(1)}, u32[]{:S(2)}, u32[]{:S(2)}) collective-permute-start(f32[128,1024]{1,0:T(8,128)} %w.1), channel_id=1, source_target_pairs={{0,3},{1,0},{2,1},{3,2},{4,7},{5,4},{6,5},{7,6},{8,11},{9,8},{10,9... | collective-permute-start | bytes 1572872 | tf_op jit(solution)/shard_map/ppermute | solution.py:30
  8.2 13.6 %collective-permute-start.1 = (f32[128,1024]{1,0:T(8,128)}, f32[128,1024]{1,0:T(8,128)S(1)}, u32[]{:S(2)}, u32[]{:S(2)}) collective-permute-start(f32[128,1024]{1,0:T(8,128)} %w.1), channel_id=1, source_target_pairs={{0,1},{1,2},{2,3},{3,0},{4,5},{5,6},{6,7},{7,4},{8,9},{9,10},{10,1... | collective-permute-start | bytes 1572872 | tf_op jit(solution)/shard_map/ppermute | solution.py:30
  8.2 16.7 %collective-permute-start.3 = (f32[8,128,128]{2,1,0:T(8,128)}, f32[8,128,128]{2,1,0:T(8,128)S(1)}, u32[]{:S(2)}, u32[]{:S(2)}) collective-permute-start(f32[8,128,128]{2,1,0:T(8,128)} %turn.1.x), channel_id=1, source_target_pairs={{0,32},{1,33},{2,34},{3,35},{4,36},{5,37},{6,38},{7,39},{8,40},{9,... | collective-permute-start | bytes 1572872 | tf_op jit(solution)/shard_map/ppermute | solution.py:30
  9.5 15.4 %collective-permute-start.4 = (f32[8,128,128]{2,1,0:T(8,128)}, f32[8,128,128]{2,1,0:T(8,128)S(1)}, u32[]{:S(2)}, u32[]{:S(2)}) collective-permute-start(f32[8,128,128]{2,1,0:T(8,128)} %turn.1.x), channel_id=1, source_target_pairs={{0,96},{1,97},{2,98},{3,99},{4,100},{5,101},{6,102},{7,103},{8,104... | collective-permute-start | bytes 1572872 | tf_op jit(solution)/shard_map/ppermute | solution.py:30
  22.2 11.9 %collective-permute-start.8 = (f32[8,128,128]{2,1,0:T(8,128)S(1)}, f32[8,128,128]{2,1,0:T(8,128)S(1)}, u32[]{:S(2)}, u32[]{:S(2)}) collective-permute-start(f32[8,128,128]{2,1,0:T(8,128)S(1)} %collective-permute-done.xx), channel_id=1, source_target_pairs={{0,96},{1,97},{2,98},{3,99},{4,100},{5,101},{6,102},{7,103},{8,104... | collective-permute-start | bytes 1572872 | tf_op jit(solution)/shard_map/ppermute | solution.py:30
  25.0 12.2 %collective-permute-start.7 = (f32[8,128,128]{2,1,0:T(8,128)S(1)}, f32[8,128,128]{2,1,0:T(8,128)S(1)}, u32[]{:S(2)}, u32[]{:S(2)}) collective-permute-start(f32[8,128,128]{2,1,0:T(8,128)S(1)} %collective-permute-done.xx), channel_id=1, source_target_pairs={{0,32},{1,33},{2,34},{3,35},{4,36},{5,37},{6,38},{7,39},{8,40},{9,... | collective-permute-start | bytes 1572872 | tf_op jit(solution)/shard_map/ppermute | solution.py:30
  25.0 12.6 %collective-permute-start.5 = (f32[128,1024]{1,0:T(8,128)S(1)}, f32[128,1024]{1,0:T(8,128)S(1)}, u32[]{:S(2)}, u32[]{:S(2)}) collective-permute-start(f32[128,1024]{1,0:T(8,128)S(1)} %copy-done.1), channel_id=1, source_target_pairs={{0,4},{1,5},{2,6},{3,7},{4,0},{5,1},{6,2},{7,3},{8,12},{9,13},{10,... | collective-permute-start | bytes 1572872 | tf_op jit(solution)/shard_map/ppermute | solution.py:30
  27.5 12.2 %collective-permute-start.6 = (f32[128,1024]{1,0:T(8,128)S(1)}, f32[128,1024]{1,0:T(8,128)S(1)}, u32[]{:S(2)}, u32[]{:S(2)}) collective-permute-start(f32[128,1024]{1,0:T(8,128)S(1)} %copy-done.1), channel_id=1, source_target_pairs={{0,2},{1,3},{2,0},{3,1},{4,6},{5,7},{6,4},{7,5},{8,10},{9,11},{10,... | collective-permute-start | bytes 1572872 | tf_op jit(solution)/shard_map/ppermute | solution.py:30
  39.8 9.1 %copy-start = (f32[8,128,128]{2,1,0:T(8,128)S(1)}, f32[8,128,128]{2,1,0:T(8,128)}, u32[]{:S(2)}) copy-start(f32[8,128,128]{2,1,0:T(8,128)} %turn.1.x) | copy-start | bytes 1572868
  39.9 9.0 %collective-permute-start.9 = (f32[8,768,128]{2,1,0:T(8,128)S(1)}, f32[8,768,128]{2,1,0:T(8,128)S(1)}, u32[]{:S(2)}, u32[]{:S(2)}) collective-permute-start(f32[8,768,128]{2,1,0:T(8,128)S(1)} %constant_dynamic-update-slice_fusion), channel_id=1, source_target_pairs={{0,8},{1,9},{2,10},{3,11},{4,12},{5,13},{6,14},{7,15},{8,0},{9,1},... | collective-permute-start | bytes 9437192 | tf_op jit(solution)/shard_map/ppermute | solution.py:30
  43.7 16.1 %collective-permute-start.11 = (f32[8,128,128]{2,1,0:T(8,128)S(1)}, f32[8,128,128]{2,1,0:T(8,128)S(1)}, u32[]{:S(2)}, u32[]{:S(2)}) collective-permute-start(f32[8,128,128]{2,1,0:T(8,128)S(1)} %pad_maximum_fusion.2), channel_id=1, source_target_pairs={{0,96},{1,97},{2,98},{3,99},{4,100},{5,101},{6,102},{7,103},{8,104... | collective-permute-start | bytes 1572872 | tf_op jit(solution)/shard_map/ppermute | solution.py:30
  46.5 14.5 %collective-permute-start.10 = (f32[8,128,128]{2,1,0:T(8,128)S(1)}, f32[8,128,128]{2,1,0:T(8,128)S(1)}, u32[]{:S(2)}, u32[]{:S(2)}) collective-permute-start(f32[8,128,128]{2,1,0:T(8,128)S(1)} %pad_maximum_fusion.1), channel_id=1, source_target_pairs={{0,32},{1,33},{2,34},{3,35},{4,36},{5,37},{6,38},{7,39},{8,40},{9,... | collective-permute-start | bytes 1572872 | tf_op jit(solution)/shard_map/ppermute | solution.py:30
  46.6 14.8 %collective-permute-start.14 = (f32[128,1024]{1,0:T(8,128)S(1)}, f32[128,1024]{1,0:T(8,128)S(1)}, u32[]{:S(2)}, u32[]{:S(2)}) collective-permute-start(f32[128,1024]{1,0:T(8,128)S(1)} %collective-permute-done.6.w2), channel_id=1, source_target_pairs={{0,4},{1,5},{2,6},{3,7},{4,0},{5,1},{6,2},{7,3},{8,12},{9,13},{10,... | collective-permute-start | bytes 1572872 | tf_op jit(solution)/shard_map/ppermute | solution.py:30
  47.2 14.2 %collective-permute-start.13 = (f32[128,1024]{1,0:T(8,128)S(1)}, f32[128,1024]{1,0:T(8,128)S(1)}, u32[]{:S(2)}, u32[]{:S(2)}) collective-permute-start(f32[128,1024]{1,0:T(8,128)S(1)} %collective-permute-done.5.wx), channel_id=1, source_target_pairs={{0,3},{1,0},{2,1},{3,2},{4,7},{5,4},{6,5},{7,6},{8,11},{9,8},{10,9... | collective-permute-start | bytes 1572872 | tf_op jit(solution)/shard_map/ppermute | solution.py:30
  48.9 14.3 %collective-permute-start.12 = (f32[128,1024]{1,0:T(8,128)S(1)}, f32[128,1024]{1,0:T(8,128)S(1)}, u32[]{:S(2)}, u32[]{:S(2)}) collective-permute-start(f32[128,1024]{1,0:T(8,128)S(1)} %collective-permute-done.5.wx), channel_id=1, source_target_pairs={{0,1},{1,2},{2,3},{3,0},{4,5},{5,6},{6,7},{7,4},{8,9},{9,10},{10,1... | collective-permute-start | bytes 1572872 | tf_op jit(solution)/shard_map/ppermute | solution.py:30
  63.3 9.0 %collective-permute-start.15 = (f32[8,256,128]{2,1,0:T(8,128)S(1)}, f32[8,256,128]{2,1,0:T(8,128)S(1)}, u32[]{:S(2)}, u32[]{:S(2)}) collective-permute-start(f32[8,256,128]{2,1,0:T(8,128)S(1)} %pad_maximum_fusion), channel_id=1, source_target_pairs={{0,8},{1,9},{2,10},{3,11},{4,12},{5,13},{6,14},{7,15},{8,0},{9,1},... | collective-permute-start | bytes 3145736 | tf_op jit(solution)/shard_map/ppermute | solution.py:30

commit v8 on v7

--- a/solution.py
+++ b/solution.py
@@ -306,9 +306,9 @@
 
     wp, wm = hop(w, z=1), hop(w, z=3)
     xp, xm, xx = hop(x, y=1), hop(x, y=3), hop(x, xl=1)
-    xx, wp, wm, info, rgap, cgap = lax.optimization_barrier((xx, wp, wm, info, rgap, cgap))
+    xx, info, rgap, cgap = lax.optimization_barrier((xx, info, rgap, cgap))
     xxp, xxm = hop(xx, y=1), hop(xx, y=3)
-    w2, wx = hop(after(w, wp, wm, xp), z=2), hop(after(w, xx, xm), xh=1)
+    w2, wx = hop(after(w, wp, wm, xp, xm), z=2), hop(after(w, xx, xp, xm, wp, wm), xh=1)
     xxp, xxm = lax.optimization_barrier((xxp, xxm))
     wx, w2, xxp, xxm = lax.optimization_barrier((wx, w2, xxp, xxm))
     s2 = hop(join(x, xx, xp, xxp, xm, xxm), core=1)

time: 79.3 us -> 77.6 us (0.979)
  waiting for transfers between devices: 22.7 us -> 17.5 us
  starting transfers between devices: 22.8 us -> 26.3 us
    ppermute x16, waiting for transfers between devices: 22.7 us -> 17.5 us  [hop(): return lax.ppermute(value, AXES, pairs)]
    ppermute x16, starting transfers between devices: 22.8 us -> 26.3 us  [hop(): return lax.ppermute(value, AXES, pairs)]
  transfers between devices with their start and end apart: 16 -> 16, of which waited for: 11 -> 10; matrix products, arithmetic and copies ran while one was open for 7% -> 7% of each run, Pallas kernels for 23% -> 24%
where the time goes in v8:
time: 77.6 us; the launch traced here: 77.3 us
  Pallas kernels  27.5 us (35%)
  starting transfers between devices  26.3 us (34%)
  waiting for transfers between devices  17.5 us (23%)
  local copies, waits for them, and re-layouts  4.8 us (6%)
  other arithmetic  0.91 us (1%)
    ppermute x16, starting transfers between devices, hop(): return lax.ppermute(value, AXES, pairs)  26.3 us
    ppermute x16, waiting for transfers between devices, hop(): return lax.ppermute(value, AXES, pairs)  17.5 us
    pallas_call x1, Pallas kernels, early(): pl.pallas_call(early_kernel, out_shape=[pltpu.VMEM((3, ROWS, columns), f3...  8.58 us
    pallas_call x1, Pallas kernels, late(): pl.pallas_call(late_kernel, out_shape=[jax.ShapeDtypeStruct((virtuals, 4,...  7.53 us
    pallas_call x1, Pallas kernels, last(): pl.pallas_call(last_kernel, out_shape=jax.ShapeDtypeStruct((virtuals, 4,...  6.55 us
    pallas_call x1, Pallas kernels, turn(): pl.pallas_call(turn_kernel, out_shape=jax.ShapeDtypeStruct((depth // 128,...  2.43 us
    pallas_call x1, Pallas kernels, ready(): pl.pallas_call(ready_kernel, out_shape=[pltpu.VMEM((ROWS, DEEP), bf16)] *...  2.37 us
    broadcast_in_dim x3, local copies, waits for them, and re-layouts, body(): jnp.broadcast_to(row_gap.reshape(virtuals, 4, 8, 1), (virtuals, 4, 8, 128))  1.83 us
  transfers between devices with their start and end apart: 16, of which 10 were waited for; matrix products, arithmetic and copies ran while one was open for 7% of the time, Pallas kernels for 24%

profile of v8, /device:TPU:1, one launch (start us, length us, event | category | flops | bytes accessed | tf_op | source)
XLA Modules:
  0.0 77.3 jit_solution(14434439592625757071)
XLA Ops:
  0.0 0.0 copy-start.1
  0.0 2.4 %turn.1.x = f32[8,128,128]{2,1,0:T(8,128)} custom-call(f32[2,1024,64]{2,1,0:T(8,128)} %bitcast.23), custom_call_target="tpu_custom_call" | custom-call | flops 1048576 | bytes 2097152 | tf_op jit(solution)/shard_map/turn/pallas_call | solution.py:51
  2.4 2.0 %collective-permute-start = (f32[8,128,128]{2,1,0:T(8,128)}, f32[8,128,128]{2,1,0:T(8,128)S(1)}, u32[]{:S(2)}, u32[]{:S(2)}) collective-permute-start(f32[8,128,128]{2,1,0:T(8,128)} %turn.1.x), channel_id=1, source_target_pairs={{0,16},{1,17},{2,18},{3,19},{4,20},{5,21},{6,22},{7,23},{8,24},{9,... | collective-permute-start | bytes 1572872 | tf_op jit(solution)/shard_map/ppermute | solution.py:30
  4.5 2.7 %collective-permute-start.2 = (f32[8,128,128]{2,1,0:T(8,128)}, f32[8,128,128]{2,1,0:T(8,128)S(1)}, u32[]{:S(2)}, u32[]{:S(2)}) collective-permute-start(f32[8,128,128]{2,1,0:T(8,128)} %turn.1.x), channel_id=1, source_target_pairs={{0,96},{1,97},{2,98},{3,99},{4,100},{5,101},{6,102},{7,103},{8,104... | collective-permute-start | bytes 1572872 | tf_op jit(solution)/shard_map/ppermute | solution.py:30
  7.2 0.0 collective-permute-start.1
  7.2 3.8 %collective-permute-start.4 = (f32[128,1024]{1,0:T(8,128)}, f32[128,1024]{1,0:T(8,128)S(1)}, u32[]{:S(2)}, u32[]{:S(2)}) collective-permute-start(f32[128,1024]{1,0:T(8,128)} %w.1), channel_id=1, source_target_pairs={{0,3},{1,0},{2,1},{3,2},{4,7},{5,4},{6,5},{7,6},{8,11},{9,8},{10,9... | collective-permute-start | bytes 1572872 | tf_op jit(solution)/shard_map/ppermute | solution.py:30
  11.0 0.0 collective-permute-start.3
  11.0 0.8 broadcast_subtract_fusion
  11.7 0.1 copy.7
  11.9 0.7 dynamic-slice_bitcast_fusion
  12.6 0.8 %copy.6 = f32[64,4,8]{2,1,0:T(4,128)S(1)} copy(f32[64,4,8]{0,2,1:T(8,128)} %dynamic-slice_bitcast_fusion) | data formatting | bytes 16384 | tf_op jit(solution)/shard_map/broadcast_in_dim | solution.py:299
  13.4 0.7 sub.37
  14.1 0.7 dynamic_slice.7
  14.8 0.1 stack.59.info_ref
  14.9 0.9 %collective-permute-done.xx = f32[8,128,128]{2,1,0:T(8,128)S(1)} collective-permute-done((f32[8,128,128]{2,1,0:T(8,128)}, f32[8,128,128]{2,1,0:T(8,128)S(1)}, u32[]{:S(2)}, u32[]{:S(2)}) %collective-permute-start) | collective-permute-done | bytes 524320 | tf_op jit(solution)/shard_map/ppermute | solution.py:30
  15.8 0.3 broadcast_in_dim.10.rgap_ref
  16.2 3.2 %collective-permute-start.8 = (f32[8,128,128]{2,1,0:T(8,128)S(1)}, f32[8,128,128]{2,1,0:T(8,128)S(1)}, u32[]{:S(2)}, u32[]{:S(2)}) collective-permute-start(f32[8,128,128]{2,1,0:T(8,128)S(1)} %collective-permute-done.xx), channel_id=1, source_target_pairs={{0,96},{1,97},{2,98},{3,99},{4,100},{5,101},{6,102},{7,103},{8,104... | collective-permute-start | bytes 1572872 | tf_op jit(solution)/shard_map/ppermute | solution.py:30
  19.4 0.0 collective-permute-done.2.xm
  19.4 0.0 collective-permute-start.7
  19.4 1.4 %collective-permute-done.1.xp = f32[8,128,128]{2,1,0:T(8,128)S(1)} collective-permute-done((f32[8,128,128]{2,1,0:T(8,128)}, f32[8,128,128]{2,1,0:T(8,128)S(1)}, u32[]{:S(2)}, u32[]{:S(2)}) %collective-permute-start.1) | collective-permute-done | bytes 524320 | tf_op jit(solution)/shard_map/ppermute | solution.py:30
  20.8 0.5 collective-permute-done.4.wm
  21.3 3.0 %collective-permute-done.3.wp = f32[128,1024]{1,0:T(8,128)S(1)} collective-permute-done((f32[128,1024]{1,0:T(8,128)}, f32[128,1024]{1,0:T(8,128)S(1)}, u32[]{:S(2)}, u32[]{:S(2)}) %collective-permute-start.3) | collective-permute-done | bytes 524320 | tf_op jit(solution)/shard_map/ppermute | solution.py:30
  24.3 0.0 copy-done.1
  24.3 0.2 collective-permute-start.6
  24.5 2.5 %collective-permute-start.5 = (f32[128,1024]{1,0:T(8,128)S(1)}, f32[128,1024]{1,0:T(8,128)S(1)}, u32[]{:S(2)}, u32[]{:S(2)}) collective-permute-start(f32[128,1024]{1,0:T(8,128)S(1)} %copy-done.1), channel_id=1, source_target_pairs={{0,4},{1,5},{2,6},{3,7},{4,0},{5,1},{6,2},{7,3},{8,12},{9,13},{10,... | collective-permute-start | bytes 1572872 | tf_op jit(solution)/shard_map/ppermute | solution.py:30
  26.9 1.1 %constant_dynamic-update-slice_fusion.5 = f32[8,768,128]{2,1,0:T(8,128)S(1)} fusion(f32[8,128,128]{2,1,0:T(8,128)} %turn.1.x), kind=kLoop, calls=%fused_computation.10 | loop fusion | bytes 1048576
  28.1 1.0 %collective-permute-done.8.xxm = f32[8,128,128]{2,1,0:T(8,128)S(1)} collective-permute-done((f32[8,128,128]{2,1,0:T(8,128)S(1)}, f32[8,128,128]{2,1,0:T(8,128)S(1)}, u32[]{:S(2)}, u32[]{:S(2)}) %collective-permute-start.8) | collective-permute-done | bytes 524320 | tf_op jit(solution)/shard_map/ppermute | solution.py:30
  29.1 3.1 %collective-permute-done.7.xxp = f32[8,128,128]{2,1,0:T(8,128)S(1)} collective-permute-done((f32[8,128,128]{2,1,0:T(8,128)S(1)}, f32[8,128,128]{2,1,0:T(8,128)S(1)}, u32[]{:S(2)}, u32[]{:S(2)}) %collective-permute-start.7) | collective-permute-done | bytes 524320 | tf_op jit(solution)/shard_map/ppermute | solution.py:30
  32.2 4.6 %collective-permute-done.6.w2 = f32[128,1024]{1,0:T(8,128)S(1)} collective-permute-done((f32[128,1024]{1,0:T(8,128)S(1)}, f32[128,1024]{1,0:T(8,128)S(1)}, u32[]{:S(2)}, u32[]{:S(2)}) %collective-permute-start.6) | collective-permute-done | bytes 524320 | tf_op jit(solution)/shard_map/ppermute | solution.py:30
  36.8 0.2 collective-permute-done.5.wx
  37.0 0.0 copy-start
  37.1 3.4 %collective-permute-start.9 = (f32[8,768,128]{2,1,0:T(8,128)S(1)}, f32[8,768,128]{2,1,0:T(8,128)S(1)}, u32[]{:S(2)}, u32[]{:S(2)}) collective-permute-start(f32[8,768,128]{2,1,0:T(8,128)S(1)} %constant_dynamic-update-slice_fusion), channel_id=1, source_target_pairs={{0,8},{1,9},{2,10},{3,11},{4,12},{5,13},{6,14},{7,15},{8,0},{9,1},... | collective-permute-start | bytes 9437192 | tf_op jit(solution)/shard_map/ppermute | solution.py:30
  40.7 2.3 %collective-permute-start.11 = (f32[8,128,128]{2,1,0:T(8,128)S(1)}, f32[8,128,128]{2,1,0:T(8,128)S(1)}, u32[]{:S(2)}, u32[]{:S(2)}) collective-permute-start(f32[8,128,128]{2,1,0:T(8,128)S(1)} %pad_maximum_fusion.2), channel_id=1, source_target_pairs={{0,96},{1,97},{2,98},{3,99},{4,100},{5,101},{6,102},{7,103},{8,104... | collective-permute-start | bytes 1572872 | tf_op jit(solution)/shard_map/ppermute | solution.py:30
  43.0 0.1 collective-permute-start.10
  43.1 2.5 %collective-permute-start.14 = (f32[128,1024]{1,0:T(8,128)S(1)}, f32[128,1024]{1,0:T(8,128)S(1)}, u32[]{:S(2)}, u32[]{:S(2)}) collective-permute-start(f32[128,1024]{1,0:T(8,128)S(1)} %collective-permute-done.6.w2), channel_id=1, source_target_pairs={{0,4},{1,5},{2,6},{3,7},{4,0},{5,1},{6,2},{7,3},{8,12},{9,13},{10,... | collective-permute-start | bytes 1572872 | tf_op jit(solution)/shard_map/ppermute | solution.py:30
  45.6 1.5 %collective-permute-start.13 = (f32[128,1024]{1,0:T(8,128)S(1)}, f32[128,1024]{1,0:T(8,128)S(1)}, u32[]{:S(2)}, u32[]{:S(2)}) collective-permute-start(f32[128,1024]{1,0:T(8,128)S(1)} %collective-permute-done.5.wx), channel_id=1, source_target_pairs={{0,3},{1,0},{2,1},{3,2},{4,7},{5,4},{6,5},{7,6},{8,11},{9,8},{10,9... | collective-permute-start | bytes 1572872 | tf_op jit(solution)/shard_map/ppermute | solution.py:30
  47.1 0.0 collective-permute-done.9.s1.s2
  47.1 0.0 collective-permute-start.12
  47.1 0.0 copy-done
  47.1 2.4 %ready.1 = (bf16[512,512]{1,0:T(8,128)(2,1)S(1)}, bf16[512,512]{1,0:T(8,128)(2,1)S(1)}, bf16[512,512]{1,0:T(8,128)(2,1)S(1)}, bf16[512,512]{1,0:T(8,128)(2,1)S(1...) custom-call(s32[14]{0:T(128)S(1)} %stack.59.info_ref, f32[8,128,128]{2,1,0:T(8,128)S(1)} %copy-done, ...), custom_call_target="tpu_custom_call" | custom-call | flops 1048576 | bytes 10485760 | tf_op jit(solution)/shard_map/ready/pallas_call | solution.py:124
  49.5 8.6 %early.1 = (f32[3,512,1024]{2,1,0:T(8,128)S(1)}, bf16[2,512,512]{2,1,0:T(8,128)(2,1)S(1)}, bf16[2,512,512]{2,1,0:T(8,128)(2,1)S(1)}, bf16[512,1024]{1,0:T(8,128)(2,1)S(1)}, bf16[512,1024]{1,0:T(8,128)(2,1)S(1)}) custom-call(s32[14]{0:T(128)S(1)} %stack.59.info_ref, f32[8,768,128]{2,1,0:T(8,128)S(1)} %collective-permute-done.9.s1.s2, ...), custom_call_target="tpu_custom_call" | custom-call | flops 4831838208 | bytes 20971520 | tf_op jit(solution)/shard_map/early/pallas_call | solution.py:160
  58.1 0.0 collective-permute-done.11.down
  58.1 0.0 collective-permute-done.10.up
  58.1 0.0 collective-permute-done.14.wx2
  58.1 0.4 collective-permute-done.13.wxm
  58.5 2.4 %collective-permute-done.12.wxp = f32[128,1024]{1,0:T(8,128)S(1)} collective-permute-done((f32[128,1024]{1,0:T(8,128)S(1)}, f32[128,1024]{1,0:T(8,128)S(1)}, u32[]{:S(2)}, u32[]{:S(2)}) %collective-permute-start.12) | collective-permute-done | bytes 524320 | tf_op jit(solution)/shard_map/ppermute | solution.py:30
  60.9 0.1 pad_maximum_fusion
  61.0 2.1 %collective-permute-start.15 = (f32[8,256,128]{2,1,0:T(8,128)S(1)}, f32[8,256,128]{2,1,0:T(8,128)S(1)}, u32[]{:S(2)}, u32[]{:S(2)}) collective-permute-start(f32[8,256,128]{2,1,0:T(8,128)S(1)} %pad_maximum_fusion), channel_id=1, source_target_pairs={{0,8},{1,9},{2,10},{3,11},{4,12},{5,13},{6,14},{7,15},{8,0},{9,1},... | collective-permute-start | bytes 3145736 | tf_op jit(solution)/shard_map/ppermute | solution.py:30
  63.0 7.5 %late.1 = (f32[64,4,8,1024]{3,2,1,0:T(8,128)}, bf16[512,1024]{1,0:T(8,128)(2,1)S(1)}, bf16[512,1024]{1,0:T(8,128)(2,1)S(1)}) custom-call(s32[14]{0:T(128)S(1)} %stack.59.info_ref, f32[3,512,1024]{2,1,0:T(8,128)S(1)} %get-tuple-element.50.part_ref, bf16[512,512]{1,0:T(8,128)(2,1)S(1)} %get-tuple-element.51.high2, ...), custom_call_target="tpu_custom_call" | custom-call | flops 4831838208 | bytes 25165824 | tf_op jit(solution)/shard_map/late/pallas_call | solution.py:210
  70.6 0.0 collective-permute-done.15.s3
  70.6 6.6 %last.1 = f32[64,4,8,1024]{3,2,1,0:T(8,128)} custom-call(s32[14]{0:T(128)S(1)} %stack.59.info_ref, f32[64,4,8,1024]{3,2,1,0:T(8,128)} %get-tuple-element.62.rest_ref, f32[8,128,128]{2,1,0:T(8,128)S(1)} %collective-permute-done.10.up, f32[8,128,128]{2,1,0:T(8,128)S(1)} %collective-permute-done.11.down, ...), custom_call_target="tpu_custom_call", output_to_operand_aliasing={{}: (1, {})} | custom-call | flops 3221225472 | bytes 8388608 | tf_op jit(solution)/shard_map/last/pallas_call | solution.py:266
  (11 shorter events, 0.3 us)
Async XLA Ops:
  0.0 24.3 %copy-start.1 = (f32[128,1024]{1,0:T(8,128)S(1)}, f32[128,1024]{1,0:T(8,128)}, u32[]{:S(2)}) copy-start(f32[128,1024]{1,0:T(8,128)} %w.1) | copy-start | bytes 1572868
  2.4 13.4 %collective-permute-start = (f32[8,128,128]{2,1,0:T(8,128)}, f32[8,128,128]{2,1,0:T(8,128)S(1)}, u32[]{:S(2)}, u32[]{:S(2)}) collective-permute-start(f32[8,128,128]{2,1,0:T(8,128)} %turn.1.x), channel_id=1, source_target_pairs={{0,16},{1,17},{2,18},{3,19},{4,20},{5,21},{6,22},{7,23},{8,24},{9,... | collective-permute-start | bytes 1572872 | tf_op jit(solution)/shard_map/ppermute | solution.py:30
  4.5 14.9 %collective-permute-start.2 = (f32[8,128,128]{2,1,0:T(8,128)}, f32[8,128,128]{2,1,0:T(8,128)S(1)}, u32[]{:S(2)}, u32[]{:S(2)}) collective-permute-start(f32[8,128,128]{2,1,0:T(8,128)} %turn.1.x), channel_id=1, source_target_pairs={{0,96},{1,97},{2,98},{3,99},{4,100},{5,101},{6,102},{7,103},{8,104... | collective-permute-start | bytes 1572872 | tf_op jit(solution)/shard_map/ppermute | solution.py:30
  7.2 13.6 %collective-permute-start.1 = (f32[8,128,128]{2,1,0:T(8,128)}, f32[8,128,128]{2,1,0:T(8,128)S(1)}, u32[]{:S(2)}, u32[]{:S(2)}) collective-permute-start(f32[8,128,128]{2,1,0:T(8,128)} %turn.1.x), channel_id=1, source_target_pairs={{0,32},{1,33},{2,34},{3,35},{4,36},{5,37},{6,38},{7,39},{8,40},{9,... | collective-permute-start | bytes 1572872 | tf_op jit(solution)/shard_map/ppermute | solution.py:30
  7.2 14.1 %collective-permute-start.4 = (f32[128,1024]{1,0:T(8,128)}, f32[128,1024]{1,0:T(8,128)S(1)}, u32[]{:S(2)}, u32[]{:S(2)}) collective-permute-start(f32[128,1024]{1,0:T(8,128)} %w.1), channel_id=1, source_target_pairs={{0,3},{1,0},{2,1},{3,2},{4,7},{5,4},{6,5},{7,6},{8,11},{9,8},{10,9... | collective-permute-start | bytes 1572872 | tf_op jit(solution)/shard_map/ppermute | solution.py:30
  11.0 13.3 %collective-permute-start.3 = (f32[128,1024]{1,0:T(8,128)}, f32[128,1024]{1,0:T(8,128)S(1)}, u32[]{:S(2)}, u32[]{:S(2)}) collective-permute-start(f32[128,1024]{1,0:T(8,128)} %w.1), channel_id=1, source_target_pairs={{0,1},{1,2},{2,3},{3,0},{4,5},{5,6},{6,7},{7,4},{8,9},{9,10},{10,1... | collective-permute-start | bytes 1572872 | tf_op jit(solution)/shard_map/ppermute | solution.py:30
  16.2 12.9 %collective-permute-start.8 = (f32[8,128,128]{2,1,0:T(8,128)S(1)}, f32[8,128,128]{2,1,0:T(8,128)S(1)}, u32[]{:S(2)}, u32[]{:S(2)}) collective-permute-start(f32[8,128,128]{2,1,0:T(8,128)S(1)} %collective-permute-done.xx), channel_id=1, source_target_pairs={{0,96},{1,97},{2,98},{3,99},{4,100},{5,101},{6,102},{7,103},{8,104... | collective-permute-start | bytes 1572872 | tf_op jit(solution)/shard_map/ppermute | solution.py:30
  19.4 12.8 %collective-permute-start.7 = (f32[8,128,128]{2,1,0:T(8,128)S(1)}, f32[8,128,128]{2,1,0:T(8,128)S(1)}, u32[]{:S(2)}, u32[]{:S(2)}) collective-permute-start(f32[8,128,128]{2,1,0:T(8,128)S(1)} %collective-permute-done.xx), channel_id=1, source_target_pairs={{0,32},{1,33},{2,34},{3,35},{4,36},{5,37},{6,38},{7,39},{8,40},{9,... | collective-permute-start | bytes 1572872 | tf_op jit(solution)/shard_map/ppermute | solution.py:30
  24.3 12.5 %collective-permute-start.6 = (f32[128,1024]{1,0:T(8,128)S(1)}, f32[128,1024]{1,0:T(8,128)S(1)}, u32[]{:S(2)}, u32[]{:S(2)}) collective-permute-start(f32[128,1024]{1,0:T(8,128)S(1)} %copy-done.1), channel_id=1, source_target_pairs={{0,2},{1,3},{2,0},{3,1},{4,6},{5,7},{6,4},{7,5},{8,10},{9,11},{10,... | collective-permute-start | bytes 1572872 | tf_op jit(solution)/shard_map/ppermute | solution.py:30
  24.5 12.5 %collective-permute-start.5 = (f32[128,1024]{1,0:T(8,128)S(1)}, f32[128,1024]{1,0:T(8,128)S(1)}, u32[]{:S(2)}, u32[]{:S(2)}) collective-permute-start(f32[128,1024]{1,0:T(8,128)S(1)} %copy-done.1), channel_id=1, source_target_pairs={{0,4},{1,5},{2,6},{3,7},{4,0},{5,1},{6,2},{7,3},{8,12},{9,13},{10,... | collective-permute-start | bytes 1572872 | tf_op jit(solution)/shard_map/ppermute | solution.py:30
  37.0 10.1 %copy-start = (f32[8,128,128]{2,1,0:T(8,128)S(1)}, f32[8,128,128]{2,1,0:T(8,128)}, u32[]{:S(2)}) copy-start(f32[8,128,128]{2,1,0:T(8,128)} %turn.1.x) | copy-start | bytes 1572868
  37.1 10.0 %collective-permute-start.9 = (f32[8,768,128]{2,1,0:T(8,128)S(1)}, f32[8,768,128]{2,1,0:T(8,128)S(1)}, u32[]{:S(2)}, u32[]{:S(2)}) collective-permute-start(f32[8,768,128]{2,1,0:T(8,128)S(1)} %constant_dynamic-update-slice_fusion), channel_id=1, source_target_pairs={{0,8},{1,9},{2,10},{3,11},{4,12},{5,13},{6,14},{7,15},{8,0},{9,1},... | collective-permute-start | bytes 9437192 | tf_op jit(solution)/shard_map/ppermute | solution.py:30
  40.7 17.4 %collective-permute-start.11 = (f32[8,128,128]{2,1,0:T(8,128)S(1)}, f32[8,128,128]{2,1,0:T(8,128)S(1)}, u32[]{:S(2)}, u32[]{:S(2)}) collective-permute-start(f32[8,128,128]{2,1,0:T(8,128)S(1)} %pad_maximum_fusion.2), channel_id=1, source_target_pairs={{0,96},{1,97},{2,98},{3,99},{4,100},{5,101},{6,102},{7,103},{8,104... | collective-permute-start | bytes 1572872 | tf_op jit(solution)/shard_map/ppermute | solution.py:30
  43.0 15.1 %collective-permute-start.10 = (f32[8,128,128]{2,1,0:T(8,128)S(1)}, f32[8,128,128]{2,1,0:T(8,128)S(1)}, u32[]{:S(2)}, u32[]{:S(2)}) collective-permute-start(f32[8,128,128]{2,1,0:T(8,128)S(1)} %pad_maximum_fusion.1), channel_id=1, source_target_pairs={{0,32},{1,33},{2,34},{3,35},{4,36},{5,37},{6,38},{7,39},{8,40},{9,... | collective-permute-start | bytes 1572872 | tf_op jit(solution)/shard_map/ppermute | solution.py:30
  43.1 15.0 %collective-permute-start.14 = (f32[128,1024]{1,0:T(8,128)S(1)}, f32[128,1024]{1,0:T(8,128)S(1)}, u32[]{:S(2)}, u32[]{:S(2)}) collective-permute-start(f32[128,1024]{1,0:T(8,128)S(1)} %collective-permute-done.6.w2), channel_id=1, source_target_pairs={{0,4},{1,5},{2,6},{3,7},{4,0},{5,1},{6,2},{7,3},{8,12},{9,13},{10,... | collective-permute-start | bytes 1572872 | tf_op jit(solution)/shard_map/ppermute | solution.py:30
  45.6 12.9 %collective-permute-start.13 = (f32[128,1024]{1,0:T(8,128)S(1)}, f32[128,1024]{1,0:T(8,128)S(1)}, u32[]{:S(2)}, u32[]{:S(2)}) collective-permute-start(f32[128,1024]{1,0:T(8,128)S(1)} %collective-permute-done.5.wx), channel_id=1, source_target_pairs={{0,3},{1,0},{2,1},{3,2},{4,7},{5,4},{6,5},{7,6},{8,11},{9,8},{10,9... | collective-permute-start | bytes 1572872 | tf_op jit(solution)/shard_map/ppermute | solution.py:30
  47.1 13.8 %collective-permute-start.12 = (f32[128,1024]{1,0:T(8,128)S(1)}, f32[128,1024]{1,0:T(8,128)S(1)}, u32[]{:S(2)}, u32[]{:S(2)}) collective-permute-start(f32[128,1024]{1,0:T(8,128)S(1)} %collective-permute-done.5.wx), channel_id=1, source_target_pairs={{0,1},{1,2},{2,3},{3,0},{4,5},{5,6},{6,7},{7,4},{8,9},{9,10},{10,1... | collective-permute-start | bytes 1572872 | tf_op jit(solution)/shard_map/ppermute | solution.py:30
  61.0 9.6 %collective-permute-start.15 = (f32[8,256,128]{2,1,0:T(8,128)S(1)}, f32[8,256,128]{2,1,0:T(8,128)S(1)}, u32[]{:S(2)}, u32[]{:S(2)}) collective-permute-start(f32[8,256,128]{2,1,0:T(8,128)S(1)} %pad_maximum_fusion), channel_id=1, source_target_pairs={{0,8},{1,9},{2,10},{3,11},{4,12},{5,13},{6,14},{7,15},{8,0},{9,1},... | collective-permute-start | bytes 3145736 | tf_op jit(solution)/shard_map/ppermute | solution.py:30

commit v9 on v8

--- a/solution.py
+++ b/solution.py
@@ -308,8 +308,8 @@
     xp, xm, xx = hop(x, y=1), hop(x, y=3), hop(x, xl=1)
     xx, info, rgap, cgap = lax.optimization_barrier((xx, info, rgap, cgap))
     xxp, xxm = hop(xx, y=1), hop(xx, y=3)
-    w2, wx = hop(after(w, wp, wm, xp, xm), z=2), hop(after(w, xx, xp, xm, wp, wm), xh=1)
-    xxp, xxm = lax.optimization_barrier((xxp, xxm))
+    w2, wx = hop(after(w, wp, wm, xp, xm), z=2), hop(after(w, xx), xh=1)
+    wx, xxp, xxm = lax.optimization_barrier((wx, xxp, xxm))
     wx, w2, xxp, xxm = lax.optimization_barrier((wx, w2, xxp, xxm))
     s2 = hop(join(x, xx, xp, xxp, xm, xxm), core=1)
     up = hop(join(xp[:, :HALF], xxp[:, :HALF]), y=1)

time: 77.6 us -> 76.4 us (0.985)
  waiting for transfers between devices: 17.5 us -> 13.7 us
  starting transfers between devices: 26.3 us -> 28.9 us
    ppermute x16, waiting for transfers between devices: 17.5 us -> 13.7 us  [hop(): return lax.ppermute(value, AXES, pairs)]
    ppermute x16, starting transfers between devices: 26.3 us -> 28.9 us  [hop(): return lax.ppermute(value, AXES, pairs)]
  transfers between devices with their start and end apart: 16 -> 16, of which waited for: 10 -> 7; matrix products, arithmetic and copies ran while one was open for 7% -> 7% of each run, Pallas kernels for 24% -> 24%
where the time goes in v9:
time: 76.4 us; the launch traced here: 76.1 us
  starting transfers between devices  28.9 us (38%)
  Pallas kernels  27.5 us (36%)
  waiting for transfers between devices  13.7 us (18%)
  local copies, waits for them, and re-layouts  4.8 us (6%)
  other arithmetic  0.91 us (1%)
    ppermute x16, starting transfers between devices, hop(): return lax.ppermute(value, AXES, pairs)  28.9 us
    ppermute x16, waiting for transfers between devices, hop(): return lax.ppermute(value, AXES, pairs)  13.7 us
    pallas_call x1, Pallas kernels, early(): pl.pallas_call(early_kernel, out_shape=[pltpu.VMEM((3, ROWS, columns), f3...  8.58 us
    pallas_call x1, Pallas kernels, late(): pl.pallas_call(late_kernel, out_shape=[jax.ShapeDtypeStruct((virtuals, 4,...  7.54 us
    pallas_call x1, Pallas kernels, last(): pl.pallas_call(last_kernel, out_shape=jax.ShapeDtypeStruct((virtuals, 4,...  6.56 us
    pallas_call x1, Pallas kernels, turn(): pl.pallas_call(turn_kernel, out_shape=jax.ShapeDtypeStruct((depth // 128,...  2.43 us
    pallas_call x1, Pallas kernels, ready(): pl.pallas_call(ready_kernel, out_shape=[pltpu.VMEM((ROWS, DEEP), bf16)] *...  2.37 us
    broadcast_in_dim x3, local copies, waits for them, and re-layouts, body(): jnp.broadcast_to(row_gap.reshape(virtuals, 4, 8, 1), (virtuals, 4, 8, 128))  1.83 us
  transfers between devices with their start and end apart: 16, of which 7 were waited for; matrix products, arithmetic and copies ran while one was open for 7% of the time, Pallas kernels for 24%

profile of v9, /device:TPU:1, one launch (start us, length us, event | category | flops | bytes accessed | tf_op | source)
XLA Modules:
  0.0 76.1 jit_solution(962959320973851152)
XLA Ops:
  0.0 0.0 copy-start.1
  0.0 2.4 %turn.1.x = f32[8,128,128]{2,1,0:T(8,128)} custom-call(f32[2,1024,64]{2,1,0:T(8,128)} %bitcast.23), custom_call_target="tpu_custom_call" | custom-call | flops 1048576 | bytes 2097152 | tf_op jit(solution)/shard_map/turn/pallas_call | solution.py:51
  2.4 2.0 %collective-permute-start = (f32[8,128,128]{2,1,0:T(8,128)}, f32[8,128,128]{2,1,0:T(8,128)S(1)}, u32[]{:S(2)}, u32[]{:S(2)}) collective-permute-start(f32[8,128,128]{2,1,0:T(8,128)} %turn.1.x), channel_id=1, source_target_pairs={{0,16},{1,17},{2,18},{3,19},{4,20},{5,21},{6,22},{7,23},{8,24},{9,... | collective-permute-start | bytes 1572872 | tf_op jit(solution)/shard_map/ppermute | solution.py:30
  4.5 2.7 %collective-permute-start.7 = (f32[8,128,128]{2,1,0:T(8,128)}, f32[8,128,128]{2,1,0:T(8,128)S(1)}, u32[]{:S(2)}, u32[]{:S(2)}) collective-permute-start(f32[8,128,128]{2,1,0:T(8,128)} %turn.1.x), channel_id=1, source_target_pairs={{0,96},{1,97},{2,98},{3,99},{4,100},{5,101},{6,102},{7,103},{8,104... | collective-permute-start | bytes 1572872 | tf_op jit(solution)/shard_map/ppermute | solution.py:30
  7.2 0.0 collective-permute-start.1
  7.2 3.8 %collective-permute-start.6 = (f32[128,1024]{1,0:T(8,128)}, f32[128,1024]{1,0:T(8,128)S(1)}, u32[]{:S(2)}, u32[]{:S(2)}) collective-permute-start(f32[128,1024]{1,0:T(8,128)} %w.1), channel_id=1, source_target_pairs={{0,3},{1,0},{2,1},{3,2},{4,7},{5,4},{6,5},{7,6},{8,11},{9,8},{10,9... | collective-permute-start | bytes 1572872 | tf_op jit(solution)/shard_map/ppermute | solution.py:30
  11.0 0.0 collective-permute-start.5
  11.0 0.8 %broadcast_subtract_fusion = f32[512,32]{0,1:T(8,128)S(1)} fusion(f32[32]{0:T(128)} %param.6, f32[512]{0:T(512)} %param.7), kind=kLoop, calls=%fused_computation.3 | loop fusion | flops 16384 | bytes 67712 | tf_op jit(solution)/shard_map/sub | solution.py:297
  11.7 0.1 copy.7
  11.9 0.7 dynamic-slice_bitcast_fusion
  12.6 0.8 %copy.6 = f32[64,4,8]{2,1,0:T(4,128)S(1)} copy(f32[64,4,8]{0,2,1:T(8,128)} %dynamic-slice_bitcast_fusion) | data formatting | bytes 16384 | tf_op jit(solution)/shard_map/broadcast_in_dim | solution.py:299
  13.4 0.7 sub.37
  14.1 0.7 dynamic_slice.7
  14.8 0.1 stack.59.info_ref
  14.9 0.9 %collective-permute-done.xx = f32[8,128,128]{2,1,0:T(8,128)S(1)} collective-permute-done((f32[8,128,128]{2,1,0:T(8,128)}, f32[8,128,128]{2,1,0:T(8,128)S(1)}, u32[]{:S(2)}, u32[]{:S(2)}) %collective-permute-start) | collective-permute-done | bytes 524320 | tf_op jit(solution)/shard_map/ppermute | solution.py:30
  15.8 0.3 broadcast_in_dim.10.rgap_ref
  16.2 3.2 %collective-permute-start.4 = (f32[8,128,128]{2,1,0:T(8,128)S(1)}, f32[8,128,128]{2,1,0:T(8,128)S(1)}, u32[]{:S(2)}, u32[]{:S(2)}) collective-permute-start(f32[8,128,128]{2,1,0:T(8,128)S(1)} %collective-permute-done.xx), channel_id=1, source_target_pairs={{0,96},{1,97},{2,98},{3,99},{4,100},{5,101},{6,102},{7,103},{8,104... | collective-permute-start | bytes 1572872 | tf_op jit(solution)/shard_map/ppermute | solution.py:30
  19.4 0.0 collective-permute-done.7.xm
  19.4 0.0 collective-permute-start.3
  19.4 1.4 %collective-permute-done.1.xp = f32[8,128,128]{2,1,0:T(8,128)S(1)} collective-permute-done((f32[8,128,128]{2,1,0:T(8,128)}, f32[8,128,128]{2,1,0:T(8,128)S(1)}, u32[]{:S(2)}, u32[]{:S(2)}) %collective-permute-start.1) | collective-permute-done | bytes 524320 | tf_op jit(solution)/shard_map/ppermute | solution.py:30
  20.8 0.0 copy-done.1
  20.8 2.5 %collective-permute-start.2 = (f32[128,1024]{1,0:T(8,128)S(1)}, f32[128,1024]{1,0:T(8,128)S(1)}, u32[]{:S(2)}, u32[]{:S(2)}) collective-permute-start(f32[128,1024]{1,0:T(8,128)S(1)} %copy-done.1), channel_id=1, source_target_pairs={{0,4},{1,5},{2,6},{3,7},{4,0},{5,1},{6,2},{7,3},{8,12},{9,13},{10,... | collective-permute-start | bytes 1572872 | tf_op jit(solution)/shard_map/ppermute | solution.py:30
  23.3 0.0 collective-permute-done.6.wm
  23.3 1.0 %collective-permute-done.5.wp = f32[128,1024]{1,0:T(8,128)S(1)} collective-permute-done((f32[128,1024]{1,0:T(8,128)}, f32[128,1024]{1,0:T(8,128)S(1)}, u32[]{:S(2)}, u32[]{:S(2)}) %collective-permute-start.5) | collective-permute-done | bytes 524320 | tf_op jit(solution)/shard_map/ppermute | solution.py:30
  24.3 2.6 %collective-permute-start.8 = (f32[128,1024]{1,0:T(8,128)S(1)}, f32[128,1024]{1,0:T(8,128)S(1)}, u32[]{:S(2)}, u32[]{:S(2)}) collective-permute-start(f32[128,1024]{1,0:T(8,128)S(1)} %copy-done.1), channel_id=1, source_target_pairs={{0,2},{1,3},{2,0},{3,1},{4,6},{5,7},{6,4},{7,5},{8,10},{9,11},{10,... | collective-permute-start | bytes 1572872 | tf_op jit(solution)/shard_map/ppermute | solution.py:30
  26.9 1.1 %constant_dynamic-update-slice_fusion.5 = f32[8,768,128]{2,1,0:T(8,128)S(1)} fusion(f32[8,128,128]{2,1,0:T(8,128)} %turn.1.x), kind=kLoop, calls=%fused_computation.10 | loop fusion | bytes 1048576
  28.0 5.5 %collective-permute-done.2.wx = f32[128,1024]{1,0:T(8,128)S(1)} collective-permute-done((f32[128,1024]{1,0:T(8,128)S(1)}, f32[128,1024]{1,0:T(8,128)S(1)}, u32[]{:S(2)}, u32[]{:S(2)}) %collective-permute-start.2) | collective-permute-done | bytes 524320 | tf_op jit(solution)/shard_map/ppermute | solution.py:30
  33.6 0.0 collective-permute-done.4.xxm
  33.6 0.0 collective-permute-done.3.xxp
  33.6 3.2 %collective-permute-done.8.w2 = f32[128,1024]{1,0:T(8,128)S(1)} collective-permute-done((f32[128,1024]{1,0:T(8,128)S(1)}, f32[128,1024]{1,0:T(8,128)S(1)}, u32[]{:S(2)}, u32[]{:S(2)}) %collective-permute-start.8) | collective-permute-done | bytes 524320 | tf_op jit(solution)/shard_map/ppermute | solution.py:30
  36.8 0.0 copy-start
  36.9 3.4 %collective-permute-start.9 = (f32[8,768,128]{2,1,0:T(8,128)S(1)}, f32[8,768,128]{2,1,0:T(8,128)S(1)}, u32[]{:S(2)}, u32[]{:S(2)}) collective-permute-start(f32[8,768,128]{2,1,0:T(8,128)S(1)} %constant_dynamic-update-slice_fusion), channel_id=1, source_target_pairs={{0,8},{1,9},{2,10},{3,11},{4,12},{5,13},{6,14},{7,15},{8,0},{9,1},... | collective-permute-start | bytes 9437192 | tf_op jit(solution)/shard_map/ppermute | solution.py:30
  40.5 2.5 %collective-permute-start.11 = (f32[8,128,128]{2,1,0:T(8,128)S(1)}, f32[8,128,128]{2,1,0:T(8,128)S(1)}, u32[]{:S(2)}, u32[]{:S(2)}) collective-permute-start(f32[8,128,128]{2,1,0:T(8,128)S(1)} %pad_maximum_fusion.2), channel_id=1, source_target_pairs={{0,96},{1,97},{2,98},{3,99},{4,100},{5,101},{6,102},{7,103},{8,104... | collective-permute-start | bytes 1572872 | tf_op jit(solution)/shard_map/ppermute | solution.py:30
  43.0 0.1 collective-permute-start.10
  43.1 2.5 %collective-permute-start.14 = (f32[128,1024]{1,0:T(8,128)S(1)}, f32[128,1024]{1,0:T(8,128)S(1)}, u32[]{:S(2)}, u32[]{:S(2)}) collective-permute-start(f32[128,1024]{1,0:T(8,128)S(1)} %collective-permute-done.8.w2), channel_id=1, source_target_pairs={{0,4},{1,5},{2,6},{3,7},{4,0},{5,1},{6,2},{7,3},{8,12},{9,13},{10,... | collective-permute-start | bytes 1572872 | tf_op jit(solution)/shard_map/ppermute | solution.py:30
  45.6 0.3 collective-permute-start.13
  45.9 0.0 collective-permute-done.9.s1.s2
  45.9 1.2 %collective-permute-start.12 = (f32[128,1024]{1,0:T(8,128)S(1)}, f32[128,1024]{1,0:T(8,128)S(1)}, u32[]{:S(2)}, u32[]{:S(2)}) collective-permute-start(f32[128,1024]{1,0:T(8,128)S(1)} %collective-permute-done.2.wx), channel_id=1, source_target_pairs={{0,1},{1,2},{2,3},{3,0},{4,5},{5,6},{6,7},{7,4},{8,9},{9,10},{10,1... | collective-permute-start | bytes 1572872 | tf_op jit(solution)/shard_map/ppermute | solution.py:30
  47.1 0.0 copy-done
  47.1 2.4 %ready.1 = (bf16[512,512]{1,0:T(8,128)(2,1)S(1)}, bf16[512,512]{1,0:T(8,128)(2,1)S(1)}, bf16[512,512]{1,0:T(8,128)(2,1)S(1)}, bf16[512,512]{1,0:T(8,128)(2,1)S(1...) custom-call(s32[14]{0:T(128)S(1)} %stack.59.info_ref, f32[8,128,128]{2,1,0:T(8,128)S(1)} %copy-done, ...), custom_call_target="tpu_custom_call" | custom-call | flops 1048576 | bytes 10485760 | tf_op jit(solution)/shard_map/ready/pallas_call | solution.py:124
  49.5 8.6 %early.1 = (f32[3,512,1024]{2,1,0:T(8,128)S(1)}, bf16[2,512,512]{2,1,0:T(8,128)(2,1)S(1)}, bf16[2,512,512]{2,1,0:T(8,128)(2,1)S(1)}, bf16[512,1024]{1,0:T(8,128)(2,1)S(1)}, bf16[512,1024]{1,0:T(8,128)(2,1)S(1)}) custom-call(s32[14]{0:T(128)S(1)} %stack.59.info_ref, f32[8,768,128]{2,1,0:T(8,128)S(1)} %collective-permute-done.9.s1.s2, ...), custom_call_target="tpu_custom_call" | custom-call | flops 4831838208 | bytes 20971520 | tf_op jit(solution)/shard_map/early/pallas_call | solution.py:160
  58.0 0.0 collective-permute-done.11.down
  58.1 0.0 collective-permute-done.10.up
  58.1 0.0 collective-permute-done.14.wx2
  58.1 0.4 collective-permute-done.13.wxm
  58.5 1.2 %collective-permute-done.12.wxp = f32[128,1024]{1,0:T(8,128)S(1)} collective-permute-done((f32[128,1024]{1,0:T(8,128)S(1)}, f32[128,1024]{1,0:T(8,128)S(1)}, u32[]{:S(2)}, u32[]{:S(2)}) %collective-permute-start.12) | collective-permute-done | bytes 524320 | tf_op jit(solution)/shard_map/ppermute | solution.py:30
  59.7 0.1 pad_maximum_fusion
  59.8 2.1 %collective-permute-start.15 = (f32[8,256,128]{2,1,0:T(8,128)S(1)}, f32[8,256,128]{2,1,0:T(8,128)S(1)}, u32[]{:S(2)}, u32[]{:S(2)}) collective-permute-start(f32[8,256,128]{2,1,0:T(8,128)S(1)} %pad_maximum_fusion), channel_id=1, source_target_pairs={{0,8},{1,9},{2,10},{3,11},{4,12},{5,13},{6,14},{7,15},{8,0},{9,1},... | collective-permute-start | bytes 3145736 | tf_op jit(solution)/shard_map/ppermute | solution.py:30
  61.8 7.5 %late.1 = (f32[64,4,8,1024]{3,2,1,0:T(8,128)}, bf16[512,1024]{1,0:T(8,128)(2,1)S(1)}, bf16[512,1024]{1,0:T(8,128)(2,1)S(1)}) custom-call(s32[14]{0:T(128)S(1)} %stack.59.info_ref, f32[3,512,1024]{2,1,0:T(8,128)S(1)} %get-tuple-element.52.part_ref, bf16[512,512]{1,0:T(8,128)(2,1)S(1)} %get-tuple-element.53.high2, ...), custom_call_target="tpu_custom_call" | custom-call | flops 4831838208 | bytes 25165824 | tf_op jit(solution)/shard_map/late/pallas_call | solution.py:210
  69.4 0.0 collective-permute-done.15.s3
  69.4 6.6 %last.1 = f32[64,4,8,1024]{3,2,1,0:T(8,128)} custom-call(s32[14]{0:T(128)S(1)} %stack.59.info_ref, f32[64,4,8,1024]{3,2,1,0:T(8,128)} %get-tuple-element.64.rest_ref, f32[8,128,128]{2,1,0:T(8,128)S(1)} %collective-permute-done.10.up, f32[8,128,128]{2,1,0:T(8,128)S(1)} %collective-permute-done.11.down, ...), custom_call_target="tpu_custom_call", output_to_operand_aliasing={{}: (1, {})} | custom-call | flops 3221225472 | bytes 8388608 | tf_op jit(solution)/shard_map/last/pallas_call | solution.py:266
  (11 shorter events, 0.3 us)
Async XLA Ops:
  0.0 20.8 %copy-start.1 = (f32[128,1024]{1,0:T(8,128)S(1)}, f32[128,1024]{1,0:T(8,128)}, u32[]{:S(2)}) copy-start(f32[128,1024]{1,0:T(8,128)} %w.1) | copy-start | bytes 1572868
  2.4 13.4 %collective-permute-start = (f32[8,128,128]{2,1,0:T(8,128)}, f32[8,128,128]{2,1,0:T(8,128)S(1)}, u32[]{:S(2)}, u32[]{:S(2)}) collective-permute-start(f32[8,128,128]{2,1,0:T(8,128)} %turn.1.x), channel_id=1, source_target_pairs={{0,16},{1,17},{2,18},{3,19},{4,20},{5,21},{6,22},{7,23},{8,24},{9,... | collective-permute-start | bytes 1572872 | tf_op jit(solution)/shard_map/ppermute | solution.py:30
  4.5 14.9 %collective-permute-start.7 = (f32[8,128,128]{2,1,0:T(8,128)}, f32[8,128,128]{2,1,0:T(8,128)S(1)}, u32[]{:S(2)}, u32[]{:S(2)}) collective-permute-start(f32[8,128,128]{2,1,0:T(8,128)} %turn.1.x), channel_id=1, source_target_pairs={{0,96},{1,97},{2,98},{3,99},{4,100},{5,101},{6,102},{7,103},{8,104... | collective-permute-start | bytes 1572872 | tf_op jit(solution)/shard_map/ppermute | solution.py:30
  7.2 13.6 %collective-permute-start.1 = (f32[8,128,128]{2,1,0:T(8,128)}, f32[8,128,128]{2,1,0:T(8,128)S(1)}, u32[]{:S(2)}, u32[]{:S(2)}) collective-permute-start(f32[8,128,128]{2,1,0:T(8,128)} %turn.1.x), channel_id=1, source_target_pairs={{0,32},{1,33},{2,34},{3,35},{4,36},{5,37},{6,38},{7,39},{8,40},{9,... | collective-permute-start | bytes 1572872 | tf_op jit(solution)/shard_map/ppermute | solution.py:30
  7.2 16.1 %collective-permute-start.6 = (f32[128,1024]{1,0:T(8,128)}, f32[128,1024]{1,0:T(8,128)S(1)}, u32[]{:S(2)}, u32[]{:S(2)}) collective-permute-start(f32[128,1024]{1,0:T(8,128)} %w.1), channel_id=1, source_target_pairs={{0,3},{1,0},{2,1},{3,2},{4,7},{5,4},{6,5},{7,6},{8,11},{9,8},{10,9... | collective-permute-start | bytes 1572872 | tf_op jit(solution)/shard_map/ppermute | solution.py:30
  11.0 13.3 %collective-permute-start.5 = (f32[128,1024]{1,0:T(8,128)}, f32[128,1024]{1,0:T(8,128)S(1)}, u32[]{:S(2)}, u32[]{:S(2)}) collective-permute-start(f32[128,1024]{1,0:T(8,128)} %w.1), channel_id=1, source_target_pairs={{0,1},{1,2},{2,3},{3,0},{4,5},{5,6},{6,7},{7,4},{8,9},{9,10},{10,1... | collective-permute-start | bytes 1572872 | tf_op jit(solution)/shard_map/ppermute | solution.py:30
  16.2 17.4 %collective-permute-start.4 = (f32[8,128,128]{2,1,0:T(8,128)S(1)}, f32[8,128,128]{2,1,0:T(8,128)S(1)}, u32[]{:S(2)}, u32[]{:S(2)}) collective-permute-start(f32[8,128,128]{2,1,0:T(8,128)S(1)} %collective-permute-done.xx), channel_id=1, source_target_pairs={{0,96},{1,97},{2,98},{3,99},{4,100},{5,101},{6,102},{7,103},{8,104... | collective-permute-start | bytes 1572872 | tf_op jit(solution)/shard_map/ppermute | solution.py:30
  19.4 14.2 %collective-permute-start.3 = (f32[8,128,128]{2,1,0:T(8,128)S(1)}, f32[8,128,128]{2,1,0:T(8,128)S(1)}, u32[]{:S(2)}, u32[]{:S(2)}) collective-permute-start(f32[8,128,128]{2,1,0:T(8,128)S(1)} %collective-permute-done.xx), channel_id=1, source_target_pairs={{0,32},{1,33},{2,34},{3,35},{4,36},{5,37},{6,38},{7,39},{8,40},{9,... | collective-permute-start | bytes 1572872 | tf_op jit(solution)/shard_map/ppermute | solution.py:30
  20.8 12.8 %collective-permute-start.2 = (f32[128,1024]{1,0:T(8,128)S(1)}, f32[128,1024]{1,0:T(8,128)S(1)}, u32[]{:S(2)}, u32[]{:S(2)}) collective-permute-start(f32[128,1024]{1,0:T(8,128)S(1)} %copy-done.1), channel_id=1, source_target_pairs={{0,4},{1,5},{2,6},{3,7},{4,0},{5,1},{6,2},{7,3},{8,12},{9,13},{10,... | collective-permute-start | bytes 1572872 | tf_op jit(solution)/shard_map/ppermute | solution.py:30
  24.3 12.5 %collective-permute-start.8 = (f32[128,1024]{1,0:T(8,128)S(1)}, f32[128,1024]{1,0:T(8,128)S(1)}, u32[]{:S(2)}, u32[]{:S(2)}) collective-permute-start(f32[128,1024]{1,0:T(8,128)S(1)} %copy-done.1), channel_id=1, source_target_pairs={{0,2},{1,3},{2,0},{3,1},{4,6},{5,7},{6,4},{7,5},{8,10},{9,11},{10,... | collective-permute-start | bytes 1572872 | tf_op jit(solution)/shard_map/ppermute | solution.py:30
  36.8 10.3 %copy-start = (f32[8,128,128]{2,1,0:T(8,128)S(1)}, f32[8,128,128]{2,1,0:T(8,128)}, u32[]{:S(2)}) copy-start(f32[8,128,128]{2,1,0:T(8,128)} %turn.1.x) | copy-start | bytes 1572868
  36.9 9.0 %collective-permute-start.9 = (f32[8,768,128]{2,1,0:T(8,128)S(1)}, f32[8,768,128]{2,1,0:T(8,128)S(1)}, u32[]{:S(2)}, u32[]{:S(2)}) collective-permute-start(f32[8,768,128]{2,1,0:T(8,128)S(1)} %constant_dynamic-update-slice_fusion), channel_id=1, source_target_pairs={{0,8},{1,9},{2,10},{3,11},{4,12},{5,13},{6,14},{7,15},{8,0},{9,1},... | collective-permute-start | bytes 9437192 | tf_op jit(solution)/shard_map/ppermute | solution.py:30
  40.5 17.6 %collective-permute-start.11 = (f32[8,128,128]{2,1,0:T(8,128)S(1)}, f32[8,128,128]{2,1,0:T(8,128)S(1)}, u32[]{:S(2)}, u32[]{:S(2)}) collective-permute-start(f32[8,128,128]{2,1,0:T(8,128)S(1)} %pad_maximum_fusion.2), channel_id=1, source_target_pairs={{0,96},{1,97},{2,98},{3,99},{4,100},{5,101},{6,102},{7,103},{8,104... | collective-permute-start | bytes 1572872 | tf_op jit(solution)/shard_map/ppermute | solution.py:30
  43.0 15.1 %collective-permute-start.10 = (f32[8,128,128]{2,1,0:T(8,128)S(1)}, f32[8,128,128]{2,1,0:T(8,128)S(1)}, u32[]{:S(2)}, u32[]{:S(2)}) collective-permute-start(f32[8,128,128]{2,1,0:T(8,128)S(1)} %pad_maximum_fusion.1), channel_id=1, source_target_pairs={{0,32},{1,33},{2,34},{3,35},{4,36},{5,37},{6,38},{7,39},{8,40},{9,... | collective-permute-start | bytes 1572872 | tf_op jit(solution)/shard_map/ppermute | solution.py:30
  43.1 15.0 %collective-permute-start.14 = (f32[128,1024]{1,0:T(8,128)S(1)}, f32[128,1024]{1,0:T(8,128)S(1)}, u32[]{:S(2)}, u32[]{:S(2)}) collective-permute-start(f32[128,1024]{1,0:T(8,128)S(1)} %collective-permute-done.8.w2), channel_id=1, source_target_pairs={{0,4},{1,5},{2,6},{3,7},{4,0},{5,1},{6,2},{7,3},{8,12},{9,13},{10,... | collective-permute-start | bytes 1572872 | tf_op jit(solution)/shard_map/ppermute | solution.py:30
  45.6 12.9 %collective-permute-start.13 = (f32[128,1024]{1,0:T(8,128)S(1)}, f32[128,1024]{1,0:T(8,128)S(1)}, u32[]{:S(2)}, u32[]{:S(2)}) collective-permute-start(f32[128,1024]{1,0:T(8,128)S(1)} %collective-permute-done.2.wx), channel_id=1, source_target_pairs={{0,3},{1,0},{2,1},{3,2},{4,7},{5,4},{6,5},{7,6},{8,11},{9,8},{10,9... | collective-permute-start | bytes 1572872 | tf_op jit(solution)/shard_map/ppermute | solution.py:30
  45.9 13.8 %collective-permute-start.12 = (f32[128,1024]{1,0:T(8,128)S(1)}, f32[128,1024]{1,0:T(8,128)S(1)}, u32[]{:S(2)}, u32[]{:S(2)}) collective-permute-start(f32[128,1024]{1,0:T(8,128)S(1)} %collective-permute-done.2.wx), channel_id=1, source_target_pairs={{0,1},{1,2},{2,3},{3,0},{4,5},{5,6},{6,7},{7,4},{8,9},{9,10},{10,1... | collective-permute-start | bytes 1572872 | tf_op jit(solution)/shard_map/ppermute | solution.py:30
  59.8 9.6 %collective-permute-start.15 = (f32[8,256,128]{2,1,0:T(8,128)S(1)}, f32[8,256,128]{2,1,0:T(8,128)S(1)}, u32[]{:S(2)}, u32[]{:S(2)}) collective-permute-start(f32[8,256,128]{2,1,0:T(8,128)S(1)} %pad_maximum_fusion), channel_id=1, source_target_pairs={{0,8},{1,9},{2,10},{3,11},{4,12},{5,13},{6,14},{7,15},{8,0},{9,1},... | collective-permute-start | bytes 3145736 | tf_op jit(solution)/shard_map/ppermute | solution.py:30

commit v10 on v9

--- a/solution.py
+++ b/solution.py
@@ -48,12 +48,13 @@
 
 def turn(amp):
     two, depth, width = amp.shape
+    steps = 2
     return pl.pallas_call(
         turn_kernel,
         out_shape=jax.ShapeDtypeStruct((depth // 128, two * width, 128), f32),
-        in_specs=[pl.BlockSpec(memory_space=pltpu.VMEM)],
-        out_specs=pl.BlockSpec(memory_space=pltpu.VMEM),
-        cost_estimate=pl.CostEstimate(flops=TURN_FLOPS, bytes_accessed=2 * MIB, transcendentals=0),
+        grid=(steps,),
+        in_specs=[pl.BlockSpec((two, depth // steps, width), lambda s: (0, s, 0))],
+        out_specs=pl.BlockSpec((depth // 128 // steps, two * width, 128), lambda s: (s, 0, 0)),
         name="turn",
     )(amp)
 

time: 76.4 us -> 76.2 us (level)
  no operation moved by 1% of the time
where the time goes in v10:
time: 76.2 us; the launch traced here: 75.9 us
  starting transfers between devices  28.9 us (38%)
  Pallas kernels  27.3 us (36%)
  waiting for transfers between devices  13.7 us (18%)
  local copies, waits for them, and re-layouts  4.8 us (6%)
  other arithmetic  0.91 us (1%)
    ppermute x16, starting transfers between devices, hop(): return lax.ppermute(value, AXES, pairs)  28.9 us
    ppermute x16, waiting for transfers between devices, hop(): return lax.ppermute(value, AXES, pairs)  13.7 us
    pallas_call x1, Pallas kernels, early(): pl.pallas_call(early_kernel, out_shape=[pltpu.VMEM((3, ROWS, columns), f3...  8.58 us
    pallas_call x1, Pallas kernels, late(): pl.pallas_call(late_kernel, out_shape=[jax.ShapeDtypeStruct((virtuals, 4,...  7.54 us
    pallas_call x1, Pallas kernels, last(): pl.pallas_call(last_kernel, out_shape=jax.ShapeDtypeStruct((virtuals, 4,...  6.55 us
    pallas_call x1, Pallas kernels, ready(): pl.pallas_call(ready_kernel, out_shape=[pltpu.VMEM((ROWS, DEEP), bf16)] *...  2.37 us
    pallas_call x1, Pallas kernels, turn(): pl.pallas_call(turn_kernel, out_shape=jax.ShapeDtypeStruct((depth // 128,...  2.26 us
    broadcast_in_dim x3, local copies, waits for them, and re-layouts, body(): jnp.broadcast_to(row_gap.reshape(virtuals, 4, 8, 1), (virtuals, 4, 8, 128))  1.83 us
  transfers between devices with their start and end apart: 16, of which 7 were waited for; matrix products, arithmetic and copies ran while one was open for 7% of the time, Pallas kernels for 24%

profile of v10, /device:TPU:1, one launch (start us, length us, event | category | flops | bytes accessed | tf_op | source)
XLA Modules:
  0.0 75.9 jit_solution(5156353453052733477)
XLA Ops:
  0.0 0.0 copy-start.1
  0.0 2.3 %turn.1.x = f32[8,128,128]{2,1,0:T(8,128)} custom-call(f32[2,1024,64]{2,1,0:T(8,128)} %bitcast.23), custom_call_target="tpu_custom_call" | custom-call | tf_op jit(solution)/shard_map/turn/pallas_call | solution.py:52
  2.3 2.0 %collective-permute-start = (f32[8,128,128]{2,1,0:T(8,128)}, f32[8,128,128]{2,1,0:T(8,128)S(1)}, u32[]{:S(2)}, u32[]{:S(2)}) collective-permute-start(f32[8,128,128]{2,1,0:T(8,128)} %turn.1.x), channel_id=1, source_target_pairs={{0,16},{1,17},{2,18},{3,19},{4,20},{5,21},{6,22},{7,23},{8,24},{9,... | collective-permute-start | bytes 1572872 | tf_op jit(solution)/shard_map/ppermute | solution.py:30
  4.3 2.7 %collective-permute-start.7 = (f32[8,128,128]{2,1,0:T(8,128)}, f32[8,128,128]{2,1,0:T(8,128)S(1)}, u32[]{:S(2)}, u32[]{:S(2)}) collective-permute-start(f32[8,128,128]{2,1,0:T(8,128)} %turn.1.x), channel_id=1, source_target_pairs={{0,96},{1,97},{2,98},{3,99},{4,100},{5,101},{6,102},{7,103},{8,104... | collective-permute-start | bytes 1572872 | tf_op jit(solution)/shard_map/ppermute | solution.py:30
  7.0 0.0 collective-permute-start.1
  7.0 3.8 %collective-permute-start.6 = (f32[128,1024]{1,0:T(8,128)}, f32[128,1024]{1,0:T(8,128)S(1)}, u32[]{:S(2)}, u32[]{:S(2)}) collective-permute-start(f32[128,1024]{1,0:T(8,128)} %w.1), channel_id=1, source_target_pairs={{0,3},{1,0},{2,1},{3,2},{4,7},{5,4},{6,5},{7,6},{8,11},{9,8},{10,9... | collective-permute-start | bytes 1572872 | tf_op jit(solution)/shard_map/ppermute | solution.py:30
  10.8 0.0 collective-permute-start.5
  10.8 0.8 %broadcast_subtract_fusion = f32[512,32]{0,1:T(8,128)S(1)} fusion(f32[32]{0:T(128)} %param.6, f32[512]{0:T(512)} %param.7), kind=kLoop, calls=%fused_computation.3 | loop fusion | flops 16384 | bytes 67712 | tf_op jit(solution)/shard_map/sub | solution.py:298
  11.6 0.1 copy.7
  11.7 0.7 dynamic-slice_bitcast_fusion
  12.4 0.8 %copy.6 = f32[64,4,8]{2,1,0:T(4,128)S(1)} copy(f32[64,4,8]{0,2,1:T(8,128)} %dynamic-slice_bitcast_fusion) | data formatting | bytes 16384 | tf_op jit(solution)/shard_map/broadcast_in_dim | solution.py:300
  13.2 0.7 sub.37
  13.9 0.7 dynamic_slice.7
  14.6 0.1 stack.59.info_ref
  14.7 0.9 %collective-permute-done.xx = f32[8,128,128]{2,1,0:T(8,128)S(1)} collective-permute-done((f32[8,128,128]{2,1,0:T(8,128)}, f32[8,128,128]{2,1,0:T(8,128)S(1)}, u32[]{:S(2)}, u32[]{:S(2)}) %collective-permute-start) | collective-permute-done | bytes 524320 | tf_op jit(solution)/shard_map/ppermute | solution.py:30
  15.6 0.3 broadcast_in_dim.10.rgap_ref
  16.0 3.2 %collective-permute-start.4 = (f32[8,128,128]{2,1,0:T(8,128)S(1)}, f32[8,128,128]{2,1,0:T(8,128)S(1)}, u32[]{:S(2)}, u32[]{:S(2)}) collective-permute-start(f32[8,128,128]{2,1,0:T(8,128)S(1)} %collective-permute-done.xx), channel_id=1, source_target_pairs={{0,96},{1,97},{2,98},{3,99},{4,100},{5,101},{6,102},{7,103},{8,104... | collective-permute-start | bytes 1572872 | tf_op jit(solution)/shard_map/ppermute | solution.py:30
  19.2 0.0 collective-permute-done.7.xm
  19.2 0.0 collective-permute-start.3
  19.2 1.4 %collective-permute-done.1.xp = f32[8,128,128]{2,1,0:T(8,128)S(1)} collective-permute-done((f32[8,128,128]{2,1,0:T(8,128)}, f32[8,128,128]{2,1,0:T(8,128)S(1)}, u32[]{:S(2)}, u32[]{:S(2)}) %collective-permute-start.1) | collective-permute-done | bytes 524320 | tf_op jit(solution)/shard_map/ppermute | solution.py:30
  20.6 0.0 copy-done.1
  20.6 2.5 %collective-permute-start.2 = (f32[128,1024]{1,0:T(8,128)S(1)}, f32[128,1024]{1,0:T(8,128)S(1)}, u32[]{:S(2)}, u32[]{:S(2)}) collective-permute-start(f32[128,1024]{1,0:T(8,128)S(1)} %copy-done.1), channel_id=1, source_target_pairs={{0,4},{1,5},{2,6},{3,7},{4,0},{5,1},{6,2},{7,3},{8,12},{9,13},{10,... | collective-permute-start | bytes 1572872 | tf_op jit(solution)/shard_map/ppermute | solution.py:30
  23.1 0.0 collective-permute-done.6.wm
  23.1 1.0 %collective-permute-done.5.wp = f32[128,1024]{1,0:T(8,128)S(1)} collective-permute-done((f32[128,1024]{1,0:T(8,128)}, f32[128,1024]{1,0:T(8,128)S(1)}, u32[]{:S(2)}, u32[]{:S(2)}) %collective-permute-start.5) | collective-permute-done | bytes 524320 | tf_op jit(solution)/shard_map/ppermute | solution.py:30
  24.1 2.6 %collective-permute-start.8 = (f32[128,1024]{1,0:T(8,128)S(1)}, f32[128,1024]{1,0:T(8,128)S(1)}, u32[]{:S(2)}, u32[]{:S(2)}) collective-permute-start(f32[128,1024]{1,0:T(8,128)S(1)} %copy-done.1), channel_id=1, source_target_pairs={{0,2},{1,3},{2,0},{3,1},{4,6},{5,7},{6,4},{7,5},{8,10},{9,11},{10,... | collective-permute-start | bytes 1572872 | tf_op jit(solution)/shard_map/ppermute | solution.py:30
  26.7 1.1 %constant_dynamic-update-slice_fusion.5 = f32[8,768,128]{2,1,0:T(8,128)S(1)} fusion(f32[8,128,128]{2,1,0:T(8,128)} %turn.1.x), kind=kLoop, calls=%fused_computation.10 | loop fusion | bytes 1048576
  27.9 5.5 %collective-permute-done.2.wx = f32[128,1024]{1,0:T(8,128)S(1)} collective-permute-done((f32[128,1024]{1,0:T(8,128)S(1)}, f32[128,1024]{1,0:T(8,128)S(1)}, u32[]{:S(2)}, u32[]{:S(2)}) %collective-permute-start.2) | collective-permute-done | bytes 524320 | tf_op jit(solution)/shard_map/ppermute | solution.py:30
  33.4 0.0 collective-permute-done.4.xxm
  33.4 0.0 collective-permute-done.3.xxp
  33.4 3.2 %collective-permute-done.8.w2 = f32[128,1024]{1,0:T(8,128)S(1)} collective-permute-done((f32[128,1024]{1,0:T(8,128)S(1)}, f32[128,1024]{1,0:T(8,128)S(1)}, u32[]{:S(2)}, u32[]{:S(2)}) %collective-permute-start.8) | collective-permute-done | bytes 524320 | tf_op jit(solution)/shard_map/ppermute | solution.py:30
  36.6 0.0 copy-start
  36.7 3.4 %collective-permute-start.9 = (f32[8,768,128]{2,1,0:T(8,128)S(1)}, f32[8,768,128]{2,1,0:T(8,128)S(1)}, u32[]{:S(2)}, u32[]{:S(2)}) collective-permute-start(f32[8,768,128]{2,1,0:T(8,128)S(1)} %constant_dynamic-update-slice_fusion), channel_id=1, source_target_pairs={{0,8},{1,9},{2,10},{3,11},{4,12},{5,13},{6,14},{7,15},{8,0},{9,1},... | collective-permute-start | bytes 9437192 | tf_op jit(solution)/shard_map/ppermute | solution.py:30
  40.3 2.5 %collective-permute-start.11 = (f32[8,128,128]{2,1,0:T(8,128)S(1)}, f32[8,128,128]{2,1,0:T(8,128)S(1)}, u32[]{:S(2)}, u32[]{:S(2)}) collective-permute-start(f32[8,128,128]{2,1,0:T(8,128)S(1)} %pad_maximum_fusion.2), channel_id=1, source_target_pairs={{0,96},{1,97},{2,98},{3,99},{4,100},{5,101},{6,102},{7,103},{8,104... | collective-permute-start | bytes 1572872 | tf_op jit(solution)/shard_map/ppermute | solution.py:30
  42.8 0.1 collective-permute-start.10
  42.9 2.5 %collective-permute-start.14 = (f32[128,1024]{1,0:T(8,128)S(1)}, f32[128,1024]{1,0:T(8,128)S(1)}, u32[]{:S(2)}, u32[]{:S(2)}) collective-permute-start(f32[128,1024]{1,0:T(8,128)S(1)} %collective-permute-done.8.w2), channel_id=1, source_target_pairs={{0,4},{1,5},{2,6},{3,7},{4,0},{5,1},{6,2},{7,3},{8,12},{9,13},{10,... | collective-permute-start | bytes 1572872 | tf_op jit(solution)/shard_map/ppermute | solution.py:30
  45.4 0.3 collective-permute-start.13
  45.7 0.0 collective-permute-done.9.s1.s2
  45.7 1.2 %collective-permute-start.12 = (f32[128,1024]{1,0:T(8,128)S(1)}, f32[128,1024]{1,0:T(8,128)S(1)}, u32[]{:S(2)}, u32[]{:S(2)}) collective-permute-start(f32[128,1024]{1,0:T(8,128)S(1)} %collective-permute-done.2.wx), channel_id=1, source_target_pairs={{0,1},{1,2},{2,3},{3,0},{4,5},{5,6},{6,7},{7,4},{8,9},{9,10},{10,1... | collective-permute-start | bytes 1572872 | tf_op jit(solution)/shard_map/ppermute | solution.py:30
  46.9 0.0 copy-done
  46.9 2.4 %ready.1 = (bf16[512,512]{1,0:T(8,128)(2,1)S(1)}, bf16[512,512]{1,0:T(8,128)(2,1)S(1)}, bf16[512,512]{1,0:T(8,128)(2,1)S(1)}, bf16[512,512]{1,0:T(8,128)(2,1)S(1...) custom-call(s32[14]{0:T(128)S(1)} %stack.59.info_ref, f32[8,128,128]{2,1,0:T(8,128)S(1)} %copy-done, ...), custom_call_target="tpu_custom_call" | custom-call | flops 1048576 | bytes 10485760 | tf_op jit(solution)/shard_map/ready/pallas_call | solution.py:125
  49.3 8.6 %early.1 = (f32[3,512,1024]{2,1,0:T(8,128)S(1)}, bf16[2,512,512]{2,1,0:T(8,128)(2,1)S(1)}, bf16[2,512,512]{2,1,0:T(8,128)(2,1)S(1)}, bf16[512,1024]{1,0:T(8,128)(2,1)S(1)}, bf16[512,1024]{1,0:T(8,128)(2,1)S(1)}) custom-call(s32[14]{0:T(128)S(1)} %stack.59.info_ref, f32[8,768,128]{2,1,0:T(8,128)S(1)} %collective-permute-done.9.s1.s2, ...), custom_call_target="tpu_custom_call" | custom-call | flops 4831838208 | bytes 20971520 | tf_op jit(solution)/shard_map/early/pallas_call | solution.py:161
  57.9 0.0 collective-permute-done.11.down
  57.9 0.0 collective-permute-done.10.up
  57.9 0.0 collective-permute-done.14.wx2
  57.9 0.4 collective-permute-done.13.wxm
  58.3 1.2 %collective-permute-done.12.wxp = f32[128,1024]{1,0:T(8,128)S(1)} collective-permute-done((f32[128,1024]{1,0:T(8,128)S(1)}, f32[128,1024]{1,0:T(8,128)S(1)}, u32[]{:S(2)}, u32[]{:S(2)}) %collective-permute-start.12) | collective-permute-done | bytes 524320 | tf_op jit(solution)/shard_map/ppermute | solution.py:30
  59.5 0.1 pad_maximum_fusion
  59.6 2.1 %collective-permute-start.15 = (f32[8,256,128]{2,1,0:T(8,128)S(1)}, f32[8,256,128]{2,1,0:T(8,128)S(1)}, u32[]{:S(2)}, u32[]{:S(2)}) collective-permute-start(f32[8,256,128]{2,1,0:T(8,128)S(1)} %pad_maximum_fusion), channel_id=1, source_target_pairs={{0,8},{1,9},{2,10},{3,11},{4,12},{5,13},{6,14},{7,15},{8,0},{9,1},... | collective-permute-start | bytes 3145736 | tf_op jit(solution)/shard_map/ppermute | solution.py:30
  61.7 7.5 %late.1 = (f32[64,4,8,1024]{3,2,1,0:T(8,128)}, bf16[512,1024]{1,0:T(8,128)(2,1)S(1)}, bf16[512,1024]{1,0:T(8,128)(2,1)S(1)}) custom-call(s32[14]{0:T(128)S(1)} %stack.59.info_ref, f32[3,512,1024]{2,1,0:T(8,128)S(1)} %get-tuple-element.52.part_ref, bf16[512,512]{1,0:T(8,128)(2,1)S(1)} %get-tuple-element.53.high2, ...), custom_call_target="tpu_custom_call" | custom-call | flops 4831838208 | bytes 25165824 | tf_op jit(solution)/shard_map/late/pallas_call | solution.py:211
  69.2 0.0 collective-permute-done.15.s3
  69.2 6.6 %last.1 = f32[64,4,8,1024]{3,2,1,0:T(8,128)} custom-call(s32[14]{0:T(128)S(1)} %stack.59.info_ref, f32[64,4,8,1024]{3,2,1,0:T(8,128)} %get-tuple-element.64.rest_ref, f32[8,128,128]{2,1,0:T(8,128)S(1)} %collective-permute-done.10.up, f32[8,128,128]{2,1,0:T(8,128)S(1)} %collective-permute-done.11.down, ...), custom_call_target="tpu_custom_call", output_to_operand_aliasing={{}: (1, {})} | custom-call | flops 3221225472 | bytes 8388608 | tf_op jit(solution)/shard_map/last/pallas_call | solution.py:267
  (11 shorter events, 0.3 us)
Async XLA Ops:
  0.0 20.6 %copy-start.1 = (f32[128,1024]{1,0:T(8,128)S(1)}, f32[128,1024]{1,0:T(8,128)}, u32[]{:S(2)}) copy-start(f32[128,1024]{1,0:T(8,128)} %w.1) | copy-start | bytes 1572868
  2.3 13.4 %collective-permute-start = (f32[8,128,128]{2,1,0:T(8,128)}, f32[8,128,128]{2,1,0:T(8,128)S(1)}, u32[]{:S(2)}, u32[]{:S(2)}) collective-permute-start(f32[8,128,128]{2,1,0:T(8,128)} %turn.1.x), channel_id=1, source_target_pairs={{0,16},{1,17},{2,18},{3,19},{4,20},{5,21},{6,22},{7,23},{8,24},{9,... | collective-permute-start | bytes 1572872 | tf_op jit(solution)/shard_map/ppermute | solution.py:30
  4.3 14.9 %collective-permute-start.7 = (f32[8,128,128]{2,1,0:T(8,128)}, f32[8,128,128]{2,1,0:T(8,128)S(1)}, u32[]{:S(2)}, u32[]{:S(2)}) collective-permute-start(f32[8,128,128]{2,1,0:T(8,128)} %turn.1.x), channel_id=1, source_target_pairs={{0,96},{1,97},{2,98},{3,99},{4,100},{5,101},{6,102},{7,103},{8,104... | collective-permute-start | bytes 1572872 | tf_op jit(solution)/shard_map/ppermute | solution.py:30
  7.0 13.6 %collective-permute-start.1 = (f32[8,128,128]{2,1,0:T(8,128)}, f32[8,128,128]{2,1,0:T(8,128)S(1)}, u32[]{:S(2)}, u32[]{:S(2)}) collective-permute-start(f32[8,128,128]{2,1,0:T(8,128)} %turn.1.x), channel_id=1, source_target_pairs={{0,32},{1,33},{2,34},{3,35},{4,36},{5,37},{6,38},{7,39},{8,40},{9,... | collective-permute-start | bytes 1572872 | tf_op jit(solution)/shard_map/ppermute | solution.py:30
  7.0 16.1 %collective-permute-start.6 = (f32[128,1024]{1,0:T(8,128)}, f32[128,1024]{1,0:T(8,128)S(1)}, u32[]{:S(2)}, u32[]{:S(2)}) collective-permute-start(f32[128,1024]{1,0:T(8,128)} %w.1), channel_id=1, source_target_pairs={{0,3},{1,0},{2,1},{3,2},{4,7},{5,4},{6,5},{7,6},{8,11},{9,8},{10,9... | collective-permute-start | bytes 1572872 | tf_op jit(solution)/shard_map/ppermute | solution.py:30
  10.8 13.3 %collective-permute-start.5 = (f32[128,1024]{1,0:T(8,128)}, f32[128,1024]{1,0:T(8,128)S(1)}, u32[]{:S(2)}, u32[]{:S(2)}) collective-permute-start(f32[128,1024]{1,0:T(8,128)} %w.1), channel_id=1, source_target_pairs={{0,1},{1,2},{2,3},{3,0},{4,5},{5,6},{6,7},{7,4},{8,9},{9,10},{10,1... | collective-permute-start | bytes 1572872 | tf_op jit(solution)/shard_map/ppermute | solution.py:30
  16.0 17.4 %collective-permute-start.4 = (f32[8,128,128]{2,1,0:T(8,128)S(1)}, f32[8,128,128]{2,1,0:T(8,128)S(1)}, u32[]{:S(2)}, u32[]{:S(2)}) collective-permute-start(f32[8,128,128]{2,1,0:T(8,128)S(1)} %collective-permute-done.xx), channel_id=1, source_target_pairs={{0,96},{1,97},{2,98},{3,99},{4,100},{5,101},{6,102},{7,103},{8,104... | collective-permute-start | bytes 1572872 | tf_op jit(solution)/shard_map/ppermute | solution.py:30
  19.2 14.2 %collective-permute-start.3 = (f32[8,128,128]{2,1,0:T(8,128)S(1)}, f32[8,128,128]{2,1,0:T(8,128)S(1)}, u32[]{:S(2)}, u32[]{:S(2)}) collective-permute-start(f32[8,128,128]{2,1,0:T(8,128)S(1)} %collective-permute-done.xx), channel_id=1, source_target_pairs={{0,32},{1,33},{2,34},{3,35},{4,36},{5,37},{6,38},{7,39},{8,40},{9,... | collective-permute-start | bytes 1572872 | tf_op jit(solution)/shard_map/ppermute | solution.py:30
  20.6 12.8 %collective-permute-start.2 = (f32[128,1024]{1,0:T(8,128)S(1)}, f32[128,1024]{1,0:T(8,128)S(1)}, u32[]{:S(2)}, u32[]{:S(2)}) collective-permute-start(f32[128,1024]{1,0:T(8,128)S(1)} %copy-done.1), channel_id=1, source_target_pairs={{0,4},{1,5},{2,6},{3,7},{4,0},{5,1},{6,2},{7,3},{8,12},{9,13},{10,... | collective-permute-start | bytes 1572872 | tf_op jit(solution)/shard_map/ppermute | solution.py:30
  24.1 12.5 %collective-permute-start.8 = (f32[128,1024]{1,0:T(8,128)S(1)}, f32[128,1024]{1,0:T(8,128)S(1)}, u32[]{:S(2)}, u32[]{:S(2)}) collective-permute-start(f32[128,1024]{1,0:T(8,128)S(1)} %copy-done.1), channel_id=1, source_target_pairs={{0,2},{1,3},{2,0},{3,1},{4,6},{5,7},{6,4},{7,5},{8,10},{9,11},{10,... | collective-permute-start | bytes 1572872 | tf_op jit(solution)/shard_map/ppermute | solution.py:30
  36.6 10.3 %copy-start = (f32[8,128,128]{2,1,0:T(8,128)S(1)}, f32[8,128,128]{2,1,0:T(8,128)}, u32[]{:S(2)}) copy-start(f32[8,128,128]{2,1,0:T(8,128)} %turn.1.x) | copy-start | bytes 1572868
  36.7 9.0 %collective-permute-start.9 = (f32[8,768,128]{2,1,0:T(8,128)S(1)}, f32[8,768,128]{2,1,0:T(8,128)S(1)}, u32[]{:S(2)}, u32[]{:S(2)}) collective-permute-start(f32[8,768,128]{2,1,0:T(8,128)S(1)} %constant_dynamic-update-slice_fusion), channel_id=1, source_target_pairs={{0,8},{1,9},{2,10},{3,11},{4,12},{5,13},{6,14},{7,15},{8,0},{9,1},... | collective-permute-start | bytes 9437192 | tf_op jit(solution)/shard_map/ppermute | solution.py:30
  40.3 17.6 %collective-permute-start.11 = (f32[8,128,128]{2,1,0:T(8,128)S(1)}, f32[8,128,128]{2,1,0:T(8,128)S(1)}, u32[]{:S(2)}, u32[]{:S(2)}) collective-permute-start(f32[8,128,128]{2,1,0:T(8,128)S(1)} %pad_maximum_fusion.2), channel_id=1, source_target_pairs={{0,96},{1,97},{2,98},{3,99},{4,100},{5,101},{6,102},{7,103},{8,104... | collective-permute-start | bytes 1572872 | tf_op jit(solution)/shard_map/ppermute | solution.py:30
  42.8 15.1 %collective-permute-start.10 = (f32[8,128,128]{2,1,0:T(8,128)S(1)}, f32[8,128,128]{2,1,0:T(8,128)S(1)}, u32[]{:S(2)}, u32[]{:S(2)}) collective-permute-start(f32[8,128,128]{2,1,0:T(8,128)S(1)} %pad_maximum_fusion.1), channel_id=1, source_target_pairs={{0,32},{1,33},{2,34},{3,35},{4,36},{5,37},{6,38},{7,39},{8,40},{9,... | collective-permute-start | bytes 1572872 | tf_op jit(solution)/shard_map/ppermute | solution.py:30
  42.9 15.0 %collective-permute-start.14 = (f32[128,1024]{1,0:T(8,128)S(1)}, f32[128,1024]{1,0:T(8,128)S(1)}, u32[]{:S(2)}, u32[]{:S(2)}) collective-permute-start(f32[128,1024]{1,0:T(8,128)S(1)} %collective-permute-done.8.w2), channel_id=1, source_target_pairs={{0,4},{1,5},{2,6},{3,7},{4,0},{5,1},{6,2},{7,3},{8,12},{9,13},{10,... | collective-permute-start | bytes 1572872 | tf_op jit(solution)/shard_map/ppermute | solution.py:30
  45.4 12.9 %collective-permute-start.13 = (f32[128,1024]{1,0:T(8,128)S(1)}, f32[128,1024]{1,0:T(8,128)S(1)}, u32[]{:S(2)}, u32[]{:S(2)}) collective-permute-start(f32[128,1024]{1,0:T(8,128)S(1)} %collective-permute-done.2.wx), channel_id=1, source_target_pairs={{0,3},{1,0},{2,1},{3,2},{4,7},{5,4},{6,5},{7,6},{8,11},{9,8},{10,9... | collective-permute-start | bytes 1572872 | tf_op jit(solution)/shard_map/ppermute | solution.py:30
  45.7 13.8 %collective-permute-start.12 = (f32[128,1024]{1,0:T(8,128)S(1)}, f32[128,1024]{1,0:T(8,128)S(1)}, u32[]{:S(2)}, u32[]{:S(2)}) collective-permute-start(f32[128,1024]{1,0:T(8,128)S(1)} %collective-permute-done.2.wx), channel_id=1, source_target_pairs={{0,1},{1,2},{2,3},{3,0},{4,5},{5,6},{6,7},{7,4},{8,9},{9,10},{10,1... | collective-permute-start | bytes 1572872 | tf_op jit(solution)/shard_map/ppermute | solution.py:30
  59.6 9.6 %collective-permute-start.15 = (f32[8,256,128]{2,1,0:T(8,128)S(1)}, f32[8,256,128]{2,1,0:T(8,128)S(1)}, u32[]{:S(2)}, u32[]{:S(2)}) collective-permute-start(f32[8,256,128]{2,1,0:T(8,128)S(1)} %pad_maximum_fusion), channel_id=1, source_target_pairs={{0,8},{1,9},{2,10},{3,11},{4,12},{5,13},{6,14},{7,15},{8,0},{9,1},... | collective-permute-start | bytes 3145736 | tf_op jit(solution)/shard_map/ppermute | solution.py:30
